TPU v7x, 256 devices: a whole 4x4x8 slice. The times are simulated.
256 devices in a mesh: dp: 8 (over y, core), cent: 32 (over z, x).
Axes of the slice: x: 4, y: 4, z: 8, core: 2. Of those that a mesh axis runs over, the one named last changes fastest.
Arguments:
- features: bfloat16 [8192, 1024], P('dp', 'cent'), may hold values from -128 to 128
- centroids: bfloat16 [65536, 1024], P('cent'), may hold values from -2 to 2
- row_weight: float32 [8192], P('dp'), may hold values from 0.5 to 18
- centroid_share: float32 [65536], P('cent'), may hold values from 0.5 to 18
Outputs:
- centroid_means: float32 [1024, 65536], P('dp', 'cent')
- centroid_mass: float32 [65536], P('cent')
All inputs are finite; a program needn't handle non-finite values.
Results may differ from a plain program's by a relative error of at most 0.001.
The roundings to bfloat16 on the way count: a program that leaves them out, or rounds other values in their place, can miss the bound.
Values may be sent and summed in bfloat16 or wider, within the bound.
No kernel may reach another device: no remote copies, remote signals or barrier semaphores. Data moves between devices by JAX's collectives and lax.ppermute only.
A program may use at most 64 MiB of HBM per device.

v0:
```python
import jax
import jax.numpy as jnp
from jax import lax
from jax.sharding import Mesh
from jax.sharding import PartitionSpec as P

ITERS = 3
CENT = ("cent_0", "cent_1")


def from_everyone(x, axis):
    devices = lax.axis_size(axis)
    return lax.all_to_all(jnp.broadcast_to(x[None], (devices, *x.shape)), axis, 0, 0, tiled=True)


def of_everyone(x, axis):
    everything = from_everyone(x, axis)
    return jnp.sum(everything, axis=0)


def gathered_by_axis(x, axes, dim):
    filled = x
    for number in range(len(axes) - 1, -1, -1):
        filled = lax.all_gather(filled, axes[number], axis=dim, tiled=True)
    return filled


def gathered_once(x, axis):
    leaves = jax.tree.leaves(x)
    order = sorted(range(len(leaves)), key=lambda k: -leaves[k].size)
    width = (1, *leaves[order[0]].shape)[-1]
    lines = [
        jnp.pad(leaves[k].reshape(-1), (0, -leaves[k].size % width)).reshape(-1, width)
        for k in order
    ]
    both, at, found = (from_everyone(jnp.concatenate(lines), axis), 0, {})
    for k, line in zip(order, lines):
        slab = both[:, at : at + len(line)].reshape(len(both), -1)
        found[k] = slab[:, : leaves[k].size].reshape(-1, *leaves[k].shape)
        at += len(line)
    numbers = iter(range(len(leaves)))
    return jax.tree.map(lambda _: found[next(numbers)], x)


def joined_by_halves(pieces, combine):
    while len(jax.tree.leaves(pieces)[0]) > 1:
        pieces = jax.vmap(combine)(
            *(jax.tree.map(lambda part: part[side::2], pieces) for side in (0, 1))
        )
    return jax.tree.map(lambda part: part[0], pieces)


def joined_all(x, axis, combine):
    pieces = gathered_once(x, axis)
    return joined_by_halves(pieces, combine)


def scaled_rows(kernel, column_scale, row_weight):
    row_terms = jnp.sum(kernel * column_scale[None, :], axis=1)
    return row_weight / of_everyone(row_terms, CENT)


def scaled_columns(kernel, row_scale, centroid_share):
    column_terms = jnp.sum(kernel * row_scale[:, None], axis=0)
    return centroid_share / of_everyone(column_terms, "dp")


def combine_peaks(earlier, later):
    joined_peak = jnp.maximum(earlier[0], later[0])
    joined_total = earlier[1] * jnp.exp(earlier[0] - joined_peak) + later[1] * jnp.exp(
        later[0] - joined_peak
    )
    return (joined_peak, joined_total)


def per_device(features, centroids, row_weight, centroid_share):
    features_all = gathered_by_axis(features, CENT, 1)
    scores = lax.dot_general(
        features_all, centroids, (((1,), (1,)), ((), ())), preferred_element_type=jnp.float32
    )
    local_peak = jnp.max(scores, axis=1)
    local_kernel = jnp.exp(scores - local_peak[:, None])
    shared_peak, row_total = joined_all(
        (local_peak, jnp.sum(local_kernel, axis=1)), CENT, combine_peaks
    )
    kernel = local_kernel * jnp.exp(local_peak - shared_peak)[:, None]
    row_scale = row_weight / row_total
    column_scale = scaled_columns(kernel, row_scale, centroid_share)
    for iteration in range(ITERS - 1):
        row_scale = scaled_rows(kernel, column_scale, row_weight)
        column_scale = scaled_columns(kernel, row_scale, centroid_share)
    row_scale = scaled_rows(kernel, column_scale, row_weight)
    transport = kernel * row_scale[:, None] * column_scale[None, :]
    centroid_total = of_everyone(jnp.sum(transport, axis=0), "dp")
    weights = transport.astype(jnp.bfloat16)
    weighted = lax.psum_scatter(
        lax.dot_general(
            features_all, weights, (((0,), (0,)), ((), ())), preferred_element_type=jnp.float32
        ),
        "dp",
        scatter_dimension=0,
        tiled=True,
    )
    return (weighted / centroid_total[None, :], centroid_total)


def solution(mesh):
    split = Mesh(mesh.devices.reshape(mesh.shape["dp"], 8, 4), ("dp", "cent_0", "cent_1"))
    return jax.shard_map(
        per_device,
        mesh=split,
        in_specs=(P("dp", CENT), P(CENT, None), P("dp"), P(CENT)),
        out_specs=(P("dp", CENT), P(CENT)),
        check_vma=False,
    )
```

profile of v0, /device:TPU:1, one launch (start us, length us, event | category | flops | bytes accessed | tf_op | source)
XLA Modules:
  0.0 260.0 jit_solution(8153557545711295909)
XLA Ops:
  7.2 12.4 %all_gather.6 = bf16[1024,128]{0,1:T(8,128)(2,1)} all-gather(bf16[1024,32]{0,1:T(8,128)(2,1)} %param.4), channel_id=1, replica_groups=mesh['dp'=8,'cent_0'=8,'cent_1'=4] {'cent_1'}, dimensions={1}, use_global_device_ids=true | all-gather | bytes 327680 | tf_op jit(solution)/shard_map/all_gather | solution.py:24
  19.7 41.1 %all-gather.2.cloned.1.call-done = bf16[1024,1024]{0,1:T(8,128)(2,1)} async-done(((bf16[1024,128]{0,1:T(8,128)(2,1)}), bf16[1024,1024]{0,1:T(8,128)(2,1)}) %all-gather.2.cloned.1.call-update) | async-done | bytes 2097168 | tf_op jit(solution)/shard_map/all_gather | solution.py:24
  60.8 7.2 %fusion.10 = (f32[1024]{0:T(1024)S(1)}, f32[1024,2048]{1,0:T(8,128)S(1)}) fusion(bf16[1024,1024]{0,1:T(8,128)(2,1)} %all-gather.2.cloned.1.call-done, bf16[2048,1024]{1,0:T(8,128)(2,1)} %param.5), kind=kOutput, calls=%fused_computation.29 | convolution fusion | flops 4297063424 | bytes 14684160 | tf_op jit(solution)/shard_map/dot_general | solution.py:78
  68.0 3.2 %copy-done = f32[1024,2048]{1,0:T(8,128)} copy-done((f32[1024,2048]{1,0:T(8,128)}, f32[1024,2048]{1,0:T(8,128)S(1)}, u32[]{:S(2)}) %copy-start) | copy-done | bytes 8388632
  71.2 1.3 fusion.1
  72.5 0.1 broadcast_in_dim.16
  72.5 16.8 %all_to_all.47 = f32[32,2,1024]{2,1,0:T(2,128)S(1)} all-to-all(f32[32,2,1024]{2,1,0:T(2,128)S(1)} %broadcast_in_dim.16), channel_id=1, replica_groups=mesh['dp'=8,'cent_0'=8,'cent_1'=4] {'cent_0','cent_1'}, dimensions={0} | all-to-all | bytes 524288 | tf_op jit(solution)/shard_map/all_to_all | solution.py:13
  89.3 0.2 fusion.9
  90.2 6.4 %multiply_reduce_fusion.5 = (f32[2048]{0:T(1024)S(1)}, f32[1024,2048]{1,0:T(8,128)}) fusion(f32[1024]{0:T(1024)S(1)} %div.29, f32[1024]{0:T(1024)S(1)} %subtract_exponential_fusion.1, f32[1024,2048]{1,0:T(8,128)} %copy-done, f32[1024]{0:T(1024)S(1)} %get-tuple-element.22), kind=kLoop, calls=%fused_computation.6 | loop fusion | flops 8386560 | bytes 16797696 | tf_op jit(solution)/shard_map/reduce_sum | solution.py:64
  96.6 15.5 %all_to_all.48 = f32[8,1,2048]{2,1,0:T(1,128)S(1)} all-to-all(f32[8,1,2048]{2,1,0:T(1,128)S(1)} %broadcast_in_dim.17), channel_id=1, replica_groups=mesh['dp'=8,'cent_0'=8,'cent_1'=4] {'dp'}, dimensions={0} | all-to-all | bytes 131072 | tf_op jit(solution)/shard_map/all_to_all | solution.py:13
  112.2 4.0 %multiply_reduce_fusion.4 = f32[1024]{0:T(1024)S(1)} fusion(f32[1024,2048]{1,0:T(8,128)} %get-tuple-element.9, f32[2048]{0:T(1024)S(1)} %div.30), kind=kLoop, calls=%fused_computation.5 | loop fusion | flops 4193280 | bytes 8400896 | tf_op jit(solution)/shard_map/reduce_sum | solution.py:59
  116.2 0.1 broadcast_in_dim.18
  116.3 12.7 %all_to_all.49 = f32[32,1,1024]{2,1,0:T(1,128)S(1)} all-to-all(f32[32,1,1024]{2,1,0:T(1,128)S(1)} %broadcast_in_dim.18), channel_id=1, replica_groups=mesh['dp'=8,'cent_0'=8,'cent_1'=4] {'cent_0','cent_1'}, dimensions={0} | all-to-all | bytes 262144 | tf_op jit(solution)/shard_map/all_to_all | solution.py:13
  129.0 0.1 reduce_sum.139
  129.1 4.0 %multiply_reduce_fusion.3 = f32[2048]{0:T(1024)S(1)} fusion(f32[1024,2048]{1,0:T(8,128)} %get-tuple-element.9, f32[1024]{0:T(1024)S(1)} %div.31), kind=kLoop, calls=%fused_computation.4 | loop fusion | flops 4192256 | bytes 8400896 | tf_op jit(solution)/shard_map/reduce_sum | solution.py:64
  133.2 9.5 %all_to_all.50 = f32[8,1,2048]{2,1,0:T(1,128)S(1)} all-to-all(f32[8,1,2048]{2,1,0:T(1,128)S(1)} %broadcast_in_dim.19), channel_id=1, replica_groups=mesh['dp'=8,'cent_0'=8,'cent_1'=4] {'dp'}, dimensions={0} | all-to-all | bytes 131072 | tf_op jit(solution)/shard_map/all_to_all | solution.py:13
  142.7 4.0 %multiply_reduce_fusion.2 = f32[1024]{0:T(1024)S(1)} fusion(f32[1024,2048]{1,0:T(8,128)} %get-tuple-element.9, f32[2048]{0:T(1024)S(1)} %div.32), kind=kLoop, calls=%fused_computation.3 | loop fusion | flops 4193280 | bytes 8400896 | tf_op jit(solution)/shard_map/reduce_sum | solution.py:59
  146.7 0.1 broadcast_in_dim.20
  146.8 12.3 %all_to_all.51 = f32[32,1,1024]{2,1,0:T(1,128)S(1)} all-to-all(f32[32,1,1024]{2,1,0:T(1,128)S(1)} %broadcast_in_dim.20), channel_id=1, replica_groups=mesh['dp'=8,'cent_0'=8,'cent_1'=4] {'cent_0','cent_1'}, dimensions={0} | all-to-all | bytes 262144 | tf_op jit(solution)/shard_map/all_to_all | solution.py:13
  159.1 0.1 reduce_sum.143
  159.2 4.2 %multiply_reduce_fusion.1 = f32[2048]{0:T(1024)S(1)} fusion(f32[1024,2048]{1,0:T(8,128)} %get-tuple-element.9, f32[1024]{0:T(1024)S(1)} %div.33), kind=kLoop, calls=%fused_computation.2 | loop fusion | flops 4192256 | bytes 8400896 | tf_op jit(solution)/shard_map/reduce_sum | solution.py:64
  163.4 9.4 %all_to_all.52 = f32[8,1,2048]{2,1,0:T(1,128)S(1)} all-to-all(f32[8,1,2048]{2,1,0:T(1,128)S(1)} %broadcast_in_dim.21), channel_id=1, replica_groups=mesh['dp'=8,'cent_0'=8,'cent_1'=4] {'dp'}, dimensions={0} | all-to-all | bytes 131072 | tf_op jit(solution)/shard_map/all_to_all | solution.py:13
  172.9 4.0 %multiply_reduce_fusion = f32[1024]{0:T(1024)S(1)} fusion(f32[1024,2048]{1,0:T(8,128)} %get-tuple-element.9, f32[2048]{0:T(1024)S(1)} %div.34), kind=kLoop, calls=%fused_computation.1 | loop fusion | flops 4193280 | bytes 8400896 | tf_op jit(solution)/shard_map/reduce_sum | solution.py:59
  176.9 0.1 broadcast_in_dim.22
  177.0 12.6 %all_to_all.53 = f32[32,1,1024]{2,1,0:T(1,128)S(1)} all-to-all(f32[32,1,1024]{2,1,0:T(1,128)S(1)} %broadcast_in_dim.22), channel_id=1, replica_groups=mesh['dp'=8,'cent_0'=8,'cent_1'=4] {'cent_0','cent_1'}, dimensions={0} | all-to-all | bytes 262144 | tf_op jit(solution)/shard_map/all_to_all | solution.py:13
  189.6 0.1 reduce_sum.147
  189.7 10.8 %convolution_bitcast_fusion = f32[1024,2048]{0,1:T(8,128)} fusion(bf16[1024,1024]{0,1:T(8,128)(2,1)S(1)} %copy-done.4, f32[1024,2048]{1,0:T(8,128)} %get-tuple-element.9, f32[1024]{0:T(1024)S(1)} %div.35, f32[2048]{0:T(1024)S(1)} %div.34), kind=kOutput, calls=%fused_computation.12 | convolution fusion | flops 4301258752 | bytes 18886656 | tf_op jit(solution)/shard_map/dot_general | solution.py:97
  200.5 4.3 %fusion.2 = f32[2048]{0:T(1024)S(1)} fusion(f32[1024,2048]{1,0:T(8,128)} %get-tuple-element.9, f32[1024]{0:T(1024)S(1)} %div.35, f32[2048]{0:T(1024)S(1)} %div.34), kind=kLoop, calls=%fused_computation.10 | loop fusion | flops 6289408 | bytes 8409088 | tf_op jit(solution)/shard_map/reduce_sum | solution.py:94
  204.9 9.5 %all_to_all.54 = f32[8,1,2048]{2,1,0:T(1,128)S(1)} all-to-all(f32[8,1,2048]{2,1,0:T(1,128)S(1)} %broadcast_in_dim.23), channel_id=1, replica_groups=mesh['dp'=8,'cent_0'=8,'cent_1'=4] {'dp'}, dimensions={0} | all-to-all | bytes 131072 | tf_op jit(solution)/shard_map/all_to_all | solution.py:13
  214.4 35.9 %reduce-scatter.2.cloned.1.call-done = f32[128,2048]{0,1:T(8,128)} async-done(((f32[1024,2048]{0,1:T(8,128)}), f32[128,2048]{0,1:T(8,128)}) %reduce-scatter.2.cloned.1.call-update) | async-done | bytes 1048592 | tf_op jit(solution)/shard_map/reduce_scatter | solution.py:96
  250.3 1.6 broadcast_divide_fusion
  251.9 1.3 copy.18
  (52 shorter events, 1.1 us)
Async XLA Ops:
  7.2 53.6 %all-gather.2.cloned.1.call-start = ((), (), s32[]{:S(2)}) async-start(), calls=%async_computation.9 | async-start | bytes 2359296 | tf_op jit(solution)/shard_map/all_gather | solution.py:24
  19.6 230.7 %reduce-scatter.2.cloned.1.call-start = ((), (), s32[]{:S(2)}) async-start(), calls=%async_computation.10 | async-start | bytes 9437184 | tf_op jit(solution)/shard_map/reduce_scatter | solution.py:96
  68.0 3.2 %copy-start = (f32[1024,2048]{1,0:T(8,128)}, f32[1024,2048]{1,0:T(8,128)S(1)}, u32[]{:S(2)}) copy-start(f32[1024,2048]{1,0:T(8,128)S(1)} %get-tuple-element.23) | copy-start | bytes 25165828
  68.0 22.2 %copy-start.2 = (f32[1024]{0:T(1024)S(1)}, f32[1024]{0:T(1024)}, u32[]{:S(2)}) copy-start(f32[1024]{0:T(1024)} %param.6) | copy-start | bytes 12292
  90.2 22.0 %copy-start.1 = (f32[2048]{0:T(1024)S(1)}, f32[2048]{0:T(1024)}, u32[]{:S(2)}) copy-start(f32[2048]{0:T(1024)} %param.7) | copy-start | bytes 24580
  159.2 30.5 %copy-start.4 = (bf16[1024,1024]{0,1:T(8,128)(2,1)S(1)}, bf16[1024,1024]{0,1:T(8,128)(2,1)}, u32[]{:S(2)}) copy-start(bf16[1024,1024]{0,1:T(8,128)(2,1)} %all-gather.2.cloned.1.call-done) | copy-start | bytes 6291460
  214.4 38.8 %copy-start.3 = (f32[2048]{0:T(1024)}, f32[2048]{0:T(1024)S(1)}, u32[]{:S(2)}) copy-start(f32[2048]{0:T(1024)S(1)} %reduce_sum.149) | copy-start | bytes 24580
Sparse Core Ops, SparseCore 0:
  19.8 40.9 all-gather.1
  200.6 49.6 reduce-scatter.1
where the time goes:
time: 261 us; the launch traced here: 260 us
  blocking collectives  111 us (43%)
  waiting for transfers between devices  77 us (30%)
  other arithmetic  34.4 us (13%)
  matrix products  18 us (7%)
  between operations  14.4 us (6%)
  local copies, waits for them, and re-layouts  5.58 us (2%)
    all_to_all x8, blocking collectives, from_everyone(): lax.all_to_all(jnp.broadcast_to(x[None], (devices, *x.shape)), axis, 0, 0...  98.2 us
    all_gather x1, waiting for transfers between devices, gathered_by_axis(): filled = lax.all_gather(filled, axes[number], axis=dim, tiled=True)  41.1 us
    reduce_scatter x1, waiting for transfers between devices, per_device(): lax.psum_scatter(lax.dot_general(features_all, weights, (((0,), (0,)), ((...  35.9 us
    reduce_sum x3, other arithmetic, scaled_columns(): column_terms = jnp.sum(kernel * row_scale[:, None], axis=0)  14.6 us
    all_gather x1, blocking collectives, gathered_by_axis(): filled = lax.all_gather(filled, axes[number], axis=dim, tiled=True)  12.4 us
    reduce_sum x3, other arithmetic, scaled_rows(): row_terms = jnp.sum(kernel * column_scale[None, :], axis=1)  12.1 us
    dot_general x1, matrix products, per_device(): lax.dot_general(features_all, weights, (((0,), (0,)), ((), ())), preferre...  10.8 us
    dot_general x1, matrix products, per_device(): lax.dot_general(features_all, centroids, (((1,), (1,)), ((), ())), prefer...  7.18 us
  transfers between devices with their start and end apart: 2, of which 2 were waited for; matrix products, arithmetic and copies ran while one was open for 2% of the time, Pallas kernels for 0%

commit v1 on v0

v1 whole, which is shorter than its diff:
```python
import jax
import jax.numpy as jnp
from jax import lax
from jax.experimental import pallas as pl
from jax.experimental.pallas import tpu as pltpu
from jax.sharding import Mesh
from jax.sharding import PartitionSpec as P

ITERS = 3
ROWS = 1024
COLS = 2048
D = 1024
RB, CB = ROWS // 128, COLS // 128
CENT = ("z", "x")
DP = ("y", "core")
F32, BF16 = jnp.float32, jnp.bfloat16
VM = pl.BlockSpec(memory_space=pltpu.VMEM)
SM = pl.BlockSpec(memory_space=pltpu.SMEM)


def call(body, outs, ins, scratch=(), mib=24, name=None, aliases=None):
    return pl.pallas_call(
        body,
        out_shape=[jax.ShapeDtypeStruct(s, d) for s, d in outs],
        in_specs=[SM if a.dtype == jnp.int32 else VM for a in ins],
        out_specs=[VM] * len(outs),
        scratch_shapes=list(scratch),
        input_output_aliases=aliases or {},
        compiler_params=pltpu.CompilerParams(vmem_limit_bytes=mib << 20),
        name=name,
    )(*ins)


def step(x, axis, by):
    n = lax.axis_size(axis)
    return lax.ppermute(x, axis, [(i, (i + by) % n) for i in range(n)])


def everyone(x, axis):
    return lax.all_to_all(x, axis, 0, 0, tiled=True)


def down(row):
    return jnp.broadcast_to(row, (128, 128)).T


def strip_body(at_ref, a_ref, b_ref, c_ref, d_ref, o_ref):
    for k, ref in enumerate((a_ref, b_ref, c_ref, d_ref)):
        o_ref[pl.ds(pl.multiple_of(at_ref[k] * 32, 32), 32), :] = ref[...]


def score_body(at_ref, s_ref, r1, l1, r2, l2, r3, l3, h0, h1, c_ref, k_ref, ft_ref, fa_ref, p_ref):
    for k, ref in enumerate((s_ref, r1, l1, r2, l2, r3, l3)):
        ft_ref[at_ref[k]] = ref[...]
    ft_ref[at_ref[7], 0:64] = h0[...]
    ft_ref[at_ref[7], 64:128] = h1[...]
    for d in range(8):
        top = jnp.max(jnp.abs(ft_ref[d].astype(F32)), axis=0, keepdims=True)
        fa_ref[d : d + 1, :] = jnp.broadcast_to(jnp.max(top, axis=1, keepdims=True), (1, 128))
    for b in range(4):
        rows = slice(256 * b, 256 * b + 256)
        feats = ft_ref[:, :, rows].reshape(D, 256).T
        s = lax.dot_general(
            feats, c_ref[...], (((1,), (1,)), ((), ())), preferred_element_type=F32
        )
        k_ref[rows, :] = s
    for b in range(RB):
        rows = slice(128 * b, 128 * b + 128)
        s = k_ref[rows, :]
        top = jnp.max(s, axis=1, keepdims=True)
        e = jnp.exp(s - top)
        k_ref[rows, :] = e
        total = jnp.sum(e, axis=1, keepdims=True)
        p_ref[:, b : b + 1, :] = jnp.broadcast_to(
            jnp.broadcast_to(top, (128, 128)).T[0:1][None], (32, 1, 128)
        )
        p_ref[:, RB + b : RB + b + 1, :] = jnp.broadcast_to(
            jnp.broadcast_to(total, (128, 128)).T[0:1][None], (32, 1, 128)
        )


def columns(k_ref, scale, o_ref):
    acc = [jnp.zeros((8, 128), F32)] * CB
    for b in range(RB):
        rows = slice(128 * b, 128 * b + 128)
        by = down(scale[b : b + 1])
        for t in range(CB):
            part = k_ref[rows, 128 * t : 128 * t + 128] * by
            acc[t] = acc[t] + jnp.sum(part.reshape(16, 8, 128), axis=0)
    z = jnp.concatenate([jnp.sum(a, axis=0, keepdims=True) for a in acc], axis=0)
    o_ref[...] = jnp.broadcast_to(z[None], o_ref.shape)


def first_column_body(e_ref, mine_ref, a_ref, k_ref, o_ref, f_ref):
    peaks = e_ref[:, 0:RB, :]
    top = jnp.max(peaks, axis=0)
    total = jnp.sum(e_ref[:, RB : 2 * RB, :] * jnp.exp(peaks - top[None]), axis=0)
    fold = jnp.exp(mine_ref[0, 0:RB, :] - top)
    f_ref[...] = fold
    columns(k_ref, (a_ref[...] / total) * fold, o_ref)


def column_body(e_ref, f_ref, a_ref, k_ref, o_ref):
    scale = a_ref[...] / jnp.sum(e_ref[...], axis=0)
    columns(k_ref, scale * f_ref[...], o_ref)


def row_body(e_ref, f_ref, b_ref, k_ref, o_ref, c_ref):
    scale = b_ref[...] / jnp.sum(e_ref[...], axis=0)
    c_ref[...] = scale
    lines = []
    for b in range(RB):
        rows = slice(128 * b, 128 * b + 128)
        acc = jnp.zeros((128, 128), F32)
        for t in range(CB):
            acc = acc + k_ref[rows, 128 * t : 128 * t + 128] * scale[t : t + 1]
        lines.append(jnp.sum(acc.T, axis=0, keepdims=True))
    y = jnp.concatenate(lines, axis=0) * f_ref[...]
    o_ref[...] = jnp.broadcast_to(y[None], o_ref.shape)


def weight_body(e_ref, f_ref, a_ref, c_ref, fa_ref, k_ref, w_ref, m_ref):
    scale = (a_ref[...] / jnp.sum(e_ref[...], axis=0)) * f_ref[...]
    acc = [jnp.zeros((8, 128), F32)] * CB
    for b in range(RB):
        rows = slice(128 * b, 128 * b + 128)
        by = down(scale[b : b + 1])
        for t in range(CB):
            cols = slice(128 * t, 128 * t + 128)
            part = (k_ref[rows, cols] * by) * c_ref[t : t + 1, :]
            acc[t] = acc[t] + jnp.sum(part.reshape(16, 8, 128), axis=0)
            w_ref[rows, cols] = part.astype(BF16)
    m_ref[0:CB, :] = jnp.concatenate([jnp.sum(a, axis=0, keepdims=True) for a in acc], axis=0)
    m_ref[CB : CB + 8, :] = fa_ref[...]


def product_body(at_ref, ft_ref, w_ref, *o_refs):
    for k, o_ref in enumerate(o_refs):
        o_ref[...] = jnp.dot(ft_ref[at_ref[k]], w_ref[...], preferred_element_type=F32)


def per_device(features, centroids, row_weight, centroid_share):
    y, core, z, x = (lax.axis_index(n) for n in ("y", "core", "z", "x"))
    a = row_weight.reshape(RB, 128)
    share = centroid_share.reshape(CB, 128)

    own = features.T
    parts = [own] + [step(own, "x", k) for k in (1, 2, 3)]
    at = jnp.stack([(x - k) % 4 for k in range(4)]).astype(jnp.int32)
    (strip,) = call(strip_body, [((128, ROWS), BF16)], [at, *parts], mib=8, name="strip")
    right = left = strip
    ring = [strip]
    for _ in range(3):
        right, left = step(right, "z", 1), step(left, "z", -1)
        ring += [right, left]
    ring += [step(right[:64], "z", 1), step(left[64:], "z", -1)]
    at = jnp.stack([(z + k) % 8 for k in (0, -1, 1, -2, 2, -3, 3, 4)]).astype(jnp.int32)
    kernel, ft, fa, peaks = call(
        score_body,
        [((ROWS, COLS), F32), ((8, 128, ROWS), BF16), ((8, 128), F32), ((32, 2 * RB, 128), F32)],
        [at, *ring, centroids],
        mib=40,
        name="score",
    )
    got = everyone(peaks, CENT)
    sums, fold = call(
        first_column_body,
        [((8, CB, 128), F32), ((RB, 128), F32)],
        [got, peaks, a, kernel],
        name="column0",
    )
    for it in range(ITERS):
        rows, cscale = call(
            row_body,
            [((32, RB, 128), F32), ((CB, 128), F32)],
            [everyone(sums, DP), fold, share, kernel],
            name="row",
        )
        got = everyone(rows, CENT)
        if it < ITERS - 1:
            (sums,) = call(
                column_body, [((8, CB, 128), F32)], [got, fold, a, kernel], name="column"
            )
    weights, mass = call(
        weight_body,
        [((ROWS, COLS), BF16), ((CB + 8, 128), F32)],
        [got, fold, a, cscale, fa, kernel],
        name="weights",
    )

    other = step(mass, "core", 1)
    chip = jnp.concatenate([mass[:CB] + other[:CB], jnp.maximum(mass[CB:], other[CB:])], axis=0)
    chips = [chip] + [step(chip, "y", k) for k in (1, 2, 3)]

    def block(by, side):
        return 2 * ((y + by) % 4) + (core + side) % 2

    def limits(m, d):
        return (m[:CB] * lax.dynamic_slice(m, (CB + d, 0), (1, 128))).reshape(1, COLS)

    def products(which):
        at = jnp.stack([block(*w) for w in which]).astype(jnp.int32)
        return call(
            product_body,
            [((128, COLS), F32)] * len(which),
            [at, ft, weights],
            name="product",
        )

    def packed(mine, theirs, by):
        q = limits(chip, block(by, 0))
        inverse = jnp.where(q > 0, 32768.0 / q, 0.0)
        return ((mine + theirs) * inverse).astype(jnp.float16)

    sent = {}
    (give,) = products([(2, 1)])
    theirs = step(give, "core", 1)
    (mine,) = products([(2, 0)])
    sent[2] = step(packed(mine, theirs, 2), "y", 2)
    gives = products([(1, 1), (3, 1)])
    theirs = [step(g, "core", 1) for g in gives]
    mines = products([(1, 0), (3, 0)])
    sent[1] = step(packed(mines[0], theirs[0], 1), "y", 1)
    sent[3] = step(packed(mines[1], theirs[1], 3), "y", 3)
    give, mine = products([(0, 1), (0, 0)])
    total = mine + step(give, "core", 1)

    here = block(0, 0)
    for by in (1, 2, 3):
        total = total + sent[by].astype(F32) * (limits(chips[by], here) * (1.0 / 32768.0))
    centroid_total = (chips[0][:CB] + chips[2][:CB]) + (chips[1][:CB] + chips[3][:CB])
    return total / centroid_total.reshape(1, COLS), centroid_total.reshape(COLS)


def solution(mesh):
    split = Mesh(mesh.devices.reshape(4, 2, 8, 4), ("y", "core", "z", "x"))
    return jax.shard_map(
        per_device,
        mesh=split,
        in_specs=(P(DP, CENT), P(CENT, None), P(DP), P(CENT)),
        out_specs=(P(DP, CENT), P(CENT)),
        check_vma=False,
    )
```

time: 261 us -> 215 us (0.82)
  blocking collectives: 111 us -> 76 us
  starting transfers between devices: 0.08 us -> 34.1 us
  other arithmetic: 34.4 us -> 2.16 us
  Pallas kernels: 0 us -> 24.4 us
  waiting for transfers between devices: 77 us -> 58.5 us
  matrix products: 18 us -> 0 us
  between operations: 14.4 us -> 1.01 us
  local copies, waits for them, and re-layouts: 5.58 us -> 18.2 us
    ppermute x0 -> x22, waiting for transfers between devices: none -> 49.5 us  [step(): return lax.ppermute(x, axis, [(i, (i + by) % n) for i in range(n)])]
    all_gather x1 -> x0, waiting for transfers between devices: 41.1 us -> none  [gathered_by_axis(): filled = lax.all_gather(filled, axes[number], axis=dim, tiled=True)]
    reduce_scatter x1 -> x0, waiting for transfers between devices: 35.9 us -> none  [per_device(): lax.psum_scatter(lax.dot_general(features_all, weights, (((0,), (0,)), ((...]
    reduce_sum x15 -> x0, other arithmetic: 32.7 us -> none  [the longest x3 14.6 us: scaled_columns(): column_terms = jnp.sum(kernel * row_scale[:, None], axis=0)]
    ppermute x0 -> x22, starting transfers between devices: none -> 30 us  [step(): return lax.ppermute(x, axis, [(i, (i + by) % n) for i in range(n)])]
    pallas_call x0 -> x14, Pallas kernels: none -> 24.4 us  [call(): pl.pallas_call(body, out_shape=[jax.ShapeDtypeStruct(s, d) for s, d in ou...]
    all_to_all x8 -> x6, blocking collectives: 98.2 us -> 76 us  [everyone(): return lax.all_to_all(x, axis, 0, 0, tiled=True)]
    dot_general x2 -> x0, matrix products: 18 us -> none  [the longest x1 10.8 us: per_device(): lax.dot_general(features_all, weights, (((0,), (0,)), ((), ())), preferre...]
  transfers between devices with their start and end apart: 2 -> 23, of which waited for: 2 -> 15; matrix products, arithmetic and copies ran while one was open for 2% -> 0% of each run, Pallas kernels for 0% -> 3%
where the time goes in v1:
time: 215 us; the launch traced here: 214 us
  blocking collectives  76 us (35%)
  waiting for transfers between devices  58.5 us (27%)
  starting transfers between devices  34.1 us (16%)
  Pallas kernels  24.4 us (11%)
  local copies, waits for them, and re-layouts  18.2 us (8%)
  other arithmetic  2.16 us (1%)
    all_to_all x6, blocking collectives, everyone(): return lax.all_to_all(x, axis, 0, 0, tiled=True)  76 us
    ppermute x22, waiting for transfers between devices, step(): return lax.ppermute(x, axis, [(i, (i + by) % n) for i in range(n)])  49.5 us
    ppermute x22, starting transfers between devices, step(): return lax.ppermute(x, axis, [(i, (i + by) % n) for i in range(n)])  30 us
    pallas_call x14, Pallas kernels, call(): pl.pallas_call(body, out_shape=[jax.ShapeDtypeStruct(s, d) for s, d in ou...  24.4 us
    unnamed x30, local copies, waits for them, and re-layouts  18.1 us
    all_to_all x1, waiting for transfers between devices, everyone(): return lax.all_to_all(x, axis, 0, 0, tiled=True)  9.06 us
  transfers between devices with their start and end apart: 23, of which 15 were waited for; matrix products, arithmetic and copies ran while one was open for 0% of the time, Pallas kernels for 3%

profile of v1, /device:TPU:1, one launch (start us, length us, event | category | flops | bytes accessed | tf_op | source)
XLA Modules:
  0.0 214.3 jit_solution(1269530492898287212)
XLA Ops:
  0.6 2.1 collective-permute-start
  2.7 2.5 %collective-permute-start.1 = (bf16[32,1024]{1,0:T(8,128)(2,1)}, bf16[32,1024]{1,0:T(8,128)(2,1)S(1)}, u32[]{:S(2)}, u32[]{:S(2)}) collective-permute-start(bf16[32,1024]{1,0:T(8,128)(2,1)} %bitcast.57), channel_id=1, source_target_pairs={{0,2},{1,3},{2,0},{3,1},{4,6},{5,7},{6,4},{7,5},{8,10},{9,11},{10,... | collective-permute-start | bytes 196616 | tf_op jit(solution)/shard_map/ppermute | solution.py:36
  10.2 5.9 %collective-permute-start.4 = (bf16[128,1024]{1,0:T(8,128)(2,1)S(1)}, bf16[128,1024]{1,0:T(8,128)(2,1)S(1)}, u32[]{:S(2)}, u32[]{:S(2)}) collective-permute-start(bf16[128,1024]{1,0:T(8,128)(2,1)S(1)} %strip.1.s_ref), channel_id=1, source_target_pairs={{0,28},{4,0},{8,4},{12,8},{16,12},{20,16},{24,20},{28,24},{1,29},{... | collective-permute-start | bytes 786440 | tf_op jit(solution)/shard_map/ppermute | solution.py:36
  16.1 3.8 %collective-permute-done.4.l1 = bf16[128,1024]{1,0:T(8,128)(2,1)S(1)} collective-permute-done((bf16[128,1024]{1,0:T(8,128)(2,1)S(1)}, bf16[128,1024]{1,0:T(8,128)(2,1)S(1)}, u32[]{:S(2)}, u32[]{:S(2)}) %collective-permute-start.4) | collective-permute-done | bytes 262176 | tf_op jit(solution)/shard_map/ppermute | solution.py:36
  19.9 3.4 %collective-permute-start.6 = (bf16[128,1024]{1,0:T(8,128)(2,1)S(1)}, bf16[128,1024]{1,0:T(8,128)(2,1)S(1)}, u32[]{:S(2)}, u32[]{:S(2)}) collective-permute-start(bf16[128,1024]{1,0:T(8,128)(2,1)S(1)} %collective-permute-done.4.l1), channel_id=1, source_target_pairs={{0,28},{4,0},{8,4},{12,8},{16,12},{20,16},{24,20},{28,24},{1,29},{... | collective-permute-start | bytes 786440 | tf_op jit(solution)/shard_map/ppermute | solution.py:36
  23.4 3.3 %collective-permute-done.6.l2 = bf16[128,1024]{1,0:T(8,128)(2,1)S(1)} collective-permute-done((bf16[128,1024]{1,0:T(8,128)(2,1)S(1)}, bf16[128,1024]{1,0:T(8,128)(2,1)S(1)}, u32[]{:S(2)}, u32[]{:S(2)}) %collective-permute-start.6) | collective-permute-done | bytes 262176 | tf_op jit(solution)/shard_map/ppermute | solution.py:36
  26.7 3.1 %collective-permute-start.8 = (bf16[128,1024]{1,0:T(8,128)(2,1)S(1)}, bf16[128,1024]{1,0:T(8,128)(2,1)S(1)}, u32[]{:S(2)}, u32[]{:S(2)}) collective-permute-start(bf16[128,1024]{1,0:T(8,128)(2,1)S(1)} %collective-permute-done.6.l2), channel_id=1, source_target_pairs={{0,28},{4,0},{8,4},{12,8},{16,12},{20,16},{24,20},{28,24},{1,29},{... | collective-permute-start | bytes 786440 | tf_op jit(solution)/shard_map/ppermute | solution.py:36
  30.5 2.6 %collective-permute-done.8.l3 = bf16[128,1024]{1,0:T(8,128)(2,1)S(1)} collective-permute-done((bf16[128,1024]{1,0:T(8,128)(2,1)S(1)}, bf16[128,1024]{1,0:T(8,128)(2,1)S(1)}, u32[]{:S(2)}, u32[]{:S(2)}) %collective-permute-start.8) | collective-permute-done | bytes 262176 | tf_op jit(solution)/shard_map/ppermute | solution.py:36
  33.1 3.2 %collective-permute-start.10 = (bf16[64,1024]{1,0:T(8,128)(2,1)S(1)}, bf16[64,1024]{1,0:T(8,128)(2,1)S(1)}, u32[]{:S(2)}, u32[]{:S(2)}) collective-permute-start(bf16[64,1024]{1,0:T(8,128)(2,1)S(1)} %slice.40), channel_id=1, source_target_pairs={{0,28},{4,0},{8,4},{12,8},{16,12},{20,16},{24,20},{28,24},{1,29},{... | collective-permute-start | bytes 393224 | tf_op jit(solution)/shard_map/ppermute | solution.py:36
  38.8 4.1 %collective-permute-done.9.h0 = bf16[64,1024]{1,0:T(8,128)(2,1)S(1)} collective-permute-done((bf16[64,1024]{1,0:T(8,128)(2,1)S(1)}, bf16[64,1024]{1,0:T(8,128)(2,1)S(1)}, u32[]{:S(2)}, u32[]{:S(2)}) %collective-permute-start.9) | collective-permute-done | bytes 131104 | tf_op jit(solution)/shard_map/ppermute | solution.py:36
  43.6 2.2 %copy-done.4 = bf16[2048,1024]{1,0:T(8,128)(2,1)S(1)} copy-done((bf16[2048,1024]{1,0:T(8,128)(2,1)S(1)}, bf16[2048,1024]{1,0:T(8,128)(2,1)}, u32[]{:S(2)}) %copy-start.4) | copy-done | bytes 4194328
  48.6 10.0 %score.1 = (f32[1024,2048]{1,0:T(8,128)}, bf16[8,128,1024]{2,1,0:T(8,128)(2,1)S(1)}, f32[8,128]{1,0:T(8,128)S(1)}, f32[32,16,128]{2,1,0:T(8,128)S(1)}) custom-call(s32[8]{0:T(128)S(1)} %stack.86.at_ref, bf16[128,1024]{1,0:T(8,128)(2,1)S(1)} %strip.1.s_ref, bf16[128,1024]{1,0:T(8,128)(2,1)S(1)} %collective-permute-done.3.r1, ...), custom_call_target="tpu_custom_call" | custom-call | tf_op jit(solution)/shard_map/score/pallas_call | solution.py:22
  58.6 15.0 %all_to_all.35.e_ref = f32[32,16,128]{2,1,0:T(8,128)S(1)} all-to-all(f32[32,16,128]{2,1,0:T(8,128)S(1)} %get-tuple-element.21.mine_ref), channel_id=1, replica_groups=mesh['y'=4,'core'=2,'z'=8,'x'=4] {'z','x'}, dimensions={0} | all-to-all | bytes 524288 | tf_op jit(solution)/shard_map/all_to_all | solution.py:40
  73.6 3.4 %copy-done = f32[1024,2048]{1,0:T(8,128)S(1)} copy-done((f32[1024,2048]{1,0:T(8,128)S(1)}, f32[1024,2048]{1,0:T(8,128)}, u32[]{:S(2)}) %copy-start) | copy-done | bytes 8388632
  77.7 17.0 %all_to_all.36.e_ref = f32[8,16,128]{2,1,0:T(8,128)S(1)} all-to-all(f32[8,16,128]{2,1,0:T(8,128)S(1)} %get-tuple-element.23), channel_id=1, replica_groups=mesh['y'=4,'core'=2,'z'=8,'x'=4] {'y','core'}, dimensions={0} | all-to-all | bytes 131072 | tf_op jit(solution)/shard_map/all_to_all | solution.py:40
  95.9 12.7 %all_to_all.37.e_ref = f32[32,8,128]{2,1,0:T(8,128)S(1)} all-to-all(f32[32,8,128]{2,1,0:T(8,128)S(1)} %get-tuple-element.25), channel_id=1, replica_groups=mesh['y'=4,'core'=2,'z'=8,'x'=4] {'z','x'}, dimensions={0} | all-to-all | bytes 262144 | tf_op jit(solution)/shard_map/all_to_all | solution.py:40
  109.3 9.5 %all_to_all.38.e_ref = f32[8,16,128]{2,1,0:T(8,128)S(1)} all-to-all(f32[8,16,128]{2,1,0:T(8,128)S(1)} %column.2), channel_id=1, replica_groups=mesh['y'=4,'core'=2,'z'=8,'x'=4] {'y','core'}, dimensions={0} | all-to-all | bytes 131072 | tf_op jit(solution)/shard_map/all_to_all | solution.py:40
  119.9 12.3 %all_to_all.39.e_ref = f32[32,8,128]{2,1,0:T(8,128)S(1)} all-to-all(f32[32,8,128]{2,1,0:T(8,128)S(1)} %get-tuple-element.26), channel_id=1, replica_groups=mesh['y'=4,'core'=2,'z'=8,'x'=4] {'z','x'}, dimensions={0} | all-to-all | bytes 262144 | tf_op jit(solution)/shard_map/all_to_all | solution.py:40
  132.9 9.4 %all_to_all.40.e_ref = f32[8,16,128]{2,1,0:T(8,128)S(1)} all-to-all(f32[8,16,128]{2,1,0:T(8,128)S(1)} %column.3), channel_id=1, replica_groups=mesh['y'=4,'core'=2,'z'=8,'x'=4] {'y','core'}, dimensions={0} | all-to-all | bytes 131072 | tf_op jit(solution)/shard_map/all_to_all | solution.py:40
  143.6 4.1 %all-to-all-start.6 = ((f32[32,8,128]{2,1,0:T(8,128)}), f32[32,8,128]{2,1,0:T(8,128)S(1)}, u32[]{:S(2)}, u32[]{:S(2)}) async-start(f32[32,8,128]{2,1,0:T(8,128)} %get-tuple-element.27), calls=%async_computation.6 | async-start | bytes 262144 | tf_op jit(solution)/shard_map/all_to_all | solution.py:40
  147.8 9.1 %all-to-all-done.6.e_ref = f32[32,8,128]{2,1,0:T(8,128)S(1)} async-done(((f32[32,8,128]{2,1,0:T(8,128)}), f32[32,8,128]{2,1,0:T(8,128)S(1)}, u32[]{:S(2)}, u32[]{:S(2)}) %all-to-all-start.6) | async-done | bytes 131104 | tf_op jit(solution)/shard_map/all_to_all | solution.py:40
  156.9 3.4 %copy-done.1 = f32[1024,2048]{1,0:T(8,128)S(1)} copy-done((f32[1024,2048]{1,0:T(8,128)S(1)}, f32[1024,2048]{1,0:T(8,128)}, u32[]{:S(2)}) %copy-start.1) | copy-done | bytes 8388632
  161.6 1.9 copy-done.2
  163.5 2.1 collective-permute-start.13
  165.7 2.2 %copy-done.3 = bf16[1024,2048]{1,0:T(8,128)(2,1)S(1)} copy-done((bf16[1024,2048]{1,0:T(8,128)(2,1)S(1)}, bf16[1024,2048]{1,0:T(8,128)(2,1)}, u32[]{:S(2)}) %copy-start.3) | copy-done | bytes 4194328
  169.8 1.8 product.7
  179.5 3.3 %collective-permute-done.18 = f32[24,128]{1,0:T(8,128)S(1)} collective-permute-done((f32[24,128]{1,0:T(8,128)S(1)}, f32[24,128]{1,0:T(8,128)S(1)}, u32[]{:S(2)}, u32[]{:S(2)}) %collective-permute-start.18) | collective-permute-done | bytes 12320 | tf_op jit(solution)/shard_map/ppermute | solution.py:36
  183.1 3.5 %collective-permute-done.15 = f32[24,128]{1,0:T(8,128)S(1)} collective-permute-done((f32[24,128]{1,0:T(8,128)S(1)}, f32[24,128]{1,0:T(8,128)S(1)}, u32[]{:S(2)}, u32[]{:S(2)}) %collective-permute-start.15) | collective-permute-done | bytes 12320 | tf_op jit(solution)/shard_map/ppermute | solution.py:36
  187.1 2.2 %collective-permute-start.17 = (f16[128,2048]{1,0:T(8,128)(2,1)S(1)}, f16[128,2048]{1,0:T(8,128)(2,1)S(1)}, u32[]{:S(2)}, u32[]{:S(2)}) collective-permute-start(f16[128,2048]{1,0:T(8,128)(2,1)S(1)} %multiply_convert_fusion.1), channel_id=1, source_target_pairs={{0,128},{64,192},{128,0},{192,64},{1,129},{65,193},{129,1},{193,65... | collective-permute-start | bytes 1572872 | tf_op jit(solution)/shard_map/ppermute | solution.py:36
  190.1 8.5 %collective-permute-done.14 = f16[128,2048]{1,0:T(8,128)(2,1)S(1)} collective-permute-done((f16[128,2048]{1,0:T(8,128)(2,1)S(1)}, f16[128,2048]{1,0:T(8,128)(2,1)S(1)}, u32[]{:S(2)}, u32[]{:S(2)}) %collective-permute-start.14) | collective-permute-done | bytes 524320 | tf_op jit(solution)/shard_map/ppermute | solution.py:36
  198.6 10.3 %collective-permute-done.17 = f16[128,2048]{1,0:T(8,128)(2,1)S(1)} collective-permute-done((f16[128,2048]{1,0:T(8,128)(2,1)S(1)}, f16[128,2048]{1,0:T(8,128)(2,1)S(1)}, u32[]{:S(2)}, u32[]{:S(2)}) %collective-permute-start.17) | collective-permute-done | bytes 524320 | tf_op jit(solution)/shard_map/ppermute | solution.py:36
  208.9 4.0 %collective-permute-done.20 = f16[128,2048]{1,0:T(8,128)(2,1)S(1)} collective-permute-done((f16[128,2048]{1,0:T(8,128)(2,1)S(1)}, f16[128,2048]{1,0:T(8,128)(2,1)S(1)}, u32[]{:S(2)}, u32[]{:S(2)}) %collective-permute-start.20) | collective-permute-done | bytes 524320 | tf_op jit(solution)/shard_map/ppermute | solution.py:36
  (82 shorter events, 31.5 us)
Async XLA Ops:
  0.6 73.0 %copy-start.12 = (f32[1024]{0:T(1024)S(1)}, f32[1024]{0:T(1024)}, u32[]{:S(2)}) copy-start(f32[1024]{0:T(1024)} %param.6) | copy-start | bytes 12292
  0.6 5.8 %collective-permute-start = (bf16[32,1024]{1,0:T(8,128)(2,1)}, bf16[32,1024]{1,0:T(8,128)(2,1)S(1)}, u32[]{:S(2)}, u32[]{:S(2)}) collective-permute-start(bf16[32,1024]{1,0:T(8,128)(2,1)} %bitcast.56), channel_id=1, source_target_pairs={{0,1},{1,2},{2,3},{3,0},{4,5},{5,6},{6,7},{7,4},{8,9},{9,10},{10,1... | collective-permute-start | bytes 196616 | tf_op jit(solution)/shard_map/ppermute | solution.py:36
  2.7 5.3 %collective-permute-start.1 = (bf16[32,1024]{1,0:T(8,128)(2,1)}, bf16[32,1024]{1,0:T(8,128)(2,1)S(1)}, u32[]{:S(2)}, u32[]{:S(2)}) collective-permute-start(bf16[32,1024]{1,0:T(8,128)(2,1)} %bitcast.57), channel_id=1, source_target_pairs={{0,2},{1,3},{2,0},{3,1},{4,6},{5,7},{6,4},{7,5},{8,10},{9,11},{10,... | collective-permute-start | bytes 196616 | tf_op jit(solution)/shard_map/ppermute | solution.py:36
  5.2 3.6 %collective-permute-start.2 = (bf16[32,1024]{1,0:T(8,128)(2,1)}, bf16[32,1024]{1,0:T(8,128)(2,1)S(1)}, u32[]{:S(2)}, u32[]{:S(2)}) collective-permute-start(bf16[32,1024]{1,0:T(8,128)(2,1)} %bitcast.58), channel_id=1, source_target_pairs={{0,3},{1,0},{2,1},{3,2},{4,7},{5,4},{6,5},{7,6},{8,11},{9,8},{10,9... | collective-permute-start | bytes 196616 | tf_op jit(solution)/shard_map/ppermute | solution.py:36
  10.2 9.7 %collective-permute-start.4 = (bf16[128,1024]{1,0:T(8,128)(2,1)S(1)}, bf16[128,1024]{1,0:T(8,128)(2,1)S(1)}, u32[]{:S(2)}, u32[]{:S(2)}) collective-permute-start(bf16[128,1024]{1,0:T(8,128)(2,1)S(1)} %strip.1.s_ref), channel_id=1, source_target_pairs={{0,28},{4,0},{8,4},{12,8},{16,12},{20,16},{24,20},{28,24},{1,29},{... | collective-permute-start | bytes 786440 | tf_op jit(solution)/shard_map/ppermute | solution.py:36
  16.1 7.2 %collective-permute-start.3 = (bf16[128,1024]{1,0:T(8,128)(2,1)S(1)}, bf16[128,1024]{1,0:T(8,128)(2,1)S(1)}, u32[]{:S(2)}, u32[]{:S(2)}) collective-permute-start(bf16[128,1024]{1,0:T(8,128)(2,1)S(1)} %strip.1.s_ref), channel_id=1, source_target_pairs={{0,4},{4,8},{8,12},{12,16},{16,20},{20,24},{24,28},{28,0},{1,5},{5... | collective-permute-start | bytes 786440 | tf_op jit(solution)/shard_map/ppermute | solution.py:36
  19.9 6.7 %collective-permute-start.6 = (bf16[128,1024]{1,0:T(8,128)(2,1)S(1)}, bf16[128,1024]{1,0:T(8,128)(2,1)S(1)}, u32[]{:S(2)}, u32[]{:S(2)}) collective-permute-start(bf16[128,1024]{1,0:T(8,128)(2,1)S(1)} %collective-permute-done.4.l1), channel_id=1, source_target_pairs={{0,28},{4,0},{8,4},{12,8},{16,12},{20,16},{24,20},{28,24},{1,29},{... | collective-permute-start | bytes 786440 | tf_op jit(solution)/shard_map/ppermute | solution.py:36
  23.4 7.1 %collective-permute-start.5 = (bf16[128,1024]{1,0:T(8,128)(2,1)S(1)}, bf16[128,1024]{1,0:T(8,128)(2,1)S(1)}, u32[]{:S(2)}, u32[]{:S(2)}) collective-permute-start(bf16[128,1024]{1,0:T(8,128)(2,1)S(1)} %collective-permute-done.3.r1), channel_id=1, source_target_pairs={{0,4},{4,8},{8,12},{12,16},{16,20},{20,24},{24,28},{28,0},{1,5},{5... | collective-permute-start | bytes 786440 | tf_op jit(solution)/shard_map/ppermute | solution.py:36
  26.7 6.4 %collective-permute-start.8 = (bf16[128,1024]{1,0:T(8,128)(2,1)S(1)}, bf16[128,1024]{1,0:T(8,128)(2,1)S(1)}, u32[]{:S(2)}, u32[]{:S(2)}) collective-permute-start(bf16[128,1024]{1,0:T(8,128)(2,1)S(1)} %collective-permute-done.6.l2), channel_id=1, source_target_pairs={{0,28},{4,0},{8,4},{12,8},{16,12},{20,16},{24,20},{28,24},{1,29},{... | collective-permute-start | bytes 786440 | tf_op jit(solution)/shard_map/ppermute | solution.py:36
  30.5 6.4 %copy-start.7 = (bf16[128,1024]{1,0:T(8,128)(2,1)}, bf16[128,1024]{1,0:T(8,128)(2,1)S(1)}, u32[]{:S(2)}) copy-start(bf16[128,1024]{1,0:T(8,128)(2,1)S(1)} %collective-permute-done.5.r2) | copy-start | bytes 786436
  30.5 6.4 %collective-permute-start.7 = (bf16[128,1024]{1,0:T(8,128)(2,1)S(1)}, bf16[128,1024]{1,0:T(8,128)(2,1)S(1)}, u32[]{:S(2)}, u32[]{:S(2)}) collective-permute-start(bf16[128,1024]{1,0:T(8,128)(2,1)S(1)} %collective-permute-done.5.r2), channel_id=1, source_target_pairs={{0,4},{4,8},{8,12},{12,16},{16,20},{20,24},{24,28},{28,0},{1,5},{5... | collective-permute-start | bytes 786440 | tf_op jit(solution)/shard_map/ppermute | solution.py:36
  33.1 5.7 %collective-permute-start.10 = (bf16[64,1024]{1,0:T(8,128)(2,1)S(1)}, bf16[64,1024]{1,0:T(8,128)(2,1)S(1)}, u32[]{:S(2)}, u32[]{:S(2)}) collective-permute-start(bf16[64,1024]{1,0:T(8,128)(2,1)S(1)} %slice.40), channel_id=1, source_target_pairs={{0,28},{4,0},{8,4},{12,8},{16,12},{20,16},{24,20},{28,24},{1,29},{... | collective-permute-start | bytes 393224 | tf_op jit(solution)/shard_map/ppermute | solution.py:36
  36.9 6.0 %collective-permute-start.9 = (bf16[64,1024]{1,0:T(8,128)(2,1)S(1)}, bf16[64,1024]{1,0:T(8,128)(2,1)S(1)}, u32[]{:S(2)}, u32[]{:S(2)}) collective-permute-start(bf16[64,1024]{1,0:T(8,128)(2,1)S(1)} %slice.39), channel_id=1, source_target_pairs={{0,4},{4,8},{8,12},{12,16},{16,20},{20,24},{24,28},{28,0},{1,5},{5... | collective-permute-start | bytes 393224 | tf_op jit(solution)/shard_map/ppermute | solution.py:36
  43.6 2.2 %copy-start.4 = (bf16[2048,1024]{1,0:T(8,128)(2,1)S(1)}, bf16[2048,1024]{1,0:T(8,128)(2,1)}, u32[]{:S(2)}) copy-start(bf16[2048,1024]{1,0:T(8,128)(2,1)} %c_ref.1) | copy-start | bytes 12582916
  73.6 3.4 %copy-start = (f32[1024,2048]{1,0:T(8,128)S(1)}, f32[1024,2048]{1,0:T(8,128)}, u32[]{:S(2)}) copy-start(f32[1024,2048]{1,0:T(8,128)} %get-tuple-element.22.k_ref) | copy-start | bytes 25165828
  77.0 17.7 %copy-start.11 = (f32[2048]{0:T(1024)S(1)}, f32[2048]{0:T(1024)}, u32[]{:S(2)}) copy-start(f32[2048]{0:T(1024)} %param.7) | copy-start | bytes 24580
  143.6 13.3 %all-to-all-start.6 = ((f32[32,8,128]{2,1,0:T(8,128)}), f32[32,8,128]{2,1,0:T(8,128)S(1)}, u32[]{:S(2)}, u32[]{:S(2)}) async-start(f32[32,8,128]{2,1,0:T(8,128)} %get-tuple-element.27), calls=%async_computation.6 | async-start | bytes 262144 | tf_op jit(solution)/shard_map/all_to_all | solution.py:40
  156.9 3.4 %copy-start.1 = (f32[1024,2048]{1,0:T(8,128)S(1)}, f32[1024,2048]{1,0:T(8,128)}, u32[]{:S(2)}) copy-start(f32[1024,2048]{1,0:T(8,128)} %get-tuple-element.22.k_ref) | copy-start | bytes 25165828
  161.6 2.0 copy-start.2
  163.5 12.6 %collective-permute-start.13 = (f32[24,128]{1,0:T(8,128)S(1)}, f32[24,128]{1,0:T(8,128)S(1)}, u32[]{:S(2)}, u32[]{:S(2)}) collective-permute-start(f32[24,128]{1,0:T(8,128)S(1)} %get-tuple-element.35), channel_id=1, source_target_pairs={{0,32},{32,0},{1,33},{33,1},{2,34},{34,2},{3,35},{35,3},{4,36},{36... | collective-permute-start | bytes 36872 | tf_op jit(solution)/shard_map/ppermute | solution.py:36
  165.7 2.2 %copy-start.3 = (bf16[1024,2048]{1,0:T(8,128)(2,1)S(1)}, bf16[1024,2048]{1,0:T(8,128)(2,1)}, u32[]{:S(2)}) copy-start(bf16[1024,2048]{1,0:T(8,128)(2,1)} %copy-done.2) | copy-start | bytes 12582916
  169.7 20.4 %collective-permute-start.11 = (f32[128,2048]{1,0:T(8,128)S(1)}, f32[128,2048]{1,0:T(8,128)S(1)}, u32[]{:S(2)}, u32[]{:S(2)}) collective-permute-start(f32[128,2048]{1,0:T(8,128)S(1)} %get-tuple-element.32), channel_id=1, source_target_pairs={{0,32},{32,0},{1,33},{33,1},{2,34},{34,2},{3,35},{35,3},{4,36},{36... | collective-permute-start | bytes 3145736 | tf_op jit(solution)/shard_map/ppermute | solution.py:36
  171.6 15.0 %collective-permute-start.12 = (f32[128,2048]{1,0:T(8,128)S(1)}, f32[128,2048]{1,0:T(8,128)S(1)}, u32[]{:S(2)}, u32[]{:S(2)}) collective-permute-start(f32[128,2048]{1,0:T(8,128)S(1)} %get-tuple-element.34), channel_id=1, source_target_pairs={{0,32},{32,0},{1,33},{33,1},{2,34},{34,2},{3,35},{35,3},{4,36},{36... | collective-permute-start | bytes 3145736 | tf_op jit(solution)/shard_map/ppermute | solution.py:36
  174.7 12.2 %collective-permute-start.16 = (f32[128,2048]{1,0:T(8,128)S(1)}, f32[128,2048]{1,0:T(8,128)S(1)}, u32[]{:S(2)}, u32[]{:S(2)}) collective-permute-start(f32[128,2048]{1,0:T(8,128)S(1)} %product.9), channel_id=1, source_target_pairs={{0,32},{32,0},{1,33},{33,1},{2,34},{34,2},{3,35},{35,3},{4,36},{36... | collective-permute-start | bytes 3145736 | tf_op jit(solution)/shard_map/ppermute | solution.py:36
  175.6 13.7 %collective-permute-start.19 = (f32[128,2048]{1,0:T(8,128)S(1)}, f32[128,2048]{1,0:T(8,128)S(1)}, u32[]{:S(2)}, u32[]{:S(2)}) collective-permute-start(f32[128,2048]{1,0:T(8,128)S(1)} %get-tuple-element.37), channel_id=1, source_target_pairs={{0,32},{32,0},{1,33},{33,1},{2,34},{34,2},{3,35},{35,3},{4,36},{36... | collective-permute-start | bytes 3145736 | tf_op jit(solution)/shard_map/ppermute | solution.py:36
  176.2 2.6 %collective-permute-start.21 = (f32[24,128]{1,0:T(8,128)S(1)}, f32[24,128]{1,0:T(8,128)S(1)}, u32[]{:S(2)}, u32[]{:S(2)}) collective-permute-start(f32[24,128]{1,0:T(8,128)S(1)} %pad_maximum_fusion), channel_id=1, source_target_pairs={{0,192},{64,0},{128,64},{192,128},{1,193},{65,1},{129,65},{193,129... | collective-permute-start | bytes 36872 | tf_op jit(solution)/shard_map/ppermute | solution.py:36
  178.8 4.0 %collective-permute-start.18 = (f32[24,128]{1,0:T(8,128)S(1)}, f32[24,128]{1,0:T(8,128)S(1)}, u32[]{:S(2)}, u32[]{:S(2)}) collective-permute-start(f32[24,128]{1,0:T(8,128)S(1)} %pad_maximum_fusion), channel_id=1, source_target_pairs={{0,128},{64,192},{128,0},{192,64},{1,129},{65,193},{129,1},{193,65... | collective-permute-start | bytes 36872 | tf_op jit(solution)/shard_map/ppermute | solution.py:36
  182.8 3.8 %collective-permute-start.15 = (f32[24,128]{1,0:T(8,128)S(1)}, f32[24,128]{1,0:T(8,128)S(1)}, u32[]{:S(2)}, u32[]{:S(2)}) collective-permute-start(f32[24,128]{1,0:T(8,128)S(1)} %pad_maximum_fusion), channel_id=1, source_target_pairs={{0,64},{64,128},{128,192},{192,0},{1,65},{65,129},{129,193},{193,1... | collective-permute-start | bytes 36872 | tf_op jit(solution)/shard_map/ppermute | solution.py:36
  186.6 27.7 %copy-start.14 = (f32[2048]{0:T(1024)}, f32[2048]{0:T(1024)S(1)}, u32[]{:S(2)}) copy-start(f32[2048]{0:T(1024)S(1)} %get-tuple-element.39) | copy-start | bytes 24580
  186.8 11.8 %collective-permute-start.14 = (f16[128,2048]{1,0:T(8,128)(2,1)S(1)}, f16[128,2048]{1,0:T(8,128)(2,1)S(1)}, u32[]{:S(2)}, u32[]{:S(2)}) collective-permute-start(f16[128,2048]{1,0:T(8,128)(2,1)S(1)} %multiply_convert_fusion.2), channel_id=1, source_target_pairs={{0,64},{64,128},{128,192},{192,0},{1,65},{65,129},{129,193},{193,1... | collective-permute-start | bytes 1572872 | tf_op jit(solution)/shard_map/ppermute | solution.py:36
  187.1 21.8 %collective-permute-start.17 = (f16[128,2048]{1,0:T(8,128)(2,1)S(1)}, f16[128,2048]{1,0:T(8,128)(2,1)S(1)}, u32[]{:S(2)}, u32[]{:S(2)}) collective-permute-start(f16[128,2048]{1,0:T(8,128)(2,1)S(1)} %multiply_convert_fusion.1), channel_id=1, source_target_pairs={{0,128},{64,192},{128,0},{192,64},{1,129},{65,193},{129,1},{193,65... | collective-permute-start | bytes 1572872 | tf_op jit(solution)/shard_map/ppermute | solution.py:36
  189.4 23.5 %collective-permute-start.20 = (f16[128,2048]{1,0:T(8,128)(2,1)S(1)}, f16[128,2048]{1,0:T(8,128)(2,1)S(1)}, u32[]{:S(2)}, u32[]{:S(2)}) collective-permute-start(f16[128,2048]{1,0:T(8,128)(2,1)S(1)} %multiply_convert_fusion), channel_id=1, source_target_pairs={{0,192},{64,0},{128,64},{192,128},{1,193},{65,1},{129,65},{193,129... | collective-permute-start | bytes 1572872 | tf_op jit(solution)/shard_map/ppermute | solution.py:36
  (6 other events, 5.0 us)

commit v2 on v1

v2 whole, which is shorter than its diff:
```python
import functools

import jax
import jax.numpy as jnp
from jax import lax
from jax.experimental import pallas as pl
from jax.experimental.pallas import tpu as pltpu
from jax.sharding import Mesh
from jax.sharding import PartitionSpec as P

ITERS = 3
ROWS = 1024
COLS = 2048
RB, CB = ROWS // 128, COLS // 128
CENT = ("z", "x")
DP = ("y", "core")
F32, BF16 = jnp.float32, jnp.bfloat16
VM = pl.BlockSpec(memory_space=pltpu.VMEM)
SM = pl.BlockSpec(memory_space=pltpu.SMEM)


def call(body, outs, ins, scratch=(), mib=24, aliases=None):
    return pl.pallas_call(
        body,
        out_shape=[jax.ShapeDtypeStruct(s, d) for s, d in outs],
        in_specs=[SM if a.dtype == jnp.int32 else VM for a in ins],
        out_specs=[VM] * len(outs),
        scratch_shapes=list(scratch),
        input_output_aliases=aliases or {},
        compiler_params=pltpu.CompilerParams(vmem_limit_bytes=mib << 20),
    )(*ins)


def step(x, axis, by):
    n = lax.axis_size(axis)
    return lax.ppermute(x, axis, [(i, (i + by) % n) for i in range(n)])


def everyone(x, axis):
    return lax.all_to_all(x, axis, 0, 0, tiled=True)


def after(x, *others):
    return lax.optimization_barrier((x, *others))[0]


def down(row):
    return jnp.broadcast_to(row, (128, 128)).T


def around(at_ref, k, by, n):
    return lax.rem(at_ref[k] + (n + by), n)


def join_body(a_ref, b_ref, o_ref):
    o_ref[0:32, :] = a_ref[...]
    o_ref[32:64, :] = b_ref[...]


def collect(at_ref, pieces, c_ref, ft_ref, fa_ref, fs_ref, cs_ref):
    for k, (by, first, second) in enumerate(pieces):
        at = around(at_ref, 2, by, 8)
        for half, refs in ((0, first), (1, second)):
            for j, (ref, row) in enumerate(refs):
                x = around(at_ref, 3, (0, -1, 1, 2)[2 * half + j], 4)
                ft_ref[4 * at + x] = ref[row : row + 32, :]
        piece = ft_ref[pl.ds(4 * at, 4)].reshape(128, ROWS)
        top = jnp.max(jnp.abs(piece.astype(F32)), axis=0, keepdims=True)
        fa_ref[pl.ds(at, 1), :] = jnp.broadcast_to(jnp.max(top, axis=1, keepdims=True), (1, 128))
        fs_ref[:, 128 * k : 128 * k + 128] = piece.T
        cs_ref[:, 128 * k : 128 * k + 128] = c_ref[:, pl.ds(pl.multiple_of(at * 128, 128), 128)]


def product(f, c):
    return lax.dot_general(f, c, (((1,), (1,)), ((), ())), preferred_element_type=F32)


def whole(ref):
    return [(ref, 0), (ref, 32)]


def score0_body(at_ref, a0, b0, ar, br, al, bl, ar2, br2, c_ref, k_ref, ft_ref, fa_ref, fs, cs):
    pieces = [(0, whole(a0), whole(b0)), (-1, whole(ar), whole(br)), (1, whole(al), whole(bl))]
    pieces.append((-2, whole(ar2), whole(br2)))
    collect(at_ref, pieces, c_ref, ft_ref, fa_ref, fs, cs)

    def block(b, carry):
        rows = pl.ds(pl.multiple_of(256 * b, 256), 256)
        k_ref[rows, :] = product(fs[rows, :], cs[...])
        return carry

    lax.fori_loop(0, 4, block, 0)


def score1_body(at_ref, al2, bl2, ar3, br3, c_ref, kin, ftin, fain, k_ref, ft_ref, fa_ref, fs, cs):
    collect(
        at_ref,
        [(2, whole(al2), whole(bl2)), (-3, whole(ar3), whole(br3))],
        c_ref, ft_ref, fa_ref, fs, cs,
    )

    def block(b, carry):
        rows = pl.ds(pl.multiple_of(256 * b, 256), 256)
        k_ref[rows, :] = kin[rows, :] + product(fs[rows, :], cs[...])
        return carry

    lax.fori_loop(0, 4, block, 0)


def score2_body(
    at_ref, al3, bl3, ah0, ah1, bh0, bh1, c_ref, kin, ftin, fain, k_ref, ft_ref, fa_ref, p_ref, fs, cs
):
    far = (4, [(ah0, 0), (ah1, 0)], [(bh0, 0), (bh1, 0)])
    collect(at_ref, [(3, whole(al3), whole(bl3)), far], c_ref, ft_ref, fa_ref, fs, cs)

    def block(b, carry):
        rows = pl.ds(pl.multiple_of(128 * b, 128), 128)
        s = kin[rows, :] + product(fs[rows, :], cs[...])
        top = jnp.max(s, axis=1, keepdims=True)
        e = jnp.exp(s - top)
        k_ref[rows, :] = e
        total = jnp.sum(e, axis=1, keepdims=True)
        for k, v in ((0, top), (RB, total)):
            line = jnp.broadcast_to(v, (128, 128)).T[0:1][None]
            p_ref[:, pl.ds(k + b, 1), :] = jnp.broadcast_to(line, (32, 1, 128))
        return carry

    lax.fori_loop(0, RB, block, 0)


def columns(k_ref, scale, o_ref):
    acc = [jnp.zeros((8, 128), F32)] * CB
    for b in range(RB):
        rows = slice(128 * b, 128 * b + 128)
        by = down(scale[b : b + 1])
        for t in range(CB):
            part = k_ref[rows, 128 * t : 128 * t + 128] * by
            acc[t] = acc[t] + jnp.sum(part.reshape(16, 8, 128), axis=0)
    z = jnp.concatenate([jnp.sum(a, axis=0, keepdims=True) for a in acc], axis=0)
    o_ref[...] = jnp.broadcast_to(z[None], o_ref.shape)


def first_column_body(e_ref, mine_ref, a_ref, k_ref, o_ref, f_ref):
    peaks = e_ref[:, 0:RB, :]
    top = jnp.max(peaks, axis=0)
    total = jnp.sum(e_ref[:, RB : 2 * RB, :] * jnp.exp(peaks - top[None]), axis=0)
    fold = jnp.exp(mine_ref[0, 0:RB, :] - top)
    f_ref[...] = fold
    columns(k_ref, (a_ref[...] / total) * fold, o_ref)


def column_body(e_ref, f_ref, a_ref, k_ref, o_ref):
    scale = a_ref[...] / jnp.sum(e_ref[...], axis=0)
    columns(k_ref, scale * f_ref[...], o_ref)


def row_body(e_ref, f_ref, b_ref, k_ref, o_ref, c_ref):
    scale = b_ref[...] / jnp.sum(e_ref[...], axis=0)
    c_ref[...] = scale
    lines = []
    for b in range(RB):
        rows = slice(128 * b, 128 * b + 128)
        acc = jnp.zeros((128, 128), F32)
        for t in range(CB):
            acc = acc + k_ref[rows, 128 * t : 128 * t + 128] * scale[t : t + 1]
        lines.append(jnp.sum(acc.T, axis=0, keepdims=True))
    y = jnp.concatenate(lines, axis=0) * f_ref[...]
    o_ref[...] = jnp.broadcast_to(y[None], o_ref.shape)


def target(at_ref, by, side):
    return 2 * around(at_ref, 0, by, 4) + around(at_ref, 1, side, 2)


def product_of(at_ref, ft_ref, w_ref, o_ref, by, side):
    d = 4 * target(at_ref, by, side)

    def block(b, carry):
        cols = pl.ds(pl.multiple_of(512 * b, 512), 512)
        feats = ft_ref[pl.ds(d, 4)].reshape(128, ROWS)
        o_ref[:, cols] = jnp.dot(feats, w_ref[:, cols], preferred_element_type=F32)
        return carry

    lax.fori_loop(0, COLS // 512, block, 0)


def weight_body(
    at_ref, e_ref, f_ref, a_ref, c_ref, fa_ref, k_ref, ft_ref, w_ref, m_ref, o_ref
):
    scale = (a_ref[...] / jnp.sum(e_ref[...], axis=0)) * f_ref[...]
    acc = [jnp.zeros((8, 128), F32)] * CB
    for b in range(RB):
        rows = slice(128 * b, 128 * b + 128)
        by = down(scale[b : b + 1])
        for t in range(CB):
            cols = slice(128 * t, 128 * t + 128)
            part = (k_ref[rows, cols] * by) * c_ref[t : t + 1, :]
            acc[t] = acc[t] + jnp.sum(part.reshape(16, 8, 128), axis=0)
            w_ref[rows, cols] = part.astype(BF16)
    m_ref[0:CB, :] = jnp.concatenate([jnp.sum(a, axis=0, keepdims=True) for a in acc], axis=0)
    m_ref[CB : CB + 8, :] = fa_ref[...]
    product_of(at_ref, ft_ref, w_ref, o_ref, 2, 1)


def limits(at_ref, m, by):
    return m[0:CB, :] * m[pl.ds(CB + target(at_ref, by, 0), 1), :]


def chip_body(at_ref, mine_ref, other_ref, m_ref, i_ref):
    m_ref[0:CB, :] = mine_ref[0:CB, :] + other_ref[0:CB, :]
    m_ref[CB : CB + 8, :] = jnp.maximum(mine_ref[CB : CB + 8, :], other_ref[CB : CB + 8, :])
    for k, by in enumerate((2, 1, 3)):
        q = limits(at_ref, m_ref, by)
        i_ref[k] = jnp.where(q > 0, 32768.0 / jnp.where(q > 0, q, 1.0), 0.0)


def share_body(at_ref, m0, m1, m2, m3, t_ref, i_ref, s_ref):
    total = (m0[0:CB, :] + m2[0:CB, :]) + (m1[0:CB, :] + m3[0:CB, :])
    t_ref[...] = total
    i_ref[...] = 1.0 / total
    for k, m in enumerate((m2, m1, m3)):
        s_ref[k] = (limits(at_ref, m, 0) * (1.0 / 32768.0)) / total


def product_body(which, at_ref, ft_ref, w_ref, *o_refs):
    for k, o_ref in enumerate(o_refs):
        product_of(at_ref, ft_ref, w_ref, o_ref, *which[k])


def assigned(features, centroids, row_weight, centroid_share):
    y, core, z, x = (lax.axis_index(n) for n in ("y", "core", "z", "x"))
    at = jnp.stack([y, core, z, x]).astype(jnp.int32)
    a = row_weight.reshape(RB, 128)
    share = centroid_share.reshape(CB, 128)

    own = after(features.T, at)
    (half_a,) = call(join_body, [((64, ROWS), BF16)], [own, step(own, "x", 1)], mib=4)
    (half_b,) = call(
        join_body, [((64, ROWS), BF16)], [step(own, "x", -1), step(own, "x", 2)], mib=4
    )
    right, left = {0: [half_a, half_b]}, {0: [half_a, half_b]}
    for k in (1, 2, 3):
        right[k] = [step(h, "z", 1) for h in right[k - 1]]
        left[k] = [step(h, "z", -1) for h in left[k - 1]]
    state = [((ROWS, COLS), F32), ((32, 32, ROWS), BF16), ((8, 128), F32)]
    kernel, ft, fa = call(
        score0_body,
        state,
        [at, *right[0], *right[1], *left[1], *right[2], centroids],
        scratch=[pltpu.VMEM((ROWS, 512), BF16), pltpu.VMEM((COLS, 512), BF16)],
        mib=16,
    )
    far = []
    for h in (0, 1):
        far += [step(after(right[3][h], fa)[:32], "z", 1), step(after(left[3][h], fa)[32:], "z", -1)]
    two = [pltpu.VMEM((ROWS, 256), BF16), pltpu.VMEM((COLS, 256), BF16)]
    kernel, ft, fa = call(
        score1_body,
        state,
        [at, *left[2], *right[3], centroids, kernel, ft, fa],
        scratch=two,
        mib=16,
        aliases={6: 0, 7: 1, 8: 2},
    )
    kernel, ft, fa, peaks = call(
        score2_body,
        [*state, ((32, 2 * RB, 128), F32)],
        [at, *left[3], *far, centroids, kernel, ft, fa],
        scratch=two,
        mib=16,
        aliases={8: 0, 9: 1, 10: 2},
    )
    got = everyone(peaks, CENT)
    sums, fold = call(
        first_column_body, [((8, CB, 128), F32), ((RB, 128), F32)], [got, peaks, a, kernel], mib=8
    )
    for it in range(ITERS):
        rows, cscale = call(
            row_body,
            [((32, RB, 128), F32), ((CB, 128), F32)],
            [everyone(sums, DP), fold, share, kernel],
            mib=8,
        )
        got = everyone(rows, CENT)
        if it < ITERS - 1:
            (sums,) = call(column_body, [((8, CB, 128), F32)], [got, fold, a, kernel], mib=8)
    weights, mass, give = call(
        weight_body,
        [((ROWS, COLS), BF16), ((CB + 8, 128), F32), ((128, COLS), F32)],
        [at, got, fold, a, cscale, fa, kernel, ft],
        mib=16,
    )

    chip, inverse = call(
        chip_body,
        [((CB + 8, 128), F32), ((3, CB, 128), F32)],
        [at, mass, step(mass, "core", 1)],
        mib=4,
    )
    inverse = inverse.reshape(3, 1, COLS)

    def products(which, where):
        return call(
            functools.partial(product_body, which),
            [((128, COLS), F32)] * len(which),
            [where, ft, weights],
            mib=16,
        )

    def send(x, by):
        return step(x, "y", by)

    def packed(mine, theirs, k):
        return ((mine + theirs) * inverse[k]).astype(jnp.float16)

    theirs = step(give, "core", 1)
    (mine,) = products([(2, 0)], at)
    ready = packed(mine, theirs, 0)
    sent = [send(ready, 2)]
    gives = products([(1, 1), (3, 1)], after(at, ready))
    theirs = [step(g, "core", 1) for g in gives]
    mines = products([(1, 0), (3, 0)], after(at, *gives))
    ready = [packed(m, t, k) for m, t, k in zip(mines, theirs, (1, 2))]
    sent += [send(ready[0], 1), send(ready[1], 3)]
    give, mine = products([(0, 1), (0, 0)], after(at, *ready))
    theirs = step(give, "core", 1)
    chip = after(chip, *ready)
    total, over, shares = call(
        share_body,
        [((CB, 128), F32), ((CB, 128), F32), ((3, CB, 128), F32)],
        [at, chip, *(step(chip, "y", k) for k in (1, 2, 3))],
        mib=4,
    )
    shares = shares.reshape(3, 1, COLS)
    means = (mine + theirs) * over.reshape(1, COLS)
    for k in range(3):
        means = means + sent[k].astype(F32) * shares[k]
    return means, total.reshape(COLS)


def solution(mesh):
    split = Mesh(mesh.devices.reshape(4, 2, 8, 4), ("y", "core", "z", "x"))
    return jax.shard_map(
        assigned,
        mesh=split,
        in_specs=(P(DP, CENT), P(CENT, None), P(DP), P(CENT)),
        out_specs=(P(DP, CENT), P(CENT)),
        check_vma=False,
    )
```

time: 215 us -> 204 us (0.949)
  waiting for transfers between devices: 58.5 us -> 29.2 us
  local copies, waits for them, and re-layouts: 18.2 us -> 3.06 us
  Pallas kernels: 24.4 us -> 36.9 us
  blocking collectives: 76 us -> 88.5 us
  starting transfers between devices: 34.1 us -> 42 us
    ppermute x22 -> x30, waiting for transfers between devices: 49.5 us -> 29.2 us  [step(): return lax.ppermute(x, axis, [(i, (i + by) % n) for i in range(n)])]
    unnamed x30 -> x8, local copies, waits for them, and re-layouts: 18.1 us -> 3.03 us
    pallas_call x14 -> x18, Pallas kernels: 24.4 us -> 36.9 us  [call(): pl.pallas_call(body, out_shape=[jax.ShapeDtypeStruct(s, d) for s, d in ou...]
    all_to_all x6 -> x7, blocking collectives: 76 us -> 88.5 us  [everyone(): return lax.all_to_all(x, axis, 0, 0, tiled=True)]
    ppermute x22 -> x30, starting transfers between devices: 30 us -> 42 us  [step(): return lax.ppermute(x, axis, [(i, (i + by) % n) for i in range(n)])]
    all_to_all x1 -> x0, waiting for transfers between devices: 9.06 us -> none  [everyone(): return lax.all_to_all(x, axis, 0, 0, tiled=True)]
    all_to_all x1 -> x0, starting transfers between devices: 4.08 us -> none  [everyone(): return lax.all_to_all(x, axis, 0, 0, tiled=True)]
  transfers between devices with their start and end apart: 23 -> 30, of which waited for: 15 -> 10; matrix products, arithmetic and copies ran while one was open for 0% -> 0% of each run, Pallas kernels for 3% -> 7%
where the time goes in v2:
time: 204 us; the launch traced here: 203 us
  blocking collectives  88.5 us (43%)
  starting transfers between devices  42 us (21%)
  Pallas kernels  36.9 us (18%)
  waiting for transfers between devices  29.2 us (14%)
  local copies, waits for them, and re-layouts  3.06 us (2%)
    all_to_all x7, blocking collectives, everyone(): return lax.all_to_all(x, axis, 0, 0, tiled=True)  88.5 us
    ppermute x30, starting transfers between devices, step(): return lax.ppermute(x, axis, [(i, (i + by) % n) for i in range(n)])  42 us
    pallas_call x18, Pallas kernels, call(): pl.pallas_call(body, out_shape=[jax.ShapeDtypeStruct(s, d) for s, d in ou...  36.9 us
    ppermute x30, waiting for transfers between devices, step(): return lax.ppermute(x, axis, [(i, (i + by) % n) for i in range(n)])  29.2 us
  transfers between devices with their start and end apart: 30, of which 10 were waited for; matrix products, arithmetic and copies ran while one was open for 0% of the time, Pallas kernels for 7%

profile of v2, /device:TPU:1, one launch (start us, length us, event | category | flops | bytes accessed | tf_op | source)
XLA Modules:
  0.0 202.6 jit_solution(7872384932349437701)
XLA Ops:
  0.7 3.6 %collective-permute-start.5 = (bf16[32,1024]{1,0:T(8,128)(2,1)}, bf16[32,1024]{1,0:T(8,128)(2,1)S(1)}, u32[]{:S(2)}, u32[]{:S(2)}) collective-permute-start(bf16[32,1024]{1,0:T(8,128)(2,1)} %bitcast.28), channel_id=1, source_target_pairs={{0,2},{1,3},{2,0},{3,1},{4,6},{5,7},{6,4},{7,5},{8,10},{9,11},{10,... | collective-permute-start | bytes 196616 | tf_op jit(solution)/shard_map/ppermute | solution.py:36
  6.2 2.4 %collective-permute-done.4.a_ref = bf16[32,1024]{1,0:T(8,128)(2,1)S(1)} collective-permute-done((bf16[32,1024]{1,0:T(8,128)(2,1)}, bf16[32,1024]{1,0:T(8,128)(2,1)S(1)}, u32[]{:S(2)}, u32[]{:S(2)}) %collective-permute-start.4) | collective-permute-done | bytes 65568 | tf_op jit(solution)/shard_map/ppermute | solution.py:36
  8.6 5.4 %collective-permute-start.6 = (bf16[64,1024]{1,0:T(8,128)(2,1)S(1)}, bf16[64,1024]{1,0:T(8,128)(2,1)S(1)}, u32[]{:S(2)}, u32[]{:S(2)}) collective-permute-start(bf16[64,1024]{1,0:T(8,128)(2,1)S(1)} %shard_map.60.b0), channel_id=1, source_target_pairs={{0,28},{4,0},{8,4},{12,8},{16,12},{20,16},{24,20},{28,24},{1,29},{... | collective-permute-start | bytes 393224 | tf_op jit(solution)/shard_map/ppermute | solution.py:36
  14.8 2.7 %collective-permute-start.1 = (bf16[64,1024]{1,0:T(8,128)(2,1)S(1)}, bf16[64,1024]{1,0:T(8,128)(2,1)S(1)}, u32[]{:S(2)}, u32[]{:S(2)}) collective-permute-start(bf16[64,1024]{1,0:T(8,128)(2,1)S(1)} %shard_map.59.a0), channel_id=1, source_target_pairs={{0,28},{4,0},{8,4},{12,8},{16,12},{20,16},{24,20},{28,24},{1,29},{... | collective-permute-start | bytes 393224 | tf_op jit(solution)/shard_map/ppermute | solution.py:36
  17.6 2.7 %collective-permute-start.7 = (bf16[64,1024]{1,0:T(8,128)(2,1)S(1)}, bf16[64,1024]{1,0:T(8,128)(2,1)S(1)}, u32[]{:S(2)}, u32[]{:S(2)}) collective-permute-start(bf16[64,1024]{1,0:T(8,128)(2,1)S(1)} %collective-permute-done.6.bl), channel_id=1, source_target_pairs={{0,28},{4,0},{8,4},{12,8},{16,12},{20,16},{24,20},{28,24},{1,29},{... | collective-permute-start | bytes 393224 | tf_op jit(solution)/shard_map/ppermute | solution.py:36
  20.3 2.7 %collective-permute-start.2 = (bf16[64,1024]{1,0:T(8,128)(2,1)S(1)}, bf16[64,1024]{1,0:T(8,128)(2,1)S(1)}, u32[]{:S(2)}, u32[]{:S(2)}) collective-permute-start(bf16[64,1024]{1,0:T(8,128)(2,1)S(1)} %collective-permute-done.1.al), channel_id=1, source_target_pairs={{0,28},{4,0},{8,4},{12,8},{16,12},{20,16},{24,20},{28,24},{1,29},{... | collective-permute-start | bytes 393224 | tf_op jit(solution)/shard_map/ppermute | solution.py:36
  23.3 3.2 %collective-permute-start.8 = (bf16[64,1024]{1,0:T(8,128)(2,1)S(1)}, bf16[64,1024]{1,0:T(8,128)(2,1)S(1)}, u32[]{:S(2)}, u32[]{:S(2)}) collective-permute-start(bf16[64,1024]{1,0:T(8,128)(2,1)S(1)} %collective-permute-done.7.bl2), channel_id=1, source_target_pairs={{0,28},{4,0},{8,4},{12,8},{16,12},{20,16},{24,20},{28,24},{1,29},{... | collective-permute-start | bytes 393224 | tf_op jit(solution)/shard_map/ppermute | solution.py:36
  27.0 2.7 %collective-permute-start.3 = (bf16[64,1024]{1,0:T(8,128)(2,1)S(1)}, bf16[64,1024]{1,0:T(8,128)(2,1)S(1)}, u32[]{:S(2)}, u32[]{:S(2)}) collective-permute-start(bf16[64,1024]{1,0:T(8,128)(2,1)S(1)} %collective-permute-done.2.al2), channel_id=1, source_target_pairs={{0,28},{4,0},{8,4},{12,8},{16,12},{20,16},{24,20},{28,24},{1,29},{... | collective-permute-start | bytes 393224 | tf_op jit(solution)/shard_map/ppermute | solution.py:36
  29.7 2.2 %copy-done = bf16[2048,1024]{1,0:T(8,128)(2,1)S(1)} copy-done((bf16[2048,1024]{1,0:T(8,128)(2,1)S(1)}, bf16[2048,1024]{1,0:T(8,128)(2,1)}, u32[]{:S(2)}) %copy-start) | copy-done | bytes 4194328
  31.8 4.5 %shard_map.61 = (f32[1024,2048]{1,0:T(8,128)S(1)}, bf16[32,32,1024]{2,1,0:T(8,128)(2,1)S(1)}, f32[8,128]{1,0:T(8,128)S(1)}) custom-call(s32[4]{0:T(128)S(1)} %pad_add_fusion.at_ref, bf16[64,1024]{1,0:T(8,128)(2,1)S(1)} %shard_map.59.a0, bf16[64,1024]{1,0:T(8,128)(2,1)S(1)} %shard_map.60.b0, bf16[64,1024]{1,0:T(8,128)(2,1)S(1)} %collective-permute-done.9.ar, ...), custom_call_target="tpu_custom_call" | custom-call | tf_op jit(solution)/shard_map/pallas_call | solution.py:23
  36.5 2.8 %collective-permute-start.18 = (bf16[32,1024]{1,0:T(8,128)(2,1)S(1)}, bf16[32,1024]{1,0:T(8,128)(2,1)S(1)}, u32[]{:S(2)}, u32[]{:S(2)}) collective-permute-start(bf16[32,1024]{1,0:T(8,128)(2,1)S(1)} %slice.39), channel_id=1, source_target_pairs={{0,28},{4,0},{8,4},{12,8},{16,12},{20,16},{24,20},{28,24},{1,29},{... | collective-permute-start | bytes 196616 | tf_op jit(solution)/shard_map/ppermute | solution.py:36
  39.2 2.7 %collective-permute-start.15 = (bf16[32,1024]{1,0:T(8,128)(2,1)S(1)}, bf16[32,1024]{1,0:T(8,128)(2,1)S(1)}, u32[]{:S(2)}, u32[]{:S(2)}) collective-permute-start(bf16[32,1024]{1,0:T(8,128)(2,1)S(1)} %slice.37), channel_id=1, source_target_pairs={{0,28},{4,0},{8,4},{12,8},{16,12},{20,16},{24,20},{28,24},{1,29},{... | collective-permute-start | bytes 196616 | tf_op jit(solution)/shard_map/ppermute | solution.py:36
  41.9 3.7 %shard_map.62 = (f32[1024,2048]{1,0:T(8,128)S(1)}, bf16[32,32,1024]{2,1,0:T(8,128)(2,1)S(1)}, f32[8,128]{1,0:T(8,128)S(1)}) custom-call(s32[4]{0:T(128)S(1)} %pad_add_fusion.at_ref, bf16[64,1024]{1,0:T(8,128)(2,1)S(1)} %collective-permute-done.2.al2, ...), custom_call_target="tpu_custom_call", output_to_operand_aliasing={{0}: (6, {}), {1}: (7, {}), {2}: (8, {})} | custom-call | tf_op jit(solution)/shard_map/pallas_call | solution.py:23
  46.2 7.5 %shard_map.63 = (f32[1024,2048]{1,0:T(8,128)S(1)}, bf16[32,32,1024]{2,1,0:T(8,128)(2,1)S(1)}, f32[8,128]{1,0:T(8,128)S(1)}, f32[32,16,128]{2,1,0:T(8,128)S(1)}) custom-call(s32[4]{0:T(128)S(1)} %pad_add_fusion.at_ref, bf16[64,1024]{1,0:T(8,128)(2,1)S(1)} %collective-permute-done.3.al3, ...), custom_call_target="tpu_custom_call", output_to_operand_aliasing={{0}: (8, {}), {1}: (9, {}), {2}: (10, {})} | custom-call | tf_op jit(solution)/shard_map/pallas_call | solution.py:23
  53.8 15.7 %all_to_all.35.e_ref = f32[32,16,128]{2,1,0:T(8,128)S(1)} all-to-all(f32[32,16,128]{2,1,0:T(8,128)S(1)} %get-tuple-element.53.mine_ref), channel_id=1, replica_groups=mesh['y'=4,'core'=2,'z'=8,'x'=4] {'z','x'}, dimensions={0} | all-to-all | bytes 524288 | tf_op jit(solution)/shard_map/all_to_all | solution.py:40
  70.2 16.5 %all_to_all.36.e_ref = f32[8,16,128]{2,1,0:T(8,128)S(1)} all-to-all(f32[8,16,128]{2,1,0:T(8,128)S(1)} %get-tuple-element.55), channel_id=1, replica_groups=mesh['y'=4,'core'=2,'z'=8,'x'=4] {'y','core'}, dimensions={0} | all-to-all | bytes 131072 | tf_op jit(solution)/shard_map/all_to_all | solution.py:40
  87.9 12.7 %all_to_all.37.e_ref = f32[32,8,128]{2,1,0:T(8,128)S(1)} all-to-all(f32[32,8,128]{2,1,0:T(8,128)S(1)} %get-tuple-element.57), channel_id=1, replica_groups=mesh['y'=4,'core'=2,'z'=8,'x'=4] {'z','x'}, dimensions={0} | all-to-all | bytes 262144 | tf_op jit(solution)/shard_map/all_to_all | solution.py:40
  101.3 9.5 %all_to_all.38.e_ref = f32[8,16,128]{2,1,0:T(8,128)S(1)} all-to-all(f32[8,16,128]{2,1,0:T(8,128)S(1)} %shard_map.66), channel_id=1, replica_groups=mesh['y'=4,'core'=2,'z'=8,'x'=4] {'y','core'}, dimensions={0} | all-to-all | bytes 131072 | tf_op jit(solution)/shard_map/all_to_all | solution.py:40
  111.9 12.3 %all_to_all.39.e_ref = f32[32,8,128]{2,1,0:T(8,128)S(1)} all-to-all(f32[32,8,128]{2,1,0:T(8,128)S(1)} %get-tuple-element.58), channel_id=1, replica_groups=mesh['y'=4,'core'=2,'z'=8,'x'=4] {'z','x'}, dimensions={0} | all-to-all | bytes 262144 | tf_op jit(solution)/shard_map/all_to_all | solution.py:40
  125.0 9.4 %all_to_all.40.e_ref = f32[8,16,128]{2,1,0:T(8,128)S(1)} all-to-all(f32[8,16,128]{2,1,0:T(8,128)S(1)} %shard_map.68), channel_id=1, replica_groups=mesh['y'=4,'core'=2,'z'=8,'x'=4] {'y','core'}, dimensions={0} | all-to-all | bytes 131072 | tf_op jit(solution)/shard_map/all_to_all | solution.py:40
  135.0 12.4 %all_to_all.41.e_ref = f32[32,8,128]{2,1,0:T(8,128)S(1)} all-to-all(f32[32,8,128]{2,1,0:T(8,128)S(1)} %get-tuple-element.59), channel_id=1, replica_groups=mesh['y'=4,'core'=2,'z'=8,'x'=4] {'z','x'}, dimensions={0} | all-to-all | bytes 262144 | tf_op jit(solution)/shard_map/all_to_all | solution.py:40
  147.4 3.2 %shard_map.70 = (bf16[1024,2048]{1,0:T(8,128)(2,1)S(1)}, f32[24,128]{1,0:T(8,128)S(1)}, f32[128,2048]{1,0:T(8,128)S(1)}) custom-call(s32[4]{0:T(128)S(1)} %pad_add_fusion.at_ref, f32[32,8,128]{2,1,0:T(8,128)S(1)} %all_to_all.41.e_ref, f32[8,128]{1,0:T(8,128)S(1)} %get-tuple-element.56.f_ref, f32[8,128]{1,0:T(8,128)S(1)} %bitcast.27, ...), custom_call_target="tpu_custom_call" | custom-call | tf_op jit(solution)/shard_map/pallas_call | solution.py:23
  150.6 2.3 %collective-permute-start.19 = (f32[128,2048]{1,0:T(8,128)S(1)}, f32[128,2048]{1,0:T(8,128)S(1)}, u32[]{:S(2)}, u32[]{:S(2)}) collective-permute-start(f32[128,2048]{1,0:T(8,128)S(1)} %get-tuple-element.63), channel_id=1, source_target_pairs={{0,32},{32,0},{1,33},{33,1},{2,34},{34,2},{3,35},{35,3},{4,36},{36... | collective-permute-start | bytes 3145736 | tf_op jit(solution)/shard_map/ppermute | solution.py:36
  153.0 1.8 shard_map.71
  156.0 3.1 %shard_map.73 = (f32[128,2048]{1,0:T(8,128)S(1)}, f32[128,2048]{1,0:T(8,128)S(1)}) custom-call(s32[4]{0:T(128)S(1)} %pad_add_fusion.at_ref, bf16[32,32,1024]{2,1,0:T(8,128)(2,1)S(1)} %get-tuple-element.52.ft_ref, bf16[1024,2048]{1,0:T(8,128)(2,1)S(1)} %get-tuple-element.62.w_ref), custom_call_target="tpu_custom_call" | custom-call | tf_op jit(solution)/shard_map/pallas_call | solution.py:23
  159.7 3.1 %shard_map.74 = (f32[128,2048]{1,0:T(8,128)S(1)}, f32[128,2048]{1,0:T(8,128)S(1)}) custom-call(s32[4]{0:T(128)S(1)} %pad_add_fusion.at_ref, bf16[32,32,1024]{2,1,0:T(8,128)(2,1)S(1)} %get-tuple-element.52.ft_ref, bf16[1024,2048]{1,0:T(8,128)(2,1)S(1)} %get-tuple-element.62.w_ref), custom_call_target="tpu_custom_call" | custom-call | tf_op jit(solution)/shard_map/pallas_call | solution.py:23
  163.5 3.1 %shard_map.75 = (f32[128,2048]{1,0:T(8,128)S(1)}, f32[128,2048]{1,0:T(8,128)S(1)}) custom-call(s32[4]{0:T(128)S(1)} %pad_add_fusion.at_ref, bf16[32,32,1024]{2,1,0:T(8,128)(2,1)S(1)} %get-tuple-element.52.ft_ref, bf16[1024,2048]{1,0:T(8,128)(2,1)S(1)} %get-tuple-element.62.w_ref), custom_call_target="tpu_custom_call" | custom-call | tf_op jit(solution)/shard_map/pallas_call | solution.py:23
  168.5 1.9 collective-permute-start.29
  171.2 20.8 %collective-permute-done.26.m3 = f32[24,128]{1,0:T(8,128)S(1)} collective-permute-done((f32[24,128]{1,0:T(8,128)S(1)}, f32[24,128]{1,0:T(8,128)S(1)}, u32[]{:S(2)}, u32[]{:S(2)}) %collective-permute-start.26) | collective-permute-done | bytes 12320 | tf_op jit(solution)/shard_map/ppermute | solution.py:36
  192.0 2.4 %collective-permute-start.25 = (f32[24,128]{1,0:T(8,128)S(1)}, f32[24,128]{1,0:T(8,128)S(1)}, u32[]{:S(2)}, u32[]{:S(2)}) collective-permute-start(f32[24,128]{1,0:T(8,128)S(1)} %get-tuple-element.76.m0), channel_id=1, source_target_pairs={{0,128},{64,192},{128,0},{192,64},{1,129},{65,193},{129,1},{193,65... | collective-permute-start | bytes 36872 | tf_op jit(solution)/shard_map/ppermute | solution.py:36
  196.0 2.2 %collective-permute-start.24 = (f32[24,128]{1,0:T(8,128)S(1)}, f32[24,128]{1,0:T(8,128)S(1)}, u32[]{:S(2)}, u32[]{:S(2)}) collective-permute-start(f32[24,128]{1,0:T(8,128)S(1)} %get-tuple-element.76.m0), channel_id=1, source_target_pairs={{0,64},{64,128},{128,192},{192,0},{1,65},{65,129},{129,193},{193,1... | collective-permute-start | bytes 36872 | tf_op jit(solution)/shard_map/ppermute | solution.py:36
  198.3 1.7 collective-permute-done.24.m1
  (72 shorter events, 18.9 us)
Async XLA Ops:
  0.7 5.5 %collective-permute-start.5 = (bf16[32,1024]{1,0:T(8,128)(2,1)}, bf16[32,1024]{1,0:T(8,128)(2,1)S(1)}, u32[]{:S(2)}, u32[]{:S(2)}) collective-permute-start(bf16[32,1024]{1,0:T(8,128)(2,1)} %bitcast.28), channel_id=1, source_target_pairs={{0,2},{1,3},{2,0},{3,1},{4,6},{5,7},{6,4},{7,5},{8,10},{9,11},{10,... | collective-permute-start | bytes 196616 | tf_op jit(solution)/shard_map/ppermute | solution.py:36
  4.3 4.3 %collective-permute-start.4 = (bf16[32,1024]{1,0:T(8,128)(2,1)}, bf16[32,1024]{1,0:T(8,128)(2,1)S(1)}, u32[]{:S(2)}, u32[]{:S(2)}) collective-permute-start(bf16[32,1024]{1,0:T(8,128)(2,1)} %bitcast.29), channel_id=1, source_target_pairs={{0,3},{1,0},{2,1},{3,2},{4,7},{5,4},{6,5},{7,6},{8,11},{9,8},{10,9... | collective-permute-start | bytes 196616 | tf_op jit(solution)/shard_map/ppermute | solution.py:36
  5.2 8.8 %collective-permute-start = (bf16[32,1024]{1,0:T(8,128)(2,1)}, bf16[32,1024]{1,0:T(8,128)(2,1)S(1)}, u32[]{:S(2)}, u32[]{:S(2)}) collective-permute-start(bf16[32,1024]{1,0:T(8,128)(2,1)} %bitcast.30), channel_id=1, source_target_pairs={{0,1},{1,2},{2,3},{3,0},{4,5},{5,6},{6,7},{7,4},{8,9},{9,10},{10,1... | collective-permute-start | bytes 196616 | tf_op jit(solution)/shard_map/ppermute | solution.py:36
  8.6 9.0 %collective-permute-start.6 = (bf16[64,1024]{1,0:T(8,128)(2,1)S(1)}, bf16[64,1024]{1,0:T(8,128)(2,1)S(1)}, u32[]{:S(2)}, u32[]{:S(2)}) collective-permute-start(bf16[64,1024]{1,0:T(8,128)(2,1)S(1)} %shard_map.60.b0), channel_id=1, source_target_pairs={{0,28},{4,0},{8,4},{12,8},{16,12},{20,16},{24,20},{28,24},{1,29},{... | collective-permute-start | bytes 393224 | tf_op jit(solution)/shard_map/ppermute | solution.py:36
  14.0 6.3 %collective-permute-start.12 = (bf16[64,1024]{1,0:T(8,128)(2,1)S(1)}, bf16[64,1024]{1,0:T(8,128)(2,1)S(1)}, u32[]{:S(2)}, u32[]{:S(2)}) collective-permute-start(bf16[64,1024]{1,0:T(8,128)(2,1)S(1)} %shard_map.60.b0), channel_id=1, source_target_pairs={{0,4},{4,8},{8,12},{12,16},{16,20},{20,24},{24,28},{28,0},{1,5},{5... | collective-permute-start | bytes 393224 | tf_op jit(solution)/shard_map/ppermute | solution.py:36
  14.8 5.4 %collective-permute-start.1 = (bf16[64,1024]{1,0:T(8,128)(2,1)S(1)}, bf16[64,1024]{1,0:T(8,128)(2,1)S(1)}, u32[]{:S(2)}, u32[]{:S(2)}) collective-permute-start(bf16[64,1024]{1,0:T(8,128)(2,1)S(1)} %shard_map.59.a0), channel_id=1, source_target_pairs={{0,28},{4,0},{8,4},{12,8},{16,12},{20,16},{24,20},{28,24},{1,29},{... | collective-permute-start | bytes 393224 | tf_op jit(solution)/shard_map/ppermute | solution.py:36
  17.6 5.4 %collective-permute-start.9 = (bf16[64,1024]{1,0:T(8,128)(2,1)S(1)}, bf16[64,1024]{1,0:T(8,128)(2,1)S(1)}, u32[]{:S(2)}, u32[]{:S(2)}) collective-permute-start(bf16[64,1024]{1,0:T(8,128)(2,1)S(1)} %shard_map.59.a0), channel_id=1, source_target_pairs={{0,4},{4,8},{8,12},{12,16},{16,20},{20,24},{24,28},{28,0},{1,5},{5... | collective-permute-start | bytes 393224 | tf_op jit(solution)/shard_map/ppermute | solution.py:36
  17.6 5.8 %collective-permute-start.7 = (bf16[64,1024]{1,0:T(8,128)(2,1)S(1)}, bf16[64,1024]{1,0:T(8,128)(2,1)S(1)}, u32[]{:S(2)}, u32[]{:S(2)}) collective-permute-start(bf16[64,1024]{1,0:T(8,128)(2,1)S(1)} %collective-permute-done.6.bl), channel_id=1, source_target_pairs={{0,28},{4,0},{8,4},{12,8},{16,12},{20,16},{24,20},{28,24},{1,29},{... | collective-permute-start | bytes 393224 | tf_op jit(solution)/shard_map/ppermute | solution.py:36
  20.3 6.7 %collective-permute-start.13 = (bf16[64,1024]{1,0:T(8,128)(2,1)S(1)}, bf16[64,1024]{1,0:T(8,128)(2,1)S(1)}, u32[]{:S(2)}, u32[]{:S(2)}) collective-permute-start(bf16[64,1024]{1,0:T(8,128)(2,1)S(1)} %collective-permute-done.12.br), channel_id=1, source_target_pairs={{0,4},{4,8},{8,12},{12,16},{16,20},{20,24},{24,28},{28,0},{1,5},{5... | collective-permute-start | bytes 393224 | tf_op jit(solution)/shard_map/ppermute | solution.py:36
  20.3 6.7 %collective-permute-start.2 = (bf16[64,1024]{1,0:T(8,128)(2,1)S(1)}, bf16[64,1024]{1,0:T(8,128)(2,1)S(1)}, u32[]{:S(2)}, u32[]{:S(2)}) collective-permute-start(bf16[64,1024]{1,0:T(8,128)(2,1)S(1)} %collective-permute-done.1.al), channel_id=1, source_target_pairs={{0,28},{4,0},{8,4},{12,8},{16,12},{20,16},{24,20},{28,24},{1,29},{... | collective-permute-start | bytes 393224 | tf_op jit(solution)/shard_map/ppermute | solution.py:36
  23.0 6.7 %collective-permute-start.10 = (bf16[64,1024]{1,0:T(8,128)(2,1)S(1)}, bf16[64,1024]{1,0:T(8,128)(2,1)S(1)}, u32[]{:S(2)}, u32[]{:S(2)}) collective-permute-start(bf16[64,1024]{1,0:T(8,128)(2,1)S(1)} %collective-permute-done.9.ar), channel_id=1, source_target_pairs={{0,4},{4,8},{8,12},{12,16},{16,20},{20,24},{24,28},{28,0},{1,5},{5... | collective-permute-start | bytes 393224 | tf_op jit(solution)/shard_map/ppermute | solution.py:36
  23.3 13.0 %collective-permute-start.8 = (bf16[64,1024]{1,0:T(8,128)(2,1)S(1)}, bf16[64,1024]{1,0:T(8,128)(2,1)S(1)}, u32[]{:S(2)}, u32[]{:S(2)}) collective-permute-start(bf16[64,1024]{1,0:T(8,128)(2,1)S(1)} %collective-permute-done.7.bl2), channel_id=1, source_target_pairs={{0,28},{4,0},{8,4},{12,8},{16,12},{20,16},{24,20},{28,24},{1,29},{... | collective-permute-start | bytes 393224 | tf_op jit(solution)/shard_map/ppermute | solution.py:36
  27.0 9.4 %collective-permute-start.16 = (bf16[64,1024]{1,0:T(8,128)(2,1)S(1)}, bf16[64,1024]{1,0:T(8,128)(2,1)S(1)}, u32[]{:S(2)}, u32[]{:S(2)}) collective-permute-start(bf16[64,1024]{1,0:T(8,128)(2,1)S(1)} %collective-permute-done.13.br2), channel_id=1, source_target_pairs={{0,4},{4,8},{8,12},{12,16},{16,20},{20,24},{24,28},{28,0},{1,5},{5... | collective-permute-start | bytes 393224 | tf_op jit(solution)/shard_map/ppermute | solution.py:36
  27.0 9.4 %collective-permute-start.3 = (bf16[64,1024]{1,0:T(8,128)(2,1)S(1)}, bf16[64,1024]{1,0:T(8,128)(2,1)S(1)}, u32[]{:S(2)}, u32[]{:S(2)}) collective-permute-start(bf16[64,1024]{1,0:T(8,128)(2,1)S(1)} %collective-permute-done.2.al2), channel_id=1, source_target_pairs={{0,28},{4,0},{8,4},{12,8},{16,12},{20,16},{24,20},{28,24},{1,29},{... | collective-permute-start | bytes 393224 | tf_op jit(solution)/shard_map/ppermute | solution.py:36
  29.6 6.8 %collective-permute-start.11 = (bf16[64,1024]{1,0:T(8,128)(2,1)S(1)}, bf16[64,1024]{1,0:T(8,128)(2,1)S(1)}, u32[]{:S(2)}, u32[]{:S(2)}) collective-permute-start(bf16[64,1024]{1,0:T(8,128)(2,1)S(1)} %collective-permute-done.10.ar2), channel_id=1, source_target_pairs={{0,4},{4,8},{8,12},{12,16},{16,20},{20,24},{24,28},{28,0},{1,5},{5... | collective-permute-start | bytes 393224 | tf_op jit(solution)/shard_map/ppermute | solution.py:36
  36.5 9.1 %collective-permute-start.18 = (bf16[32,1024]{1,0:T(8,128)(2,1)S(1)}, bf16[32,1024]{1,0:T(8,128)(2,1)S(1)}, u32[]{:S(2)}, u32[]{:S(2)}) collective-permute-start(bf16[32,1024]{1,0:T(8,128)(2,1)S(1)} %slice.39), channel_id=1, source_target_pairs={{0,28},{4,0},{8,4},{12,8},{16,12},{20,16},{24,20},{28,24},{1,29},{... | collective-permute-start | bytes 196616 | tf_op jit(solution)/shard_map/ppermute | solution.py:36
  39.2 6.4 %collective-permute-start.17 = (bf16[32,1024]{1,0:T(8,128)(2,1)S(1)}, bf16[32,1024]{1,0:T(8,128)(2,1)S(1)}, u32[]{:S(2)}, u32[]{:S(2)}) collective-permute-start(bf16[32,1024]{1,0:T(8,128)(2,1)S(1)} %slice.38), channel_id=1, source_target_pairs={{0,4},{4,8},{8,12},{12,16},{16,20},{20,24},{24,28},{28,0},{1,5},{5... | collective-permute-start | bytes 196616 | tf_op jit(solution)/shard_map/ppermute | solution.py:36
  39.2 6.4 %collective-permute-start.15 = (bf16[32,1024]{1,0:T(8,128)(2,1)S(1)}, bf16[32,1024]{1,0:T(8,128)(2,1)S(1)}, u32[]{:S(2)}, u32[]{:S(2)}) collective-permute-start(bf16[32,1024]{1,0:T(8,128)(2,1)S(1)} %slice.37), channel_id=1, source_target_pairs={{0,28},{4,0},{8,4},{12,8},{16,12},{20,16},{24,20},{28,24},{1,29},{... | collective-permute-start | bytes 196616 | tf_op jit(solution)/shard_map/ppermute | solution.py:36
  41.9 4.3 %collective-permute-start.14 = (bf16[32,1024]{1,0:T(8,128)(2,1)S(1)}, bf16[32,1024]{1,0:T(8,128)(2,1)S(1)}, u32[]{:S(2)}, u32[]{:S(2)}) collective-permute-start(bf16[32,1024]{1,0:T(8,128)(2,1)S(1)} %slice.36), channel_id=1, source_target_pairs={{0,4},{4,8},{8,12},{12,16},{16,20},{20,24},{24,28},{28,0},{1,5},{5... | collective-permute-start | bytes 196616 | tf_op jit(solution)/shard_map/ppermute | solution.py:36
  46.2 23.2 %copy-start.2 = (f32[1024]{0:T(1024)S(1)}, f32[1024]{0:T(1024)}, u32[]{:S(2)}) copy-start(f32[1024]{0:T(1024)} %param.6) | copy-start | bytes 12292
  69.5 17.3 %copy-start.1 = (f32[2048]{0:T(1024)S(1)}, f32[2048]{0:T(1024)}, u32[]{:S(2)}) copy-start(f32[2048]{0:T(1024)} %param.7) | copy-start | bytes 24580
  150.6 5.2 %collective-permute-start.19 = (f32[128,2048]{1,0:T(8,128)S(1)}, f32[128,2048]{1,0:T(8,128)S(1)}, u32[]{:S(2)}, u32[]{:S(2)}) collective-permute-start(f32[128,2048]{1,0:T(8,128)S(1)} %get-tuple-element.63), channel_id=1, source_target_pairs={{0,32},{32,0},{1,33},{33,1},{2,34},{34,2},{3,35},{35,3},{4,36},{36... | collective-permute-start | bytes 3145736 | tf_op jit(solution)/shard_map/ppermute | solution.py:36
  152.9 2.3 %collective-permute-start.20 = (f32[24,128]{1,0:T(8,128)S(1)}, f32[24,128]{1,0:T(8,128)S(1)}, u32[]{:S(2)}, u32[]{:S(2)}) collective-permute-start(f32[24,128]{1,0:T(8,128)S(1)} %get-tuple-element.64.mine_ref), channel_id=1, source_target_pairs={{0,32},{32,0},{1,33},{33,1},{2,34},{34,2},{3,35},{35,3},{4,36},{36... | collective-permute-start | bytes 36872 | tf_op jit(solution)/shard_map/ppermute | solution.py:36
  159.1 3.7 %collective-permute-start.22 = (f32[128,2048]{1,0:T(8,128)S(1)}, f32[128,2048]{1,0:T(8,128)S(1)}, u32[]{:S(2)}, u32[]{:S(2)}) collective-permute-start(f32[128,2048]{1,0:T(8,128)S(1)} %get-tuple-element.68), channel_id=1, source_target_pairs={{0,32},{32,0},{1,33},{33,1},{2,34},{34,2},{3,35},{35,3},{4,36},{36... | collective-permute-start | bytes 3145736 | tf_op jit(solution)/shard_map/ppermute | solution.py:36
  159.5 3.8 %collective-permute-start.21 = (f32[128,2048]{1,0:T(8,128)S(1)}, f32[128,2048]{1,0:T(8,128)S(1)}, u32[]{:S(2)}, u32[]{:S(2)}) collective-permute-start(f32[128,2048]{1,0:T(8,128)S(1)} %get-tuple-element.67), channel_id=1, source_target_pairs={{0,32},{32,0},{1,33},{33,1},{2,34},{34,2},{3,35},{35,3},{4,36},{36... | collective-permute-start | bytes 3145736 | tf_op jit(solution)/shard_map/ppermute | solution.py:36
  166.6 34.5 %collective-permute-start.23 = (f32[128,2048]{1,0:T(8,128)S(1)}, f32[128,2048]{1,0:T(8,128)S(1)}, u32[]{:S(2)}, u32[]{:S(2)}) collective-permute-start(f32[128,2048]{1,0:T(8,128)S(1)} %get-tuple-element.74), channel_id=1, source_target_pairs={{0,32},{32,0},{1,33},{33,1},{2,34},{34,2},{3,35},{35,3},{4,36},{36... | collective-permute-start | bytes 3145736 | tf_op jit(solution)/shard_map/ppermute | solution.py:36
  167.1 34.0 %collective-permute-start.27 = (f16[128,2048]{1,0:T(8,128)(2,1)S(1)}, f16[128,2048]{1,0:T(8,128)(2,1)S(1)}, u32[]{:S(2)}, u32[]{:S(2)}) collective-permute-start(f16[128,2048]{1,0:T(8,128)(2,1)S(1)} %multiply_convert_fusion.2), channel_id=1, source_target_pairs={{0,128},{64,192},{128,0},{192,64},{1,129},{65,193},{129,1},{193,65... | collective-permute-start | bytes 1572872 | tf_op jit(solution)/shard_map/ppermute | solution.py:36
  167.8 33.3 %collective-permute-start.28 = (f16[128,2048]{1,0:T(8,128)(2,1)S(1)}, f16[128,2048]{1,0:T(8,128)(2,1)S(1)}, u32[]{:S(2)}, u32[]{:S(2)}) collective-permute-start(f16[128,2048]{1,0:T(8,128)(2,1)S(1)} %multiply_convert_fusion.1), channel_id=1, source_target_pairs={{0,64},{64,128},{128,192},{192,0},{1,65},{65,129},{129,193},{193,1... | collective-permute-start | bytes 1572872 | tf_op jit(solution)/shard_map/ppermute | solution.py:36
  168.5 32.6 %collective-permute-start.29 = (f16[128,2048]{1,0:T(8,128)(2,1)S(1)}, f16[128,2048]{1,0:T(8,128)(2,1)S(1)}, u32[]{:S(2)}, u32[]{:S(2)}) collective-permute-start(f16[128,2048]{1,0:T(8,128)(2,1)S(1)} %multiply_convert_fusion), channel_id=1, source_target_pairs={{0,192},{64,0},{128,64},{192,128},{1,193},{65,1},{129,65},{193,129... | collective-permute-start | bytes 1572872 | tf_op jit(solution)/shard_map/ppermute | solution.py:36
  170.5 21.5 %collective-permute-start.26 = (f32[24,128]{1,0:T(8,128)S(1)}, f32[24,128]{1,0:T(8,128)S(1)}, u32[]{:S(2)}, u32[]{:S(2)}) collective-permute-start(f32[24,128]{1,0:T(8,128)S(1)} %get-tuple-element.76.m0), channel_id=1, source_target_pairs={{0,192},{64,0},{128,64},{192,128},{1,193},{65,1},{129,65},{193,129... | collective-permute-start | bytes 36872 | tf_op jit(solution)/shard_map/ppermute | solution.py:36
  192.0 4.0 %collective-permute-start.25 = (f32[24,128]{1,0:T(8,128)S(1)}, f32[24,128]{1,0:T(8,128)S(1)}, u32[]{:S(2)}, u32[]{:S(2)}) collective-permute-start(f32[24,128]{1,0:T(8,128)S(1)} %get-tuple-element.76.m0), channel_id=1, source_target_pairs={{0,128},{64,192},{128,0},{192,64},{1,129},{65,193},{129,1},{193,65... | collective-permute-start | bytes 36872 | tf_op jit(solution)/shard_map/ppermute | solution.py:36
  196.0 3.9 %collective-permute-start.24 = (f32[24,128]{1,0:T(8,128)S(1)}, f32[24,128]{1,0:T(8,128)S(1)}, u32[]{:S(2)}, u32[]{:S(2)}) collective-permute-start(f32[24,128]{1,0:T(8,128)S(1)} %get-tuple-element.76.m0), channel_id=1, source_target_pairs={{0,64},{64,128},{128,192},{192,0},{1,65},{65,129},{129,193},{193,1... | collective-permute-start | bytes 36872 | tf_op jit(solution)/shard_map/ppermute | solution.py:36
  (2 other events, 3.0 us)

commit v3 on v2

v3 whole, which is shorter than its diff:
```python
import functools

import jax
import jax.numpy as jnp
from jax import lax
from jax.experimental import pallas as pl
from jax.experimental.pallas import tpu as pltpu
from jax.sharding import Mesh
from jax.sharding import PartitionSpec as P

ITERS = 3
ROWS = 1024
COLS = 2048
RB, CB = ROWS // 128, COLS // 128
CENT = ("z", "x")
DP = ("y", "core")
F32, BF16 = jnp.float32, jnp.bfloat16
VM = pl.BlockSpec(memory_space=pltpu.VMEM)
SM = pl.BlockSpec(memory_space=pltpu.SMEM)


def call(body, outs, ins, scratch=(), mib=24, aliases=None):
    return pl.pallas_call(
        body,
        out_shape=[jax.ShapeDtypeStruct(s, d) for s, d in outs],
        in_specs=[SM if a.dtype == jnp.int32 else VM for a in ins],
        out_specs=[VM] * len(outs),
        scratch_shapes=list(scratch),
        input_output_aliases=aliases or {},
        compiler_params=pltpu.CompilerParams(vmem_limit_bytes=mib << 20),
    )(*ins)


def step(x, axis, by):
    n = lax.axis_size(axis)
    return lax.ppermute(x, axis, [(i, (i + by) % n) for i in range(n)])


def everyone(x, axis):
    return lax.all_to_all(x, axis, 0, 0, tiled=True)


def after(x, *others):
    return lax.optimization_barrier((x, *others))[0]


def down(row):
    return jnp.broadcast_to(row, (128, 128)).T


def around(at_ref, k, by, n):
    return lax.rem(at_ref[k] + (n + by), n)


def own_body(a_ref, o_ref):
    o_ref[0:32, :] = a_ref[...]


def join_body(b_ref, c_ref, d_ref, in_ref, o_ref):
    for k, ref in enumerate((b_ref, c_ref, d_ref)):
        o_ref[32 * k + 32 : 32 * k + 64, :] = ref[...]


def collect(at_ref, pieces, c_ref, ft_ref, fa_ref, fs_ref, cs_ref):
    for k, (by, parts) in enumerate(pieces):
        at = around(at_ref, 2, by, 8)
        for (ref, row), off in zip(parts, (0, -1, 1, 2)):
            ft_ref[4 * at + around(at_ref, 3, off, 4)] = ref[row : row + 32, :]
        piece = ft_ref[pl.ds(4 * at, 4)].reshape(128, ROWS)
        top = jnp.max(jnp.abs(piece), axis=0, keepdims=True).astype(F32)
        fa_ref[pl.ds(at, 1), :] = jnp.broadcast_to(jnp.max(top, axis=1, keepdims=True), (1, 128))
        fs_ref[:, 128 * k : 128 * k + 128] = piece.T
        cs_ref[:, 128 * k : 128 * k + 128] = c_ref[:, pl.ds(pl.multiple_of(at * 128, 128), 128)]


def product(f, c):
    return lax.dot_general(f, c, (((1,), (1,)), ((), ())), preferred_element_type=F32)


def whole(ref):
    return [(ref, 32 * k) for k in range(4)]


def accumulate(kin, k_ref, fs, cs):
    def block(b, carry):
        rows = pl.ds(pl.multiple_of(256 * b, 256), 256)
        s = product(fs[rows, :], cs[...])
        k_ref[rows, :] = s if kin is None else kin[rows, :] + s
        return carry

    lax.fori_loop(0, 4, block, 0)


def score0_body(at_ref, s_ref, c_ref, k_ref, ft_ref, fa_ref, fs, cs):
    collect(at_ref, [(0, whole(s_ref))], c_ref, ft_ref, fa_ref, fs, cs)
    accumulate(None, k_ref, fs, cs)


def score_body(by, at_ref, l, r, c_ref, kin, ftin, fain, k_ref, ft_ref, fa_ref, fs, cs):
    collect(at_ref, [(by, whole(l)), (-by, whole(r))], c_ref, ft_ref, fa_ref, fs, cs)
    accumulate(kin, k_ref, fs, cs)


def score4_body(at_ref, h0, h1, c_ref, kin, ftin, fain, k_ref, ft_ref, fa_ref, p_ref, fs, cs, tops, sums):
    far = (4, [(h0, 0), (h0, 32), (h1, 0), (h1, 32)])
    collect(at_ref, [far], c_ref, ft_ref, fa_ref, fs, cs)

    def scored(b):
        rows = pl.ds(pl.multiple_of(128 * b, 128), 128)
        s = kin[rows, :] + product(fs[rows, :], cs[...])
        k_ref[rows, :] = s
        tops[rows, :] = jnp.broadcast_to(jnp.max(s, axis=1, keepdims=True), (128, 128))

    def raised(b):
        rows = pl.ds(pl.multiple_of(128 * b, 128), 128)
        top, acc = tops[rows, :], jnp.zeros((128, 128), F32)
        for t in range(CB):
            cols = slice(128 * t, 128 * t + 128)
            e = jnp.exp(k_ref[rows, cols] - top)
            k_ref[rows, cols] = e
            acc = acc + e
        sums[rows, :] = acc

    def block(b, carry):
        raised(b)
        scored(b + 1)
        return carry

    scored(0)
    lax.fori_loop(0, RB - 1, block, 0)
    raised(RB - 1)
    lines = [tops[128 * b : 128 * b + 128, :].T[0:1] for b in range(RB)]
    lines += [jnp.sum(sums[128 * b : 128 * b + 128, :].T, axis=0, keepdims=True) for b in range(RB)]
    p_ref[...] = jnp.broadcast_to(jnp.concatenate(lines, axis=0)[None], p_ref.shape)


def columns(k_ref, scale, by_ref, o_ref):
    for b in range(RB):
        by_ref[128 * b : 128 * b + 128, :] = down(scale[b : b + 1])

    def block(b, acc):
        rows = pl.ds(pl.multiple_of(128 * b, 128), 128)
        by = by_ref[rows, :]
        parts = (k_ref[rows, 128 * t : 128 * t + 128] * by for t in range(CB))
        return tuple(a + jnp.sum(p.reshape(16, 8, 128), axis=0) for a, p in zip(acc, parts))

    acc = lax.fori_loop(0, RB, block, (jnp.zeros((8, 128), F32),) * CB)
    z = jnp.concatenate([jnp.sum(a, axis=0, keepdims=True) for a in acc], axis=0)
    o_ref[...] = jnp.broadcast_to(z[None], o_ref.shape)


def first_column_body(e_ref, mine_ref, a_ref, k_ref, o_ref, f_ref, by_ref):
    peaks = e_ref[:, 0:RB, :]
    top = jnp.max(peaks, axis=0)
    total = jnp.sum(e_ref[:, RB : 2 * RB, :] * jnp.exp(peaks - top[None]), axis=0)
    fold = jnp.exp(mine_ref[0, 0:RB, :] - top)
    f_ref[...] = fold
    columns(k_ref, (a_ref[...] / total) * fold, by_ref, o_ref)


def column_body(e_ref, f_ref, a_ref, k_ref, o_ref, by_ref):
    scale = a_ref[...] / jnp.sum(e_ref[...], axis=0)
    columns(k_ref, scale * f_ref[...], by_ref, o_ref)


def row_body(e_ref, f_ref, b_ref, k_ref, o_ref, c_ref, acc_ref):
    scale = b_ref[...] / jnp.sum(e_ref[...], axis=0)
    c_ref[...] = scale

    def block(b, carry):
        rows = pl.ds(pl.multiple_of(128 * b, 128), 128)
        acc = jnp.zeros((128, 128), F32)
        for t in range(CB):
            acc = acc + k_ref[rows, 128 * t : 128 * t + 128] * scale[t : t + 1]
        acc_ref[rows, :] = acc
        return carry

    lax.fori_loop(0, RB, block, 0)
    lines = [
        jnp.sum(acc_ref[128 * b : 128 * b + 128, :].T, axis=0, keepdims=True) for b in range(RB)
    ]
    y = jnp.concatenate(lines, axis=0) * f_ref[...]
    o_ref[...] = jnp.broadcast_to(y[None], o_ref.shape)


def target(at_ref, by, side):
    return 2 * around(at_ref, 0, by, 4) + around(at_ref, 1, side, 2)


def product_of(at_ref, ft_ref, w_ref, o_ref, by, side):
    feats = ft_ref[pl.ds(4 * target(at_ref, by, side), 4)].reshape(128, ROWS)
    o_ref[...] = jnp.dot(feats, w_ref[...], preferred_element_type=F32)


def halves_of(at_ref, ft_ref, w_ref, o_ref, by, side):
    d = 4 * target(at_ref, by, side)

    def block(b, carry):
        cols = pl.ds(pl.multiple_of(1024 * b, 1024), 1024)
        feats = ft_ref[pl.ds(d, 4)].reshape(128, ROWS)
        o_ref[:, cols] = jnp.dot(feats, w_ref[:, cols], preferred_element_type=F32)
        return carry

    lax.fori_loop(0, 2, block, 0)


def weight_body(e_ref, f_ref, a_ref, c_ref, fa_ref, k_ref, w_ref, m_ref, by_ref):
    scale = (a_ref[...] / jnp.sum(e_ref[...], axis=0)) * f_ref[...]
    for b in range(RB):
        by_ref[128 * b : 128 * b + 128, :] = down(scale[b : b + 1])

    def block(b, acc):
        rows = pl.ds(pl.multiple_of(128 * b, 128), 128)
        by, total = by_ref[rows, :], []
        for t in range(CB):
            cols = slice(128 * t, 128 * t + 128)
            part = (k_ref[rows, cols] * by) * c_ref[t : t + 1, :]
            total.append(acc[t] + jnp.sum(part.reshape(16, 8, 128), axis=0))
            w_ref[rows, cols] = part.astype(BF16)
        return tuple(total)

    acc = lax.fori_loop(0, RB, block, (jnp.zeros((8, 128), F32),) * CB)
    m_ref[0:CB, :] = jnp.concatenate([jnp.sum(a, axis=0, keepdims=True) for a in acc], axis=0)
    m_ref[CB : CB + 8, :] = fa_ref[...]


def limits(at_ref, m, by):
    return m[0:CB, :] * m[pl.ds(CB + target(at_ref, by, 0), 1), :]


def inverse(q):
    return jnp.where(q > 0, 32768.0 / jnp.where(q > 0, q, 1.0), 0.0)


def chip_body(at_ref, mine_ref, other_ref, m_ref, i_ref):
    m_ref[0:CB, :] = mine_ref[0:CB, :] + other_ref[0:CB, :]
    m_ref[CB : CB + 8, :] = jnp.maximum(mine_ref[CB : CB + 8, :], other_ref[CB : CB + 8, :])
    for k, by in enumerate((2, 1, 3)):
        i_ref[k] = inverse(limits(at_ref, m_ref, by))


def relay_body(at_ref, m0, m1, m3, i_ref, s_ref):
    for k, (m, by) in enumerate(((m1, 1), (m3, 3))):
        q = limits(at_ref, m, by)
        s_ref[k] = q * (1.0 / 32768.0)
        i_ref[k] = inverse(q + limits(at_ref, m0, by))


def share_body(at_ref, m0, m1, m2, m3, t_ref, i_ref, s_ref):
    total = (m0[0:CB, :] + m2[0:CB, :]) + (m1[0:CB, :] + m3[0:CB, :])
    t_ref[...] = total
    over = 1.0 / total
    i_ref[...] = over
    q1, q2, q3 = (limits(at_ref, m, 0) * (1.0 / 32768.0) for m in (m1, m2, m3))
    for k, q in enumerate((q1, q3, q1 + q2, q3 + q2)):
        s_ref[k] = q * over


def product_body(which, at_ref, ft_ref, w_ref, *o_refs):
    one = product_of if len(which) == 1 else halves_of
    for k, o_ref in enumerate(o_refs):
        one(at_ref, ft_ref, w_ref, o_ref, *which[k])


def assigned(features, centroids, row_weight, centroid_share):
    y, core, z, x = (lax.axis_index(n) for n in ("y", "core", "z", "x"))
    at = jnp.stack([y, core, z, x]).astype(jnp.int32)
    a = row_weight.reshape(RB, 128)
    share = centroid_share.reshape(CB, 128)

    own = after(features.T, at)

    def ring(x, by):
        return step(x, "z", by)

    def scores(body, outs, ins, depth, aliases=None, more=()):
        return call(
            body,
            outs,
            ins,
            scratch=[pltpu.VMEM((ROWS, depth), BF16), pltpu.VMEM((COLS, depth), BF16), *more],
            mib=16,
            aliases=aliases,
        )

    parts = []
    for by in (1, -1, 2):
        parts.append(step(own, "x", by))
    strip_shape = [((128, ROWS), BF16)]
    (strip,) = call(own_body, strip_shape, [own], mib=4)
    (strip,) = call(join_body, strip_shape, [*parts, strip], mib=4, aliases={3: 0})
    state = [((ROWS, COLS), F32), ((32, 32, ROWS), BF16), ((8, 128), F32)]
    right = [strip, ring(strip, 1)]
    left = [strip, ring(strip, -1)]
    kernel, ft, fa = scores(score0_body, state, [at, strip, centroids], 128)
    for k in (1, 2):
        right.append(ring(right[k], 1))
        left.append(ring(left[k], -1))
    far = [ring(right[3][:64], 1), ring(left[3][64:], -1)]
    for k in (1, 2, 3):
        kernel, ft, fa = scores(
            functools.partial(score_body, k),
            state,
            [at, left[k], right[k], centroids, kernel, ft, fa],
            256,
            {4: 0, 5: 1, 6: 2},
        )
    kernel, ft, fa, peaks = scores(
        score4_body,
        [*state, ((32, 2 * RB, 128), F32)],
        [at, *far, centroids, kernel, ft, fa],
        128,
        {4: 0, 5: 1, 6: 2},
        [pltpu.VMEM((ROWS, 128), F32)] * 2,
    )
    lines = [pltpu.VMEM((ROWS, 128), F32)]
    got = everyone(peaks, CENT)
    sums, fold = call(
        first_column_body,
        [((8, CB, 128), F32), ((RB, 128), F32)],
        [got, peaks, a, kernel],
        scratch=lines,
        mib=8,
    )
    for it in range(ITERS):
        rows, cscale = call(
            row_body,
            [((32, RB, 128), F32), ((CB, 128), F32)],
            [everyone(sums, DP), fold, share, kernel],
            scratch=lines,
            mib=8,
        )
        got = everyone(rows, CENT)
        if it < ITERS - 1:
            (sums,) = call(
                column_body, [((8, CB, 128), F32)], [got, fold, a, kernel], scratch=lines, mib=8
            )
    weights, mass = call(
        weight_body,
        [((ROWS, COLS), BF16), ((CB + 8, 128), F32)],
        [got, fold, a, cscale, fa, kernel],
        scratch=lines,
        mib=8,
    )

    other = step(mass, "core", 1)
    chip, packs = call(
        chip_body, [((CB + 8, 128), F32), ((3, CB, 128), F32)], [at, mass, other], mib=4
    )
    packs = packs.reshape(3, 1, COLS)

    def products(which, where):
        return call(
            functools.partial(product_body, which),
            [((128, COLS), F32)] * len(which),
            [where, ft, weights],
            mib=16,
        )

    def send(x, by):
        return step(x.astype(jnp.float16), "y", by)

    low, high = slice(0, 64), slice(64, 128)
    (give,) = products([(2, 1)], at)
    theirs = step(give, "core", 1)
    (mine,) = products([(2, 0)], after(at, give))
    chips = {}
    for by in (1, 3, 2):
        chips[by] = step(chip, "y", by)
    up = ((mine[low] + theirs[low]) * packs[0]).astype(jnp.float16)
    down_ = ((mine[high] + theirs[high]) * packs[0]).astype(jnp.float16)
    first = (send(up, 1), send(down_, 3))
    gives = products([(1, 1), (3, 1)], after(at, up, down_))
    theirs = [step(g, "core", 1) for g in gives]
    mines = products([(1, 0), (3, 0)], after(at, *gives))
    up = ((mines[0][high] + theirs[0][high]) * packs[1]).astype(jnp.float16)
    down_ = ((mines[1][low] + theirs[1][low]) * packs[2]).astype(jnp.float16)
    second = (send(up, 1), send(down_, 3))
    repacks, unpacks = call(
        relay_body, [((2, CB, 128), F32)] * 2, [at, chip, chips[1], chips[3]], mib=4
    )
    repacks, unpacks = repacks.reshape(2, 1, COLS), unpacks.reshape(2, 1, COLS)
    give, mine0 = products([(0, 1), (0, 0)], at)
    theirs0 = step(give, "core", 1)
    total, over, shares = call(
        share_body,
        [((CB, 128), F32), ((CB, 128), F32), ((4, CB, 128), F32)],
        [at, chip, chips[1], chips[2], chips[3]],
        mib=4,
    )
    mines, theirs, *_ = lax.optimization_barrier((mines, theirs, up, down_))
    up = mines[0][low] + theirs[0][low] + first[0].astype(F32) * unpacks[0]
    down_ = mines[1][high] + theirs[1][high] + first[1].astype(F32) * unpacks[1]
    third = (send(up * repacks[0], 1), send(down_ * repacks[1], 3))

    over, shares = over.reshape(1, COLS), shares.reshape(4, 1, COLS)
    own_part = (mine0 + theirs0) * over
    top = own_part[low] + second[1].astype(F32) * shares[1] + third[0].astype(F32) * shares[2]
    bottom = own_part[high] + second[0].astype(F32) * shares[0] + third[1].astype(F32) * shares[3]
    return jnp.concatenate([top, bottom], axis=0), total.reshape(COLS)


def solution(mesh):
    split = Mesh(mesh.devices.reshape(4, 2, 8, 4), ("y", "core", "z", "x"))
    return jax.shard_map(
        assigned,
        mesh=split,
        in_specs=(P(DP, CENT), P(CENT, None), P(DP), P(CENT)),
        out_specs=(P(DP, CENT), P(CENT)),
        check_vma=False,
    )
```

time: 204 us -> 194 us (0.951)
  starting transfers between devices: 42 us -> 35.3 us
  waiting for transfers between devices: 29.2 us -> 23.7 us
    ppermute x30 -> x25, starting transfers between devices: 42 us -> 35.3 us  [step(): return lax.ppermute(x, axis, [(i, (i + by) % n) for i in range(n)])]
    ppermute x30 -> x25, waiting for transfers between devices: 29.2 us -> 23.7 us  [step(): return lax.ppermute(x, axis, [(i, (i + by) % n) for i in range(n)])]
    pallas_call x18 -> x22, Pallas kernels: 36.9 us -> 38.2 us  [call(): pl.pallas_call(body, out_shape=[jax.ShapeDtypeStruct(s, d) for s, d in ou...]
  transfers between devices with their start and end apart: 30 -> 25, of which waited for: 10 -> 9; matrix products, arithmetic and copies ran while one was open for 0% -> 0% of each run, Pallas kernels for 7% -> 11%
where the time goes in v3:
time: 194 us
  blocking collectives  90.4 us (47%)
  Pallas kernels  38.2 us (20%)
  starting transfers between devices  35.3 us (18%)
  waiting for transfers between devices  23.7 us (12%)
  local copies, waits for them, and re-layouts  3.1 us (2%)
  other arithmetic  2.2 us (1%)
    all_to_all x7, blocking collectives, everyone(): return lax.all_to_all(x, axis, 0, 0, tiled=True)  90.4 us
    pallas_call x22, Pallas kernels, call(): pl.pallas_call(body, out_shape=[jax.ShapeDtypeStruct(s, d) for s, d in ou...  38.2 us
    ppermute x25, starting transfers between devices, step(): return lax.ppermute(x, axis, [(i, (i + by) % n) for i in range(n)])  35.3 us
    ppermute x25, waiting for transfers between devices, step(): return lax.ppermute(x, axis, [(i, (i + by) % n) for i in range(n)])  23.7 us
  transfers between devices with their start and end apart: 25, of which 9 were waited for; matrix products, arithmetic and copies ran while one was open for 0% of the time, Pallas kernels for 11%

profile of v3, /device:TPU:1, one launch (start us, length us, event | category | flops | bytes accessed | tf_op | source)
XLA Modules:
  0.0 193.9 jit_solution(90899816521011789)
XLA Ops:
  0.7 2.0 %collective-permute-start = (bf16[32,1024]{1,0:T(8,128)(2,1)}, bf16[32,1024]{1,0:T(8,128)(2,1)S(1)}, u32[]{:S(2)}, u32[]{:S(2)}) collective-permute-start(bf16[32,1024]{1,0:T(8,128)(2,1)} %bitcast.38), channel_id=1, source_target_pairs={{0,1},{1,2},{2,3},{3,0},{4,5},{5,6},{6,7},{7,4},{8,9},{9,10},{10,1... | collective-permute-start | bytes 196616 | tf_op jit(solution)/shard_map/ppermute | solution.py:36
  6.7 2.4 %collective-permute-done.2.d_ref = bf16[32,1024]{1,0:T(8,128)(2,1)S(1)} collective-permute-done((bf16[32,1024]{1,0:T(8,128)(2,1)}, bf16[32,1024]{1,0:T(8,128)(2,1)S(1)}, u32[]{:S(2)}, u32[]{:S(2)}) %collective-permute-start.2) | collective-permute-done | bytes 65568 | tf_op jit(solution)/shard_map/ppermute | solution.py:36
  9.1 5.7 %collective-permute-start.7 = (bf16[128,1024]{1,0:T(8,128)(2,1)S(1)}, bf16[128,1024]{1,0:T(8,128)(2,1)S(1)}, u32[]{:S(2)}, u32[]{:S(2)}) collective-permute-start(bf16[128,1024]{1,0:T(8,128)(2,1)S(1)} %shard_map.60.s_ref), channel_id=1, source_target_pairs={{0,28},{4,0},{8,4},{12,8},{16,12},{20,16},{24,20},{28,24},{1,29},{... | collective-permute-start | bytes 786440 | tf_op jit(solution)/shard_map/ppermute | solution.py:36
  14.7 3.3 %collective-permute-done.7.l = bf16[128,1024]{1,0:T(8,128)(2,1)S(1)} collective-permute-done((bf16[128,1024]{1,0:T(8,128)(2,1)S(1)}, bf16[128,1024]{1,0:T(8,128)(2,1)S(1)}, u32[]{:S(2)}, u32[]{:S(2)}) %collective-permute-start.7) | collective-permute-done | bytes 262176 | tf_op jit(solution)/shard_map/ppermute | solution.py:36
  18.0 3.1 %collective-permute-start.8 = (bf16[128,1024]{1,0:T(8,128)(2,1)S(1)}, bf16[128,1024]{1,0:T(8,128)(2,1)S(1)}, u32[]{:S(2)}, u32[]{:S(2)}) collective-permute-start(bf16[128,1024]{1,0:T(8,128)(2,1)S(1)} %collective-permute-done.7.l), channel_id=1, source_target_pairs={{0,28},{4,0},{8,4},{12,8},{16,12},{20,16},{24,20},{28,24},{1,29},{... | collective-permute-start | bytes 786440 | tf_op jit(solution)/shard_map/ppermute | solution.py:36
  21.2 3.3 %collective-permute-done.8.l = bf16[128,1024]{1,0:T(8,128)(2,1)S(1)} collective-permute-done((bf16[128,1024]{1,0:T(8,128)(2,1)S(1)}, bf16[128,1024]{1,0:T(8,128)(2,1)S(1)}, u32[]{:S(2)}, u32[]{:S(2)}) %collective-permute-start.8) | collective-permute-done | bytes 262176 | tf_op jit(solution)/shard_map/ppermute | solution.py:36
  24.5 3.1 %collective-permute-start.9 = (bf16[128,1024]{1,0:T(8,128)(2,1)S(1)}, bf16[128,1024]{1,0:T(8,128)(2,1)S(1)}, u32[]{:S(2)}, u32[]{:S(2)}) collective-permute-start(bf16[128,1024]{1,0:T(8,128)(2,1)S(1)} %collective-permute-done.8.l), channel_id=1, source_target_pairs={{0,28},{4,0},{8,4},{12,8},{16,12},{20,16},{24,20},{28,24},{1,29},{... | collective-permute-start | bytes 786440 | tf_op jit(solution)/shard_map/ppermute | solution.py:36
  27.6 3.7 %collective-permute-done.9.l = bf16[128,1024]{1,0:T(8,128)(2,1)S(1)} collective-permute-done((bf16[128,1024]{1,0:T(8,128)(2,1)S(1)}, bf16[128,1024]{1,0:T(8,128)(2,1)S(1)}, u32[]{:S(2)}, u32[]{:S(2)}) %collective-permute-start.9) | collective-permute-done | bytes 262176 | tf_op jit(solution)/shard_map/ppermute | solution.py:36
  31.3 3.2 %collective-permute-start.10 = (bf16[64,1024]{1,0:T(8,128)(2,1)S(1)}, bf16[64,1024]{1,0:T(8,128)(2,1)S(1)}, u32[]{:S(2)}, u32[]{:S(2)}) collective-permute-start(bf16[64,1024]{1,0:T(8,128)(2,1)S(1)} %slice.121), channel_id=1, source_target_pairs={{0,28},{4,0},{8,4},{12,8},{16,12},{20,16},{24,20},{28,24},{1,29},{... | collective-permute-start | bytes 393224 | tf_op jit(solution)/shard_map/ppermute | solution.py:36
  35.0 2.2 %copy-done = bf16[2048,1024]{1,0:T(8,128)(2,1)S(1)} copy-done((bf16[2048,1024]{1,0:T(8,128)(2,1)S(1)}, bf16[2048,1024]{1,0:T(8,128)(2,1)}, u32[]{:S(2)}) %copy-start) | copy-done | bytes 4194328
  37.2 2.6 %shard_map.61 = (f32[1024,2048]{1,0:T(8,128)S(1)}, bf16[32,32,1024]{2,1,0:T(8,128)(2,1)S(1)}, f32[8,128]{1,0:T(8,128)S(1)}) custom-call(s32[4]{0:T(128)S(1)} %pad_add_fusion.at_ref, bf16[128,1024]{1,0:T(8,128)(2,1)S(1)} %shard_map.60.s_ref, bf16[2048,1024]{1,0:T(8,128)(2,1)S(1)} %copy-done), custom_call_target="tpu_custom_call" | custom-call | tf_op jit(solution)/shard_map/pallas_call | solution.py:23
  39.8 3.6 %shard_map.62 = (f32[1024,2048]{1,0:T(8,128)S(1)}, bf16[32,32,1024]{2,1,0:T(8,128)(2,1)S(1)}, f32[8,128]{1,0:T(8,128)S(1)}) custom-call(s32[4]{0:T(128)S(1)} %pad_add_fusion.at_ref, bf16[128,1024]{1,0:T(8,128)(2,1)S(1)} %collective-permute-done.7.l, ...), custom_call_target="tpu_custom_call", output_to_operand_aliasing={{0}: (4, {}), {1}: (5, {}), {2}: (6, {})} | custom-call | tf_op jit(solution)/shard_map/pallas_call | solution.py:23
  43.4 3.7 %shard_map.63 = (f32[1024,2048]{1,0:T(8,128)S(1)}, bf16[32,32,1024]{2,1,0:T(8,128)(2,1)S(1)}, f32[8,128]{1,0:T(8,128)S(1)}) custom-call(s32[4]{0:T(128)S(1)} %pad_add_fusion.at_ref, bf16[128,1024]{1,0:T(8,128)(2,1)S(1)} %collective-permute-done.8.l, ...), custom_call_target="tpu_custom_call", output_to_operand_aliasing={{0}: (4, {}), {1}: (5, {}), {2}: (6, {})} | custom-call | tf_op jit(solution)/shard_map/pallas_call | solution.py:23
  47.1 3.7 %shard_map.64 = (f32[1024,2048]{1,0:T(8,128)S(1)}, bf16[32,32,1024]{2,1,0:T(8,128)(2,1)S(1)}, f32[8,128]{1,0:T(8,128)S(1)}) custom-call(s32[4]{0:T(128)S(1)} %pad_add_fusion.at_ref, bf16[128,1024]{1,0:T(8,128)(2,1)S(1)} %collective-permute-done.9.l, ...), custom_call_target="tpu_custom_call", output_to_operand_aliasing={{0}: (4, {}), {1}: (5, {}), {2}: (6, {})} | custom-call | tf_op jit(solution)/shard_map/pallas_call | solution.py:23
  50.8 4.8 %shard_map.65 = (f32[1024,2048]{1,0:T(8,128)S(1)}, bf16[32,32,1024]{2,1,0:T(8,128)(2,1)S(1)}, f32[8,128]{1,0:T(8,128)S(1)}, f32[32,16,128]{2,1,0:T(8,128)S(1)}) custom-call(s32[4]{0:T(128)S(1)} %pad_add_fusion.at_ref, bf16[64,1024]{1,0:T(8,128)(2,1)S(1)} %collective-permute-done.6.h0, ...), custom_call_target="tpu_custom_call", output_to_operand_aliasing={{0}: (4, {}), {1}: (5, {}), {2}: (6, {})} | custom-call | tf_op jit(solution)/shard_map/pallas_call | solution.py:23
  55.6 16.0 %all_to_all.35.e_ref = f32[32,16,128]{2,1,0:T(8,128)S(1)} all-to-all(f32[32,16,128]{2,1,0:T(8,128)S(1)} %get-tuple-element.61.mine_ref), channel_id=1, replica_groups=mesh['y'=4,'core'=2,'z'=8,'x'=4] {'z','x'}, dimensions={0} | all-to-all | bytes 524288 | tf_op jit(solution)/shard_map/all_to_all | solution.py:40
  72.6 18.2 %all_to_all.36.e_ref = f32[8,16,128]{2,1,0:T(8,128)S(1)} all-to-all(f32[8,16,128]{2,1,0:T(8,128)S(1)} %get-tuple-element.63), channel_id=1, replica_groups=mesh['y'=4,'core'=2,'z'=8,'x'=4] {'y','core'}, dimensions={0} | all-to-all | bytes 131072 | tf_op jit(solution)/shard_map/all_to_all | solution.py:40
  91.9 12.7 %all_to_all.37.e_ref = f32[32,8,128]{2,1,0:T(8,128)S(1)} all-to-all(f32[32,8,128]{2,1,0:T(8,128)S(1)} %get-tuple-element.65), channel_id=1, replica_groups=mesh['y'=4,'core'=2,'z'=8,'x'=4] {'z','x'}, dimensions={0} | all-to-all | bytes 262144 | tf_op jit(solution)/shard_map/all_to_all | solution.py:40
  105.6 9.5 %all_to_all.38.e_ref = f32[8,16,128]{2,1,0:T(8,128)S(1)} all-to-all(f32[8,16,128]{2,1,0:T(8,128)S(1)} %shard_map.68), channel_id=1, replica_groups=mesh['y'=4,'core'=2,'z'=8,'x'=4] {'y','core'}, dimensions={0} | all-to-all | bytes 131072 | tf_op jit(solution)/shard_map/all_to_all | solution.py:40
  116.3 12.3 %all_to_all.39.e_ref = f32[32,8,128]{2,1,0:T(8,128)S(1)} all-to-all(f32[32,8,128]{2,1,0:T(8,128)S(1)} %get-tuple-element.66), channel_id=1, replica_groups=mesh['y'=4,'core'=2,'z'=8,'x'=4] {'z','x'}, dimensions={0} | all-to-all | bytes 262144 | tf_op jit(solution)/shard_map/all_to_all | solution.py:40
  129.6 9.4 %all_to_all.40.e_ref = f32[8,16,128]{2,1,0:T(8,128)S(1)} all-to-all(f32[8,16,128]{2,1,0:T(8,128)S(1)} %shard_map.70), channel_id=1, replica_groups=mesh['y'=4,'core'=2,'z'=8,'x'=4] {'y','core'}, dimensions={0} | all-to-all | bytes 131072 | tf_op jit(solution)/shard_map/all_to_all | solution.py:40
  139.8 12.4 %all_to_all.41.e_ref = f32[32,8,128]{2,1,0:T(8,128)S(1)} all-to-all(f32[32,8,128]{2,1,0:T(8,128)S(1)} %get-tuple-element.67), channel_id=1, replica_groups=mesh['y'=4,'core'=2,'z'=8,'x'=4] {'z','x'}, dimensions={0} | all-to-all | bytes 262144 | tf_op jit(solution)/shard_map/all_to_all | solution.py:40
  155.2 2.3 %collective-permute-start.16 = (f32[128,2048]{1,0:T(8,128)S(1)}, f32[128,2048]{1,0:T(8,128)S(1)}, u32[]{:S(2)}, u32[]{:S(2)}) collective-permute-start(f32[128,2048]{1,0:T(8,128)S(1)} %shard_map.76), channel_id=1, source_target_pairs={{0,32},{32,0},{1,33},{33,1},{2,34},{34,2},{3,35},{35,3},{4,36},{36... | collective-permute-start | bytes 3145736 | tf_op jit(solution)/shard_map/ppermute | solution.py:36
  160.6 2.4 %shard_map.78 = (f32[128,2048]{1,0:T(8,128)S(1)}, f32[128,2048]{1,0:T(8,128)S(1)}) custom-call(s32[4]{0:T(128)S(1)} %pad_add_fusion.at_ref, bf16[32,32,1024]{2,1,0:T(8,128)(2,1)S(1)} %get-tuple-element.60.ft_ref, bf16[1024,2048]{1,0:T(8,128)(2,1)S(1)} %get-tuple-element.70.w_ref), custom_call_target="tpu_custom_call" | custom-call | tf_op jit(solution)/shard_map/pallas_call | solution.py:23
  163.9 2.4 %collective-permute-start.15 = (f32[24,128]{1,0:T(8,128)S(1)}, f32[24,128]{1,0:T(8,128)S(1)}, u32[]{:S(2)}, u32[]{:S(2)}) collective-permute-start(f32[24,128]{1,0:T(8,128)S(1)} %get-tuple-element.74.m0), channel_id=1, source_target_pairs={{0,192},{64,0},{128,64},{192,128},{1,193},{65,1},{129,65},{193,129... | collective-permute-start | bytes 36872 | tf_op jit(solution)/shard_map/ppermute | solution.py:36
  166.3 2.4 %shard_map.73 = (f32[128,2048]{1,0:T(8,128)S(1)}, f32[128,2048]{1,0:T(8,128)S(1)}) custom-call(s32[4]{0:T(128)S(1)} %pad_add_fusion.at_ref, bf16[32,32,1024]{2,1,0:T(8,128)(2,1)S(1)} %get-tuple-element.60.ft_ref, bf16[1024,2048]{1,0:T(8,128)(2,1)S(1)} %get-tuple-element.70.w_ref), custom_call_target="tpu_custom_call" | custom-call | tf_op jit(solution)/shard_map/pallas_call | solution.py:23
  171.5 1.8 collective-permute-start.23
  173.2 2.4 %shard_map.79 = (f32[128,2048]{1,0:T(8,128)S(1)}, f32[128,2048]{1,0:T(8,128)S(1)}) custom-call(s32[4]{0:T(128)S(1)} %pad_add_fusion.at_ref, bf16[32,32,1024]{2,1,0:T(8,128)(2,1)S(1)} %get-tuple-element.60.ft_ref, bf16[1024,2048]{1,0:T(8,128)(2,1)S(1)} %get-tuple-element.70.w_ref), custom_call_target="tpu_custom_call" | custom-call | tf_op jit(solution)/shard_map/pallas_call | solution.py:23
  175.7 2.8 %collective-permute-start.18 = (f16[64,2048]{1,0:T(8,128)(2,1)S(1)}, f16[64,2048]{1,0:T(8,128)(2,1)S(1)}, u32[]{:S(2)}, u32[]{:S(2)}) collective-permute-start(f16[64,2048]{1,0:T(8,128)(2,1)S(1)} %fusion.4), channel_id=1, source_target_pairs={{0,192},{64,0},{128,64},{192,128},{1,193},{65,1},{129,65},{193,129... | collective-permute-start | bytes 786440 | tf_op jit(solution)/shard_map/ppermute | solution.py:36
  178.8 3.3 %collective-permute-start.24 = (f16[64,2048]{1,0:T(8,128)(2,1)S(1)}, f16[64,2048]{1,0:T(8,128)(2,1)S(1)}, u32[]{:S(2)}, u32[]{:S(2)}) collective-permute-start(f16[64,2048]{1,0:T(8,128)(2,1)S(1)} %multiply_convert_fusion), channel_id=1, source_target_pairs={{0,192},{64,0},{128,64},{192,128},{1,193},{65,1},{129,65},{193,129... | collective-permute-start | bytes 786440 | tf_op jit(solution)/shard_map/ppermute | solution.py:36
  182.5 7.1 %collective-permute-done.24 = f16[64,2048]{1,0:T(8,128)(2,1)S(1)} collective-permute-done((f16[64,2048]{1,0:T(8,128)(2,1)S(1)}, f16[64,2048]{1,0:T(8,128)(2,1)S(1)}, u32[]{:S(2)}, u32[]{:S(2)}) %collective-permute-start.24) | collective-permute-done | bytes 262176 | tf_op jit(solution)/shard_map/ppermute | solution.py:36
  189.6 2.9 %collective-permute-done.21 = f16[64,2048]{1,0:T(8,128)(2,1)S(1)} collective-permute-done((f16[64,2048]{1,0:T(8,128)(2,1)S(1)}, f16[64,2048]{1,0:T(8,128)(2,1)S(1)}, u32[]{:S(2)}, u32[]{:S(2)}) %collective-permute-start.21) | collective-permute-done | bytes 262176 | tf_op jit(solution)/shard_map/ppermute | solution.py:36
  (69 shorter events, 22.5 us)
Async XLA Ops:
  0.7 5.9 %collective-permute-start = (bf16[32,1024]{1,0:T(8,128)(2,1)}, bf16[32,1024]{1,0:T(8,128)(2,1)S(1)}, u32[]{:S(2)}, u32[]{:S(2)}) collective-permute-start(bf16[32,1024]{1,0:T(8,128)(2,1)} %bitcast.38), channel_id=1, source_target_pairs={{0,1},{1,2},{2,3},{3,0},{4,5},{5,6},{6,7},{7,4},{8,9},{9,10},{10,1... | collective-permute-start | bytes 196616 | tf_op jit(solution)/shard_map/ppermute | solution.py:36
  2.8 3.9 %collective-permute-start.1 = (bf16[32,1024]{1,0:T(8,128)(2,1)}, bf16[32,1024]{1,0:T(8,128)(2,1)S(1)}, u32[]{:S(2)}, u32[]{:S(2)}) collective-permute-start(bf16[32,1024]{1,0:T(8,128)(2,1)} %bitcast.39), channel_id=1, source_target_pairs={{0,3},{1,0},{2,1},{3,2},{4,7},{5,4},{6,5},{7,6},{8,11},{9,8},{10,9... | collective-permute-start | bytes 196616 | tf_op jit(solution)/shard_map/ppermute | solution.py:36
  4.1 4.9 %collective-permute-start.2 = (bf16[32,1024]{1,0:T(8,128)(2,1)}, bf16[32,1024]{1,0:T(8,128)(2,1)S(1)}, u32[]{:S(2)}, u32[]{:S(2)}) collective-permute-start(bf16[32,1024]{1,0:T(8,128)(2,1)} %bitcast.40), channel_id=1, source_target_pairs={{0,2},{1,3},{2,0},{3,1},{4,6},{5,7},{6,4},{7,5},{8,10},{9,11},{10,... | collective-permute-start | bytes 196616 | tf_op jit(solution)/shard_map/ppermute | solution.py:36
  5.8 0.9 copy-start.3
  9.1 9.0 %collective-permute-start.7 = (bf16[128,1024]{1,0:T(8,128)(2,1)S(1)}, bf16[128,1024]{1,0:T(8,128)(2,1)S(1)}, u32[]{:S(2)}, u32[]{:S(2)}) collective-permute-start(bf16[128,1024]{1,0:T(8,128)(2,1)S(1)} %shard_map.60.s_ref), channel_id=1, source_target_pairs={{0,28},{4,0},{8,4},{12,8},{16,12},{20,16},{24,20},{28,24},{1,29},{... | collective-permute-start | bytes 786440 | tf_op jit(solution)/shard_map/ppermute | solution.py:36
  14.7 6.4 %collective-permute-start.3 = (bf16[128,1024]{1,0:T(8,128)(2,1)S(1)}, bf16[128,1024]{1,0:T(8,128)(2,1)S(1)}, u32[]{:S(2)}, u32[]{:S(2)}) collective-permute-start(bf16[128,1024]{1,0:T(8,128)(2,1)S(1)} %shard_map.60.s_ref), channel_id=1, source_target_pairs={{0,4},{4,8},{8,12},{12,16},{16,20},{20,24},{24,28},{28,0},{1,5},{5... | collective-permute-start | bytes 786440 | tf_op jit(solution)/shard_map/ppermute | solution.py:36
  18.0 6.4 %collective-permute-start.8 = (bf16[128,1024]{1,0:T(8,128)(2,1)S(1)}, bf16[128,1024]{1,0:T(8,128)(2,1)S(1)}, u32[]{:S(2)}, u32[]{:S(2)}) collective-permute-start(bf16[128,1024]{1,0:T(8,128)(2,1)S(1)} %collective-permute-done.7.l), channel_id=1, source_target_pairs={{0,28},{4,0},{8,4},{12,8},{16,12},{20,16},{24,20},{28,24},{1,29},{... | collective-permute-start | bytes 786440 | tf_op jit(solution)/shard_map/ppermute | solution.py:36
  21.2 6.4 %collective-permute-start.4 = (bf16[128,1024]{1,0:T(8,128)(2,1)S(1)}, bf16[128,1024]{1,0:T(8,128)(2,1)S(1)}, u32[]{:S(2)}, u32[]{:S(2)}) collective-permute-start(bf16[128,1024]{1,0:T(8,128)(2,1)S(1)} %collective-permute-done.3.r), channel_id=1, source_target_pairs={{0,4},{4,8},{8,12},{12,16},{16,20},{20,24},{24,28},{28,0},{1,5},{5... | collective-permute-start | bytes 786440 | tf_op jit(solution)/shard_map/ppermute | solution.py:36
  24.5 6.8 %collective-permute-start.9 = (bf16[128,1024]{1,0:T(8,128)(2,1)S(1)}, bf16[128,1024]{1,0:T(8,128)(2,1)S(1)}, u32[]{:S(2)}, u32[]{:S(2)}) collective-permute-start(bf16[128,1024]{1,0:T(8,128)(2,1)S(1)} %collective-permute-done.8.l), channel_id=1, source_target_pairs={{0,28},{4,0},{8,4},{12,8},{16,12},{20,16},{24,20},{28,24},{1,29},{... | collective-permute-start | bytes 786440 | tf_op jit(solution)/shard_map/ppermute | solution.py:36
  27.6 7.1 %collective-permute-start.5 = (bf16[128,1024]{1,0:T(8,128)(2,1)S(1)}, bf16[128,1024]{1,0:T(8,128)(2,1)S(1)}, u32[]{:S(2)}, u32[]{:S(2)}) collective-permute-start(bf16[128,1024]{1,0:T(8,128)(2,1)S(1)} %collective-permute-done.4.r), channel_id=1, source_target_pairs={{0,4},{4,8},{8,12},{12,16},{16,20},{20,24},{24,28},{28,0},{1,5},{5... | collective-permute-start | bytes 786440 | tf_op jit(solution)/shard_map/ppermute | solution.py:36
  31.3 19.5 %collective-permute-start.10 = (bf16[64,1024]{1,0:T(8,128)(2,1)S(1)}, bf16[64,1024]{1,0:T(8,128)(2,1)S(1)}, u32[]{:S(2)}, u32[]{:S(2)}) collective-permute-start(bf16[64,1024]{1,0:T(8,128)(2,1)S(1)} %slice.121), channel_id=1, source_target_pairs={{0,28},{4,0},{8,4},{12,8},{16,12},{20,16},{24,20},{28,24},{1,29},{... | collective-permute-start | bytes 393224 | tf_op jit(solution)/shard_map/ppermute | solution.py:36
  34.7 16.1 %collective-permute-start.6 = (bf16[64,1024]{1,0:T(8,128)(2,1)S(1)}, bf16[64,1024]{1,0:T(8,128)(2,1)S(1)}, u32[]{:S(2)}, u32[]{:S(2)}) collective-permute-start(bf16[64,1024]{1,0:T(8,128)(2,1)S(1)} %slice.120), channel_id=1, source_target_pairs={{0,4},{4,8},{8,12},{12,16},{16,20},{20,24},{24,28},{28,0},{1,5},{5... | collective-permute-start | bytes 393224 | tf_op jit(solution)/shard_map/ppermute | solution.py:36
  35.0 2.2 %copy-start = (bf16[2048,1024]{1,0:T(8,128)(2,1)S(1)}, bf16[2048,1024]{1,0:T(8,128)(2,1)}, u32[]{:S(2)}) copy-start(bf16[2048,1024]{1,0:T(8,128)(2,1)} %c_ref.9) | copy-start | bytes 12582916
  50.8 20.8 %copy-start.2 = (f32[1024]{0:T(1024)S(1)}, f32[1024]{0:T(1024)}, u32[]{:S(2)}) copy-start(f32[1024]{0:T(1024)} %param.6) | copy-start | bytes 12292
  71.6 19.2 %copy-start.1 = (f32[2048]{0:T(1024)S(1)}, f32[2048]{0:T(1024)}, u32[]{:S(2)}) copy-start(f32[2048]{0:T(1024)} %param.7) | copy-start | bytes 24580
  155.2 5.2 %collective-permute-start.16 = (f32[128,2048]{1,0:T(8,128)S(1)}, f32[128,2048]{1,0:T(8,128)S(1)}, u32[]{:S(2)}, u32[]{:S(2)}) collective-permute-start(f32[128,2048]{1,0:T(8,128)S(1)} %shard_map.76), channel_id=1, source_target_pairs={{0,32},{32,0},{1,33},{33,1},{2,34},{34,2},{3,35},{35,3},{4,36},{36... | collective-permute-start | bytes 3145736 | tf_op jit(solution)/shard_map/ppermute | solution.py:36
  157.5 2.3 %collective-permute-start.12 = (f32[24,128]{1,0:T(8,128)S(1)}, f32[24,128]{1,0:T(8,128)S(1)}, u32[]{:S(2)}, u32[]{:S(2)}) collective-permute-start(f32[24,128]{1,0:T(8,128)S(1)} %get-tuple-element.73.mine_ref), channel_id=1, source_target_pairs={{0,32},{32,0},{1,33},{33,1},{2,34},{34,2},{3,35},{35,3},{4,36},{36... | collective-permute-start | bytes 36872 | tf_op jit(solution)/shard_map/ppermute | solution.py:36
  163.0 12.6 %collective-permute-start.17 = (f32[128,2048]{1,0:T(8,128)S(1)}, f32[128,2048]{1,0:T(8,128)S(1)}, u32[]{:S(2)}, u32[]{:S(2)}) collective-permute-start(f32[128,2048]{1,0:T(8,128)S(1)} %get-tuple-element.80), channel_id=1, source_target_pairs={{0,32},{32,0},{1,33},{33,1},{2,34},{34,2},{3,35},{35,3},{4,36},{36... | collective-permute-start | bytes 3145736 | tf_op jit(solution)/shard_map/ppermute | solution.py:36
  163.4 15.0 %collective-permute-start.19 = (f32[128,2048]{1,0:T(8,128)S(1)}, f32[128,2048]{1,0:T(8,128)S(1)}, u32[]{:S(2)}, u32[]{:S(2)}) collective-permute-start(f32[128,2048]{1,0:T(8,128)S(1)} %get-tuple-element.79), channel_id=1, source_target_pairs={{0,32},{32,0},{1,33},{33,1},{2,34},{34,2},{3,35},{35,3},{4,36},{36... | collective-permute-start | bytes 3145736 | tf_op jit(solution)/shard_map/ppermute | solution.py:36
  163.6 5.1 %collective-permute-start.13 = (f32[24,128]{1,0:T(8,128)S(1)}, f32[24,128]{1,0:T(8,128)S(1)}, u32[]{:S(2)}, u32[]{:S(2)}) collective-permute-start(f32[24,128]{1,0:T(8,128)S(1)} %get-tuple-element.74.m0), channel_id=1, source_target_pairs={{0,64},{64,128},{128,192},{192,0},{1,65},{65,129},{129,193},{193,1... | collective-permute-start | bytes 36872 | tf_op jit(solution)/shard_map/ppermute | solution.py:36
  163.9 5.8 %collective-permute-start.15 = (f32[24,128]{1,0:T(8,128)S(1)}, f32[24,128]{1,0:T(8,128)S(1)}, u32[]{:S(2)}, u32[]{:S(2)}) collective-permute-start(f32[24,128]{1,0:T(8,128)S(1)} %get-tuple-element.74.m0), channel_id=1, source_target_pairs={{0,192},{64,0},{128,64},{192,128},{1,193},{65,1},{129,65},{193,129... | collective-permute-start | bytes 36872 | tf_op jit(solution)/shard_map/ppermute | solution.py:36
  166.3 4.0 %collective-permute-start.14 = (f32[24,128]{1,0:T(8,128)S(1)}, f32[24,128]{1,0:T(8,128)S(1)}, u32[]{:S(2)}, u32[]{:S(2)}) collective-permute-start(f32[24,128]{1,0:T(8,128)S(1)} %get-tuple-element.74.m0), channel_id=1, source_target_pairs={{0,128},{64,192},{128,0},{192,64},{1,129},{65,193},{129,1},{193,65... | collective-permute-start | bytes 36872 | tf_op jit(solution)/shard_map/ppermute | solution.py:36
  168.6 13.7 %collective-permute-start.11 = (f32[128,2048]{1,0:T(8,128)S(1)}, f32[128,2048]{1,0:T(8,128)S(1)}, u32[]{:S(2)}, u32[]{:S(2)}) collective-permute-start(f32[128,2048]{1,0:T(8,128)S(1)} %get-tuple-element.72), channel_id=1, source_target_pairs={{0,32},{32,0},{1,33},{33,1},{2,34},{34,2},{3,35},{35,3},{4,36},{36... | collective-permute-start | bytes 3145736 | tf_op jit(solution)/shard_map/ppermute | solution.py:36
  171.5 7.2 %collective-permute-start.23 = (f16[64,2048]{1,0:T(8,128)(2,1)S(1)}, f16[64,2048]{1,0:T(8,128)(2,1)S(1)}, u32[]{:S(2)}, u32[]{:S(2)}) collective-permute-start(f16[64,2048]{1,0:T(8,128)(2,1)S(1)} %get-tuple-element.93), channel_id=1, source_target_pairs={{0,192},{64,0},{128,64},{192,128},{1,193},{65,1},{129,65},{193,129... | collective-permute-start | bytes 786440 | tf_op jit(solution)/shard_map/ppermute | solution.py:36
  173.2 8.9 %collective-permute-start.20 = (f16[64,2048]{1,0:T(8,128)(2,1)S(1)}, f16[64,2048]{1,0:T(8,128)(2,1)S(1)}, u32[]{:S(2)}, u32[]{:S(2)}) collective-permute-start(f16[64,2048]{1,0:T(8,128)(2,1)S(1)} %get-tuple-element.92), channel_id=1, source_target_pairs={{0,64},{64,128},{128,192},{192,0},{1,65},{65,129},{129,193},{193,1... | collective-permute-start | bytes 786440 | tf_op jit(solution)/shard_map/ppermute | solution.py:36
  175.7 16.8 %collective-permute-start.18 = (f16[64,2048]{1,0:T(8,128)(2,1)S(1)}, f16[64,2048]{1,0:T(8,128)(2,1)S(1)}, u32[]{:S(2)}, u32[]{:S(2)}) collective-permute-start(f16[64,2048]{1,0:T(8,128)(2,1)S(1)} %fusion.4), channel_id=1, source_target_pairs={{0,192},{64,0},{128,64},{192,128},{1,193},{65,1},{129,65},{193,129... | collective-permute-start | bytes 786440 | tf_op jit(solution)/shard_map/ppermute | solution.py:36
  178.5 14.0 %collective-permute-start.22 = (f16[64,2048]{1,0:T(8,128)(2,1)S(1)}, f16[64,2048]{1,0:T(8,128)(2,1)S(1)}, u32[]{:S(2)}, u32[]{:S(2)}) collective-permute-start(f16[64,2048]{1,0:T(8,128)(2,1)S(1)} %fusion.2), channel_id=1, source_target_pairs={{0,64},{64,128},{128,192},{192,0},{1,65},{65,129},{129,193},{193,1... | collective-permute-start | bytes 786440 | tf_op jit(solution)/shard_map/ppermute | solution.py:36
  178.8 10.8 %collective-permute-start.24 = (f16[64,2048]{1,0:T(8,128)(2,1)S(1)}, f16[64,2048]{1,0:T(8,128)(2,1)S(1)}, u32[]{:S(2)}, u32[]{:S(2)}) collective-permute-start(f16[64,2048]{1,0:T(8,128)(2,1)S(1)} %multiply_convert_fusion), channel_id=1, source_target_pairs={{0,192},{64,0},{128,64},{192,128},{1,193},{65,1},{129,65},{193,129... | collective-permute-start | bytes 786440 | tf_op jit(solution)/shard_map/ppermute | solution.py:36
  182.3 10.3 %collective-permute-start.21 = (f16[64,2048]{1,0:T(8,128)(2,1)S(1)}, f16[64,2048]{1,0:T(8,128)(2,1)S(1)}, u32[]{:S(2)}, u32[]{:S(2)}) collective-permute-start(f16[64,2048]{1,0:T(8,128)(2,1)S(1)} %multiply_convert_fusion.1), channel_id=1, source_target_pairs={{0,64},{64,128},{128,192},{192,0},{1,65},{65,129},{129,193},{193,1... | collective-permute-start | bytes 786440 | tf_op jit(solution)/shard_map/ppermute | solution.py:36

commit v4 on v3

--- a/solution.py
+++ b/solution.py
@@ -65,8 +65,9 @@
     for k, (by, parts) in enumerate(pieces):
         at = around(at_ref, 2, by, 8)
         for (ref, row), off in zip(parts, (0, -1, 1, 2)):
-            ft_ref[4 * at + around(at_ref, 3, off, 4)] = ref[row : row + 32, :]
-        piece = ft_ref[pl.ds(4 * at, 4)].reshape(128, ROWS)
+            place = pl.multiple_of(32 * around(at_ref, 3, off, 4), 32)
+            ft_ref[at, pl.ds(place, 32), :] = ref[row : row + 32, :]
+        piece = ft_ref[at]
         top = jnp.max(jnp.abs(piece), axis=0, keepdims=True).astype(F32)
         fa_ref[pl.ds(at, 1), :] = jnp.broadcast_to(jnp.max(top, axis=1, keepdims=True), (1, 128))
         fs_ref[:, 128 * k : 128 * k + 128] = piece.T
@@ -134,38 +135,37 @@
     p_ref[...] = jnp.broadcast_to(jnp.concatenate(lines, axis=0)[None], p_ref.shape)
 
 
-def columns(k_ref, scale, by_ref, o_ref):
+def columns(k_ref, scale, o_ref):
+    acc = [jnp.zeros((8, 128), F32)] * CB
     for b in range(RB):
-        by_ref[128 * b : 128 * b + 128, :] = down(scale[b : b + 1])
-
-    def block(b, acc):
-        rows = pl.ds(pl.multiple_of(128 * b, 128), 128)
-        by = by_ref[rows, :]
-        parts = (k_ref[rows, 128 * t : 128 * t + 128] * by for t in range(CB))
-        return tuple(a + jnp.sum(p.reshape(16, 8, 128), axis=0) for a, p in zip(acc, parts))
-
-    acc = lax.fori_loop(0, RB, block, (jnp.zeros((8, 128), F32),) * CB)
+        rows = slice(128 * b, 128 * b + 128)
+        by = down(scale[b : b + 1])
+        for t in range(CB):
+            part = k_ref[rows, 128 * t : 128 * t + 128] * by
+            acc[t] = acc[t] + jnp.sum(part.reshape(16, 8, 128), axis=0)
     z = jnp.concatenate([jnp.sum(a, axis=0, keepdims=True) for a in acc], axis=0)
     o_ref[...] = jnp.broadcast_to(z[None], o_ref.shape)
 
 
-def first_column_body(e_ref, mine_ref, a_ref, k_ref, o_ref, f_ref, by_ref):
+def first_column_body(e_ref, mine_ref, a_ref, k_ref, o_ref, f_ref):
     peaks = e_ref[:, 0:RB, :]
     top = jnp.max(peaks, axis=0)
     total = jnp.sum(e_ref[:, RB : 2 * RB, :] * jnp.exp(peaks - top[None]), axis=0)
     fold = jnp.exp(mine_ref[0, 0:RB, :] - top)
     f_ref[...] = fold
-    columns(k_ref, (a_ref[...] / total) * fold, by_ref, o_ref)
-
-
-def column_body(e_ref, f_ref, a_ref, k_ref, o_ref, by_ref):
+    columns(k_ref, (a_ref[...] / total) * fold, o_ref)
+
+
+def column_body(e_ref, f_ref, a_ref, k_ref, o_ref):
     scale = a_ref[...] / jnp.sum(e_ref[...], axis=0)
-    columns(k_ref, scale * f_ref[...], by_ref, o_ref)
-
-
-def row_body(e_ref, f_ref, b_ref, k_ref, o_ref, c_ref, acc_ref):
+    columns(k_ref, scale * f_ref[...], o_ref)
+
+
+def row_body(e_ref, f_ref, b_ref, k_ref, o_ref, *refs):
     scale = b_ref[...] / jnp.sum(e_ref[...], axis=0)
-    c_ref[...] = scale
+    acc_ref = refs[-1]
+    if len(refs) > 1:
+        refs[0][...] = scale
 
     def block(b, carry):
         rows = pl.ds(pl.multiple_of(128 * b, 128), 128)
@@ -188,38 +188,21 @@
 
 
 def product_of(at_ref, ft_ref, w_ref, o_ref, by, side):
-    feats = ft_ref[pl.ds(4 * target(at_ref, by, side), 4)].reshape(128, ROWS)
+    feats = ft_ref[target(at_ref, by, side)]
     o_ref[...] = jnp.dot(feats, w_ref[...], preferred_element_type=F32)
 
 
-def halves_of(at_ref, ft_ref, w_ref, o_ref, by, side):
-    d = 4 * target(at_ref, by, side)
-
-    def block(b, carry):
-        cols = pl.ds(pl.multiple_of(1024 * b, 1024), 1024)
-        feats = ft_ref[pl.ds(d, 4)].reshape(128, ROWS)
-        o_ref[:, cols] = jnp.dot(feats, w_ref[:, cols], preferred_element_type=F32)
-        return carry
-
-    lax.fori_loop(0, 2, block, 0)
-
-
-def weight_body(e_ref, f_ref, a_ref, c_ref, fa_ref, k_ref, w_ref, m_ref, by_ref):
+def weight_body(e_ref, f_ref, a_ref, c_ref, fa_ref, k_ref, w_ref, m_ref):
     scale = (a_ref[...] / jnp.sum(e_ref[...], axis=0)) * f_ref[...]
+    acc = [jnp.zeros((8, 128), F32)] * CB
     for b in range(RB):
-        by_ref[128 * b : 128 * b + 128, :] = down(scale[b : b + 1])
-
-    def block(b, acc):
-        rows = pl.ds(pl.multiple_of(128 * b, 128), 128)
-        by, total = by_ref[rows, :], []
+        rows = slice(128 * b, 128 * b + 128)
+        by = down(scale[b : b + 1])
         for t in range(CB):
             cols = slice(128 * t, 128 * t + 128)
             part = (k_ref[rows, cols] * by) * c_ref[t : t + 1, :]
-            total.append(acc[t] + jnp.sum(part.reshape(16, 8, 128), axis=0))
+            acc[t] = acc[t] + jnp.sum(part.reshape(16, 8, 128), axis=0)
             w_ref[rows, cols] = part.astype(BF16)
-        return tuple(total)
-
-    acc = lax.fori_loop(0, RB, block, (jnp.zeros((8, 128), F32),) * CB)
     m_ref[0:CB, :] = jnp.concatenate([jnp.sum(a, axis=0, keepdims=True) for a in acc], axis=0)
     m_ref[CB : CB + 8, :] = fa_ref[...]
 
@@ -232,7 +215,8 @@
     return jnp.where(q > 0, 32768.0 / jnp.where(q > 0, q, 1.0), 0.0)
 
 
-def chip_body(at_ref, mine_ref, other_ref, m_ref, i_ref):
+def chip_body(at_ref, ft_ref, w_ref, mine_ref, other_ref, o_ref, m_ref, i_ref):
+    product_of(at_ref, ft_ref, w_ref, o_ref, 2, 0)
     m_ref[0:CB, :] = mine_ref[0:CB, :] + other_ref[0:CB, :]
     m_ref[CB : CB + 8, :] = jnp.maximum(mine_ref[CB : CB + 8, :], other_ref[CB : CB + 8, :])
     for k, by in enumerate((2, 1, 3)):
@@ -257,9 +241,8 @@
 
 
 def product_body(which, at_ref, ft_ref, w_ref, *o_refs):
-    one = product_of if len(which) == 1 else halves_of
     for k, o_ref in enumerate(o_refs):
-        one(at_ref, ft_ref, w_ref, o_ref, *which[k])
+        product_of(at_ref, ft_ref, w_ref, o_ref, *which[k])
 
 
 def assigned(features, centroids, row_weight, centroid_share):
@@ -289,7 +272,7 @@
     strip_shape = [((128, ROWS), BF16)]
     (strip,) = call(own_body, strip_shape, [own], mib=4)
     (strip,) = call(join_body, strip_shape, [*parts, strip], mib=4, aliases={3: 0})
-    state = [((ROWS, COLS), F32), ((32, 32, ROWS), BF16), ((8, 128), F32)]
+    state = [((ROWS, COLS), F32), ((8, 128, ROWS), BF16), ((8, 128), F32)]
     right = [strip, ring(strip, 1)]
     left = [strip, ring(strip, -1)]
     kernel, ft, fa = scores(score0_body, state, [at, strip, centroids], 128)
@@ -316,38 +299,27 @@
     lines = [pltpu.VMEM((ROWS, 128), F32)]
     got = everyone(peaks, CENT)
     sums, fold = call(
-        first_column_body,
-        [((8, CB, 128), F32), ((RB, 128), F32)],
-        [got, peaks, a, kernel],
-        scratch=lines,
-        mib=8,
+        first_column_body, [((8, CB, 128), F32), ((RB, 128), F32)], [got, peaks, a, kernel], mib=8
     )
     for it in range(ITERS):
-        rows, cscale = call(
+        rows, *cscale = call(
             row_body,
-            [((32, RB, 128), F32), ((CB, 128), F32)],
+            [((32, RB, 128), F32)] + [((CB, 128), F32)] * (it == ITERS - 1),
             [everyone(sums, DP), fold, share, kernel],
             scratch=lines,
             mib=8,
         )
         got = everyone(rows, CENT)
         if it < ITERS - 1:
-            (sums,) = call(
-                column_body, [((8, CB, 128), F32)], [got, fold, a, kernel], scratch=lines, mib=8
-            )
+            (sums,) = call(column_body, [((8, CB, 128), F32)], [got, fold, a, kernel], mib=8)
     weights, mass = call(
         weight_body,
         [((ROWS, COLS), BF16), ((CB + 8, 128), F32)],
-        [got, fold, a, cscale, fa, kernel],
-        scratch=lines,
+        [got, fold, a, *cscale, fa, kernel],
         mib=8,
     )
 
     other = step(mass, "core", 1)
-    chip, packs = call(
-        chip_body, [((CB + 8, 128), F32), ((3, CB, 128), F32)], [at, mass, other], mib=4
-    )
-    packs = packs.reshape(3, 1, COLS)
 
     def products(which, where):
         return call(
@@ -363,10 +335,16 @@
     low, high = slice(0, 64), slice(64, 128)
     (give,) = products([(2, 1)], at)
     theirs = step(give, "core", 1)
-    (mine,) = products([(2, 0)], after(at, give))
+    mine, chip, packs = call(
+        chip_body,
+        [((128, COLS), F32), ((CB + 8, 128), F32), ((3, CB, 128), F32)],
+        [after(at, give), ft, weights, mass, other],
+        mib=16,
+    )
+    packs = packs.reshape(3, 1, COLS)
     chips = {}
-    for by in (1, 3, 2):
-        chips[by] = step(chip, "y", by)
+    for by, mass in ((1, chip), (3, chip), (2, None)):
+        chips[by] = step(chips[1], "y", 1) if mass is None else step(mass, "y", by)
     up = ((mine[low] + theirs[low]) * packs[0]).astype(jnp.float16)
     down_ = ((mine[high] + theirs[high]) * packs[0]).astype(jnp.float16)
     first = (send(up, 1), send(down_, 3))

time: 194 us -> 194 us (level)
  waiting for transfers between devices: 23.7 us -> 30.6 us
  Pallas kernels: 38.2 us -> 34.3 us
  starting transfers between devices: 35.3 us -> 31.9 us
    ppermute x25, waiting for transfers between devices: 23.7 us -> 30.6 us  [step(): return lax.ppermute(x, axis, [(i, (i + by) % n) for i in range(n)])]
    pallas_call x22 -> x21, Pallas kernels: 38.2 us -> 34.3 us  [call(): pl.pallas_call(body, out_shape=[jax.ShapeDtypeStruct(s, d) for s, d in ou...]
    ppermute x25, starting transfers between devices: 35.3 us -> 31.9 us  [step(): return lax.ppermute(x, axis, [(i, (i + by) % n) for i in range(n)])]
  transfers between devices with their start and end apart: 25 -> 25, of which waited for: 9 -> 10; matrix products, arithmetic and copies ran while one was open for 0% -> 0% of each run, Pallas kernels for 11% -> 10%
where the time goes in v4:
time: 194 us; the launch traced here: 193 us
  blocking collectives  90.4 us (47%)
  Pallas kernels  34.3 us (18%)
  starting transfers between devices  31.9 us (16%)
  waiting for transfers between devices  30.6 us (16%)
  local copies, waits for them, and re-layouts  3.1 us (2%)
  other arithmetic  2.18 us (1%)
    all_to_all x7, blocking collectives, everyone(): return lax.all_to_all(x, axis, 0, 0, tiled=True)  90.4 us
    pallas_call x21, Pallas kernels, call(): pl.pallas_call(body, out_shape=[jax.ShapeDtypeStruct(s, d) for s, d in ou...  34.3 us
    ppermute x25, starting transfers between devices, step(): return lax.ppermute(x, axis, [(i, (i + by) % n) for i in range(n)])  31.9 us
    ppermute x25, waiting for transfers between devices, step(): return lax.ppermute(x, axis, [(i, (i + by) % n) for i in range(n)])  30.6 us
  transfers between devices with their start and end apart: 25, of which 10 were waited for; matrix products, arithmetic and copies ran while one was open for 0% of the time, Pallas kernels for 10%

profile of v4, /device:TPU:1, one launch (start us, length us, event | category | flops | bytes accessed | tf_op | source)
XLA Modules:
  0.0 193.3 jit_solution(10824608595844054464)
XLA Ops:
  0.7 2.0 %collective-permute-start = (bf16[32,1024]{1,0:T(8,128)(2,1)}, bf16[32,1024]{1,0:T(8,128)(2,1)S(1)}, u32[]{:S(2)}, u32[]{:S(2)}) collective-permute-start(bf16[32,1024]{1,0:T(8,128)(2,1)} %bitcast.38), channel_id=1, source_target_pairs={{0,1},{1,2},{2,3},{3,0},{4,5},{5,6},{6,7},{7,4},{8,9},{9,10},{10,1... | collective-permute-start | bytes 196616 | tf_op jit(solution)/shard_map/ppermute | solution.py:36
  4.1 1.6 collective-permute-start.2
  6.7 2.4 %collective-permute-done.2.d_ref = bf16[32,1024]{1,0:T(8,128)(2,1)S(1)} collective-permute-done((bf16[32,1024]{1,0:T(8,128)(2,1)}, bf16[32,1024]{1,0:T(8,128)(2,1)S(1)}, u32[]{:S(2)}, u32[]{:S(2)}) %collective-permute-start.2) | collective-permute-done | bytes 65568 | tf_op jit(solution)/shard_map/ppermute | solution.py:36
  9.1 5.7 %collective-permute-start.7 = (bf16[128,1024]{1,0:T(8,128)(2,1)S(1)}, bf16[128,1024]{1,0:T(8,128)(2,1)S(1)}, u32[]{:S(2)}, u32[]{:S(2)}) collective-permute-start(bf16[128,1024]{1,0:T(8,128)(2,1)S(1)} %shard_map.60.s_ref), channel_id=1, source_target_pairs={{0,28},{4,0},{8,4},{12,8},{16,12},{20,16},{24,20},{28,24},{1,29},{... | collective-permute-start | bytes 786440 | tf_op jit(solution)/shard_map/ppermute | solution.py:36
  14.7 3.3 %collective-permute-done.7.l = bf16[128,1024]{1,0:T(8,128)(2,1)S(1)} collective-permute-done((bf16[128,1024]{1,0:T(8,128)(2,1)S(1)}, bf16[128,1024]{1,0:T(8,128)(2,1)S(1)}, u32[]{:S(2)}, u32[]{:S(2)}) %collective-permute-start.7) | collective-permute-done | bytes 262176 | tf_op jit(solution)/shard_map/ppermute | solution.py:36
  18.0 3.1 %collective-permute-start.8 = (bf16[128,1024]{1,0:T(8,128)(2,1)S(1)}, bf16[128,1024]{1,0:T(8,128)(2,1)S(1)}, u32[]{:S(2)}, u32[]{:S(2)}) collective-permute-start(bf16[128,1024]{1,0:T(8,128)(2,1)S(1)} %collective-permute-done.7.l), channel_id=1, source_target_pairs={{0,28},{4,0},{8,4},{12,8},{16,12},{20,16},{24,20},{28,24},{1,29},{... | collective-permute-start | bytes 786440 | tf_op jit(solution)/shard_map/ppermute | solution.py:36
  21.2 3.3 %collective-permute-done.8.l = bf16[128,1024]{1,0:T(8,128)(2,1)S(1)} collective-permute-done((bf16[128,1024]{1,0:T(8,128)(2,1)S(1)}, bf16[128,1024]{1,0:T(8,128)(2,1)S(1)}, u32[]{:S(2)}, u32[]{:S(2)}) %collective-permute-start.8) | collective-permute-done | bytes 262176 | tf_op jit(solution)/shard_map/ppermute | solution.py:36
  24.5 3.1 %collective-permute-start.9 = (bf16[128,1024]{1,0:T(8,128)(2,1)S(1)}, bf16[128,1024]{1,0:T(8,128)(2,1)S(1)}, u32[]{:S(2)}, u32[]{:S(2)}) collective-permute-start(bf16[128,1024]{1,0:T(8,128)(2,1)S(1)} %collective-permute-done.8.l), channel_id=1, source_target_pairs={{0,28},{4,0},{8,4},{12,8},{16,12},{20,16},{24,20},{28,24},{1,29},{... | collective-permute-start | bytes 786440 | tf_op jit(solution)/shard_map/ppermute | solution.py:36
  27.6 3.7 %collective-permute-done.9.l = bf16[128,1024]{1,0:T(8,128)(2,1)S(1)} collective-permute-done((bf16[128,1024]{1,0:T(8,128)(2,1)S(1)}, bf16[128,1024]{1,0:T(8,128)(2,1)S(1)}, u32[]{:S(2)}, u32[]{:S(2)}) %collective-permute-start.9) | collective-permute-done | bytes 262176 | tf_op jit(solution)/shard_map/ppermute | solution.py:36
  31.3 3.2 %collective-permute-start.10 = (bf16[64,1024]{1,0:T(8,128)(2,1)S(1)}, bf16[64,1024]{1,0:T(8,128)(2,1)S(1)}, u32[]{:S(2)}, u32[]{:S(2)}) collective-permute-start(bf16[64,1024]{1,0:T(8,128)(2,1)S(1)} %slice.121), channel_id=1, source_target_pairs={{0,28},{4,0},{8,4},{12,8},{16,12},{20,16},{24,20},{28,24},{1,29},{... | collective-permute-start | bytes 393224 | tf_op jit(solution)/shard_map/ppermute | solution.py:36
  35.0 2.2 %copy-done = bf16[2048,1024]{1,0:T(8,128)(2,1)S(1)} copy-done((bf16[2048,1024]{1,0:T(8,128)(2,1)S(1)}, bf16[2048,1024]{1,0:T(8,128)(2,1)}, u32[]{:S(2)}) %copy-start) | copy-done | bytes 4194328
  37.2 2.6 %shard_map.61 = (f32[1024,2048]{1,0:T(8,128)S(1)}, bf16[8,128,1024]{2,1,0:T(8,128)(2,1)S(1)}, f32[8,128]{1,0:T(8,128)S(1)}) custom-call(s32[4]{0:T(128)S(1)} %pad_add_fusion.at_ref, bf16[128,1024]{1,0:T(8,128)(2,1)S(1)} %shard_map.60.s_ref, bf16[2048,1024]{1,0:T(8,128)(2,1)S(1)} %copy-done), custom_call_target="tpu_custom_call" | custom-call | tf_op jit(solution)/shard_map/pallas_call | solution.py:23
  39.8 3.7 %shard_map.62 = (f32[1024,2048]{1,0:T(8,128)S(1)}, bf16[8,128,1024]{2,1,0:T(8,128)(2,1)S(1)}, f32[8,128]{1,0:T(8,128)S(1)}) custom-call(s32[4]{0:T(128)S(1)} %pad_add_fusion.at_ref, bf16[128,1024]{1,0:T(8,128)(2,1)S(1)} %collective-permute-done.7.l, ...), custom_call_target="tpu_custom_call", output_to_operand_aliasing={{0}: (4, {}), {1}: (5, {}), {2}: (6, {})} | custom-call | tf_op jit(solution)/shard_map/pallas_call | solution.py:23
  43.4 3.7 %shard_map.63 = (f32[1024,2048]{1,0:T(8,128)S(1)}, bf16[8,128,1024]{2,1,0:T(8,128)(2,1)S(1)}, f32[8,128]{1,0:T(8,128)S(1)}) custom-call(s32[4]{0:T(128)S(1)} %pad_add_fusion.at_ref, bf16[128,1024]{1,0:T(8,128)(2,1)S(1)} %collective-permute-done.8.l, ...), custom_call_target="tpu_custom_call", output_to_operand_aliasing={{0}: (4, {}), {1}: (5, {}), {2}: (6, {})} | custom-call | tf_op jit(solution)/shard_map/pallas_call | solution.py:23
  47.1 3.7 %shard_map.64 = (f32[1024,2048]{1,0:T(8,128)S(1)}, bf16[8,128,1024]{2,1,0:T(8,128)(2,1)S(1)}, f32[8,128]{1,0:T(8,128)S(1)}) custom-call(s32[4]{0:T(128)S(1)} %pad_add_fusion.at_ref, bf16[128,1024]{1,0:T(8,128)(2,1)S(1)} %collective-permute-done.9.l, ...), custom_call_target="tpu_custom_call", output_to_operand_aliasing={{0}: (4, {}), {1}: (5, {}), {2}: (6, {})} | custom-call | tf_op jit(solution)/shard_map/pallas_call | solution.py:23
  50.8 4.8 %shard_map.65 = (f32[1024,2048]{1,0:T(8,128)S(1)}, bf16[8,128,1024]{2,1,0:T(8,128)(2,1)S(1)}, f32[8,128]{1,0:T(8,128)S(1)}, f32[32,16,128]{2,1,0:T(8,128)S(1)}) custom-call(s32[4]{0:T(128)S(1)} %pad_add_fusion.at_ref, bf16[64,1024]{1,0:T(8,128)(2,1)S(1)} %collective-permute-done.6.h0, ...), custom_call_target="tpu_custom_call", output_to_operand_aliasing={{0}: (4, {}), {1}: (5, {}), {2}: (6, {})} | custom-call | tf_op jit(solution)/shard_map/pallas_call | solution.py:23
  55.7 15.9 %all_to_all.35.e_ref = f32[32,16,128]{2,1,0:T(8,128)S(1)} all-to-all(f32[32,16,128]{2,1,0:T(8,128)S(1)} %get-tuple-element.60.mine_ref), channel_id=1, replica_groups=mesh['y'=4,'core'=2,'z'=8,'x'=4] {'z','x'}, dimensions={0} | all-to-all | bytes 524288 | tf_op jit(solution)/shard_map/all_to_all | solution.py:40
  72.4 18.2 %all_to_all.36.e_ref = f32[8,16,128]{2,1,0:T(8,128)S(1)} all-to-all(f32[8,16,128]{2,1,0:T(8,128)S(1)} %get-tuple-element.62), channel_id=1, replica_groups=mesh['y'=4,'core'=2,'z'=8,'x'=4] {'y','core'}, dimensions={0} | all-to-all | bytes 131072 | tf_op jit(solution)/shard_map/all_to_all | solution.py:40
  91.4 12.7 %all_to_all.37.e_ref = f32[32,8,128]{2,1,0:T(8,128)S(1)} all-to-all(f32[32,8,128]{2,1,0:T(8,128)S(1)} %shard_map.67), channel_id=1, replica_groups=mesh['y'=4,'core'=2,'z'=8,'x'=4] {'z','x'}, dimensions={0} | all-to-all | bytes 262144 | tf_op jit(solution)/shard_map/all_to_all | solution.py:40
  104.8 9.5 %all_to_all.38.e_ref = f32[8,16,128]{2,1,0:T(8,128)S(1)} all-to-all(f32[8,16,128]{2,1,0:T(8,128)S(1)} %shard_map.68), channel_id=1, replica_groups=mesh['y'=4,'core'=2,'z'=8,'x'=4] {'y','core'}, dimensions={0} | all-to-all | bytes 131072 | tf_op jit(solution)/shard_map/all_to_all | solution.py:40
  115.1 12.3 %all_to_all.39.e_ref = f32[32,8,128]{2,1,0:T(8,128)S(1)} all-to-all(f32[32,8,128]{2,1,0:T(8,128)S(1)} %shard_map.69), channel_id=1, replica_groups=mesh['y'=4,'core'=2,'z'=8,'x'=4] {'z','x'}, dimensions={0} | all-to-all | bytes 262144 | tf_op jit(solution)/shard_map/all_to_all | solution.py:40
  128.2 9.4 %all_to_all.40.e_ref = f32[8,16,128]{2,1,0:T(8,128)S(1)} all-to-all(f32[8,16,128]{2,1,0:T(8,128)S(1)} %shard_map.70), channel_id=1, replica_groups=mesh['y'=4,'core'=2,'z'=8,'x'=4] {'y','core'}, dimensions={0} | all-to-all | bytes 131072 | tf_op jit(solution)/shard_map/all_to_all | solution.py:40
  138.5 12.4 %all_to_all.41.e_ref = f32[32,8,128]{2,1,0:T(8,128)S(1)} all-to-all(f32[32,8,128]{2,1,0:T(8,128)S(1)} %get-tuple-element.64), channel_id=1, replica_groups=mesh['y'=4,'core'=2,'z'=8,'x'=4] {'z','x'}, dimensions={0} | all-to-all | bytes 262144 | tf_op jit(solution)/shard_map/all_to_all | solution.py:40
  153.5 2.3 %collective-permute-start.16 = (f32[128,2048]{1,0:T(8,128)S(1)}, f32[128,2048]{1,0:T(8,128)S(1)}, u32[]{:S(2)}, u32[]{:S(2)}) collective-permute-start(f32[128,2048]{1,0:T(8,128)S(1)} %shard_map.74), channel_id=1, source_target_pairs={{0,32},{32,0},{1,33},{33,1},{2,34},{34,2},{3,35},{35,3},{4,36},{36... | collective-permute-start | bytes 3145736 | tf_op jit(solution)/shard_map/ppermute | solution.py:36
  155.9 2.2 %collective-permute-done.12.other_ref = f32[24,128]{1,0:T(8,128)S(1)} collective-permute-done((f32[24,128]{1,0:T(8,128)S(1)}, f32[24,128]{1,0:T(8,128)S(1)}, u32[]{:S(2)}, u32[]{:S(2)}) %collective-permute-start.12) | collective-permute-done | bytes 12320 | tf_op jit(solution)/shard_map/ppermute | solution.py:36
  159.6 1.8 shard_map.77
  162.3 2.4 %collective-permute-start.15 = (f32[24,128]{1,0:T(8,128)S(1)}, f32[24,128]{1,0:T(8,128)S(1)}, u32[]{:S(2)}, u32[]{:S(2)}) collective-permute-start(f32[24,128]{1,0:T(8,128)S(1)} %get-tuple-element.72.m0), channel_id=1, source_target_pairs={{0,192},{64,0},{128,64},{192,128},{1,193},{65,1},{129,65},{193,129... | collective-permute-start | bytes 36872 | tf_op jit(solution)/shard_map/ppermute | solution.py:36
  164.7 1.8 shard_map.73
  168.1 3.2 %collective-permute-done.14.m2 = f32[24,128]{1,0:T(8,128)S(1)} collective-permute-done((f32[24,128]{1,0:T(8,128)S(1)}, f32[24,128]{1,0:T(8,128)S(1)}, u32[]{:S(2)}, u32[]{:S(2)}) %collective-permute-start.14) | collective-permute-done | bytes 12320 | tf_op jit(solution)/shard_map/ppermute | solution.py:36
  173.9 1.8 shard_map.78
  181.2 9.1 %collective-permute-done.24 = f16[64,2048]{1,0:T(8,128)(2,1)S(1)} collective-permute-done((f16[64,2048]{1,0:T(8,128)(2,1)S(1)}, f16[64,2048]{1,0:T(8,128)(2,1)S(1)}, u32[]{:S(2)}, u32[]{:S(2)}) %collective-permute-start.24) | collective-permute-done | bytes 262176 | tf_op jit(solution)/shard_map/ppermute | solution.py:36
  190.3 1.6 collective-permute-done.21
  (68 shorter events, 23.6 us)
Async XLA Ops:
  0.7 5.9 %collective-permute-start = (bf16[32,1024]{1,0:T(8,128)(2,1)}, bf16[32,1024]{1,0:T(8,128)(2,1)S(1)}, u32[]{:S(2)}, u32[]{:S(2)}) collective-permute-start(bf16[32,1024]{1,0:T(8,128)(2,1)} %bitcast.38), channel_id=1, source_target_pairs={{0,1},{1,2},{2,3},{3,0},{4,5},{5,6},{6,7},{7,4},{8,9},{9,10},{10,1... | collective-permute-start | bytes 196616 | tf_op jit(solution)/shard_map/ppermute | solution.py:36
  2.8 3.9 %collective-permute-start.1 = (bf16[32,1024]{1,0:T(8,128)(2,1)}, bf16[32,1024]{1,0:T(8,128)(2,1)S(1)}, u32[]{:S(2)}, u32[]{:S(2)}) collective-permute-start(bf16[32,1024]{1,0:T(8,128)(2,1)} %bitcast.39), channel_id=1, source_target_pairs={{0,3},{1,0},{2,1},{3,2},{4,7},{5,4},{6,5},{7,6},{8,11},{9,8},{10,9... | collective-permute-start | bytes 196616 | tf_op jit(solution)/shard_map/ppermute | solution.py:36
  4.1 4.9 %collective-permute-start.2 = (bf16[32,1024]{1,0:T(8,128)(2,1)}, bf16[32,1024]{1,0:T(8,128)(2,1)S(1)}, u32[]{:S(2)}, u32[]{:S(2)}) collective-permute-start(bf16[32,1024]{1,0:T(8,128)(2,1)} %bitcast.40), channel_id=1, source_target_pairs={{0,2},{1,3},{2,0},{3,1},{4,6},{5,7},{6,4},{7,5},{8,10},{9,11},{10,... | collective-permute-start | bytes 196616 | tf_op jit(solution)/shard_map/ppermute | solution.py:36
  5.8 0.9 copy-start.3
  9.1 9.0 %collective-permute-start.7 = (bf16[128,1024]{1,0:T(8,128)(2,1)S(1)}, bf16[128,1024]{1,0:T(8,128)(2,1)S(1)}, u32[]{:S(2)}, u32[]{:S(2)}) collective-permute-start(bf16[128,1024]{1,0:T(8,128)(2,1)S(1)} %shard_map.60.s_ref), channel_id=1, source_target_pairs={{0,28},{4,0},{8,4},{12,8},{16,12},{20,16},{24,20},{28,24},{1,29},{... | collective-permute-start | bytes 786440 | tf_op jit(solution)/shard_map/ppermute | solution.py:36
  14.7 6.4 %collective-permute-start.3 = (bf16[128,1024]{1,0:T(8,128)(2,1)S(1)}, bf16[128,1024]{1,0:T(8,128)(2,1)S(1)}, u32[]{:S(2)}, u32[]{:S(2)}) collective-permute-start(bf16[128,1024]{1,0:T(8,128)(2,1)S(1)} %shard_map.60.s_ref), channel_id=1, source_target_pairs={{0,4},{4,8},{8,12},{12,16},{16,20},{20,24},{24,28},{28,0},{1,5},{5... | collective-permute-start | bytes 786440 | tf_op jit(solution)/shard_map/ppermute | solution.py:36
  18.0 6.4 %collective-permute-start.8 = (bf16[128,1024]{1,0:T(8,128)(2,1)S(1)}, bf16[128,1024]{1,0:T(8,128)(2,1)S(1)}, u32[]{:S(2)}, u32[]{:S(2)}) collective-permute-start(bf16[128,1024]{1,0:T(8,128)(2,1)S(1)} %collective-permute-done.7.l), channel_id=1, source_target_pairs={{0,28},{4,0},{8,4},{12,8},{16,12},{20,16},{24,20},{28,24},{1,29},{... | collective-permute-start | bytes 786440 | tf_op jit(solution)/shard_map/ppermute | solution.py:36
  21.2 6.4 %collective-permute-start.4 = (bf16[128,1024]{1,0:T(8,128)(2,1)S(1)}, bf16[128,1024]{1,0:T(8,128)(2,1)S(1)}, u32[]{:S(2)}, u32[]{:S(2)}) collective-permute-start(bf16[128,1024]{1,0:T(8,128)(2,1)S(1)} %collective-permute-done.3.r), channel_id=1, source_target_pairs={{0,4},{4,8},{8,12},{12,16},{16,20},{20,24},{24,28},{28,0},{1,5},{5... | collective-permute-start | bytes 786440 | tf_op jit(solution)/shard_map/ppermute | solution.py:36
  24.5 6.8 %collective-permute-start.9 = (bf16[128,1024]{1,0:T(8,128)(2,1)S(1)}, bf16[128,1024]{1,0:T(8,128)(2,1)S(1)}, u32[]{:S(2)}, u32[]{:S(2)}) collective-permute-start(bf16[128,1024]{1,0:T(8,128)(2,1)S(1)} %collective-permute-done.8.l), channel_id=1, source_target_pairs={{0,28},{4,0},{8,4},{12,8},{16,12},{20,16},{24,20},{28,24},{1,29},{... | collective-permute-start | bytes 786440 | tf_op jit(solution)/shard_map/ppermute | solution.py:36
  27.6 7.1 %collective-permute-start.5 = (bf16[128,1024]{1,0:T(8,128)(2,1)S(1)}, bf16[128,1024]{1,0:T(8,128)(2,1)S(1)}, u32[]{:S(2)}, u32[]{:S(2)}) collective-permute-start(bf16[128,1024]{1,0:T(8,128)(2,1)S(1)} %collective-permute-done.4.r), channel_id=1, source_target_pairs={{0,4},{4,8},{8,12},{12,16},{16,20},{20,24},{24,28},{28,0},{1,5},{5... | collective-permute-start | bytes 786440 | tf_op jit(solution)/shard_map/ppermute | solution.py:36
  31.3 19.5 %collective-permute-start.10 = (bf16[64,1024]{1,0:T(8,128)(2,1)S(1)}, bf16[64,1024]{1,0:T(8,128)(2,1)S(1)}, u32[]{:S(2)}, u32[]{:S(2)}) collective-permute-start(bf16[64,1024]{1,0:T(8,128)(2,1)S(1)} %slice.121), channel_id=1, source_target_pairs={{0,28},{4,0},{8,4},{12,8},{16,12},{20,16},{24,20},{28,24},{1,29},{... | collective-permute-start | bytes 393224 | tf_op jit(solution)/shard_map/ppermute | solution.py:36
  34.7 16.1 %collective-permute-start.6 = (bf16[64,1024]{1,0:T(8,128)(2,1)S(1)}, bf16[64,1024]{1,0:T(8,128)(2,1)S(1)}, u32[]{:S(2)}, u32[]{:S(2)}) collective-permute-start(bf16[64,1024]{1,0:T(8,128)(2,1)S(1)} %slice.120), channel_id=1, source_target_pairs={{0,4},{4,8},{8,12},{12,16},{16,20},{20,24},{24,28},{28,0},{1,5},{5... | collective-permute-start | bytes 393224 | tf_op jit(solution)/shard_map/ppermute | solution.py:36
  35.0 2.2 %copy-start = (bf16[2048,1024]{1,0:T(8,128)(2,1)S(1)}, bf16[2048,1024]{1,0:T(8,128)(2,1)}, u32[]{:S(2)}) copy-start(bf16[2048,1024]{1,0:T(8,128)(2,1)} %c_ref.9) | copy-start | bytes 12582916
  50.8 20.8 %copy-start.2 = (f32[1024]{0:T(1024)S(1)}, f32[1024]{0:T(1024)}, u32[]{:S(2)}) copy-start(f32[1024]{0:T(1024)} %param.6) | copy-start | bytes 12292
  71.6 18.9 %copy-start.1 = (f32[2048]{0:T(1024)S(1)}, f32[2048]{0:T(1024)}, u32[]{:S(2)}) copy-start(f32[2048]{0:T(1024)} %param.7) | copy-start | bytes 24580
  153.5 5.9 %collective-permute-start.16 = (f32[128,2048]{1,0:T(8,128)S(1)}, f32[128,2048]{1,0:T(8,128)S(1)}, u32[]{:S(2)}, u32[]{:S(2)}) collective-permute-start(f32[128,2048]{1,0:T(8,128)S(1)} %shard_map.74), channel_id=1, source_target_pairs={{0,32},{32,0},{1,33},{33,1},{2,34},{34,2},{3,35},{35,3},{4,36},{36... | collective-permute-start | bytes 3145736 | tf_op jit(solution)/shard_map/ppermute | solution.py:36
  155.8 2.3 %collective-permute-start.12 = (f32[24,128]{1,0:T(8,128)S(1)}, f32[24,128]{1,0:T(8,128)S(1)}, u32[]{:S(2)}, u32[]{:S(2)}) collective-permute-start(f32[24,128]{1,0:T(8,128)S(1)} %get-tuple-element.71.mine_ref), channel_id=1, source_target_pairs={{0,32},{32,0},{1,33},{33,1},{2,34},{34,2},{3,35},{35,3},{4,36},{36... | collective-permute-start | bytes 36872 | tf_op jit(solution)/shard_map/ppermute | solution.py:36
  161.4 14.3 %collective-permute-start.17 = (f32[128,2048]{1,0:T(8,128)S(1)}, f32[128,2048]{1,0:T(8,128)S(1)}, u32[]{:S(2)}, u32[]{:S(2)}) collective-permute-start(f32[128,2048]{1,0:T(8,128)S(1)} %get-tuple-element.78), channel_id=1, source_target_pairs={{0,32},{32,0},{1,33},{33,1},{2,34},{34,2},{3,35},{35,3},{4,36},{36... | collective-permute-start | bytes 3145736 | tf_op jit(solution)/shard_map/ppermute | solution.py:36
  161.9 15.5 %collective-permute-start.19 = (f32[128,2048]{1,0:T(8,128)S(1)}, f32[128,2048]{1,0:T(8,128)S(1)}, u32[]{:S(2)}, u32[]{:S(2)}) collective-permute-start(f32[128,2048]{1,0:T(8,128)S(1)} %get-tuple-element.77), channel_id=1, source_target_pairs={{0,32},{32,0},{1,33},{33,1},{2,34},{34,2},{3,35},{35,3},{4,36},{36... | collective-permute-start | bytes 3145736 | tf_op jit(solution)/shard_map/ppermute | solution.py:36
  162.0 5.5 %collective-permute-start.13 = (f32[24,128]{1,0:T(8,128)S(1)}, f32[24,128]{1,0:T(8,128)S(1)}, u32[]{:S(2)}, u32[]{:S(2)}) collective-permute-start(f32[24,128]{1,0:T(8,128)S(1)} %get-tuple-element.72.m0), channel_id=1, source_target_pairs={{0,64},{64,128},{128,192},{192,0},{1,65},{65,129},{129,193},{193,1... | collective-permute-start | bytes 36872 | tf_op jit(solution)/shard_map/ppermute | solution.py:36
  162.3 5.2 %collective-permute-start.15 = (f32[24,128]{1,0:T(8,128)S(1)}, f32[24,128]{1,0:T(8,128)S(1)}, u32[]{:S(2)}, u32[]{:S(2)}) collective-permute-start(f32[24,128]{1,0:T(8,128)S(1)} %get-tuple-element.72.m0), channel_id=1, source_target_pairs={{0,192},{64,0},{128,64},{192,128},{1,193},{65,1},{129,65},{193,129... | collective-permute-start | bytes 36872 | tf_op jit(solution)/shard_map/ppermute | solution.py:36
  166.5 14.5 %collective-permute-start.11 = (f32[128,2048]{1,0:T(8,128)S(1)}, f32[128,2048]{1,0:T(8,128)S(1)}, u32[]{:S(2)}, u32[]{:S(2)}) collective-permute-start(f32[128,2048]{1,0:T(8,128)S(1)} %get-tuple-element.69), channel_id=1, source_target_pairs={{0,32},{32,0},{1,33},{33,1},{2,34},{34,2},{3,35},{35,3},{4,36},{36... | collective-permute-start | bytes 3145736 | tf_op jit(solution)/shard_map/ppermute | solution.py:36
  167.5 3.8 %collective-permute-start.14 = (f32[24,128]{1,0:T(8,128)S(1)}, f32[24,128]{1,0:T(8,128)S(1)}, u32[]{:S(2)}, u32[]{:S(2)}) collective-permute-start(f32[24,128]{1,0:T(8,128)S(1)} %collective-permute-done.13.m1), channel_id=1, source_target_pairs={{0,64},{64,128},{128,192},{192,0},{1,65},{65,129},{129,193},{193,1... | collective-permute-start | bytes 36872 | tf_op jit(solution)/shard_map/ppermute | solution.py:36
  172.4 6.6 %collective-permute-start.23 = (f16[64,2048]{1,0:T(8,128)(2,1)S(1)}, f16[64,2048]{1,0:T(8,128)(2,1)S(1)}, u32[]{:S(2)}, u32[]{:S(2)}) collective-permute-start(f16[64,2048]{1,0:T(8,128)(2,1)S(1)} %get-tuple-element.91), channel_id=1, source_target_pairs={{0,192},{64,0},{128,64},{192,128},{1,193},{65,1},{129,65},{193,129... | collective-permute-start | bytes 786440 | tf_op jit(solution)/shard_map/ppermute | solution.py:36
  172.5 8.3 %collective-permute-start.20 = (f16[64,2048]{1,0:T(8,128)(2,1)S(1)}, f16[64,2048]{1,0:T(8,128)(2,1)S(1)}, u32[]{:S(2)}, u32[]{:S(2)}) collective-permute-start(f16[64,2048]{1,0:T(8,128)(2,1)S(1)} %get-tuple-element.90), channel_id=1, source_target_pairs={{0,64},{64,128},{128,192},{192,0},{1,65},{65,129},{129,193},{193,1... | collective-permute-start | bytes 786440 | tf_op jit(solution)/shard_map/ppermute | solution.py:36
  175.9 16.1 %collective-permute-start.18 = (f16[64,2048]{1,0:T(8,128)(2,1)S(1)}, f16[64,2048]{1,0:T(8,128)(2,1)S(1)}, u32[]{:S(2)}, u32[]{:S(2)}) collective-permute-start(f16[64,2048]{1,0:T(8,128)(2,1)S(1)} %fusion.4), channel_id=1, source_target_pairs={{0,192},{64,0},{128,64},{192,128},{1,193},{65,1},{129,65},{193,129... | collective-permute-start | bytes 786440 | tf_op jit(solution)/shard_map/ppermute | solution.py:36
  177.4 14.5 %collective-permute-start.22 = (f16[64,2048]{1,0:T(8,128)(2,1)S(1)}, f16[64,2048]{1,0:T(8,128)(2,1)S(1)}, u32[]{:S(2)}, u32[]{:S(2)}) collective-permute-start(f16[64,2048]{1,0:T(8,128)(2,1)S(1)} %fusion.2), channel_id=1, source_target_pairs={{0,64},{64,128},{128,192},{192,0},{1,65},{65,129},{129,193},{193,1... | collective-permute-start | bytes 786440 | tf_op jit(solution)/shard_map/ppermute | solution.py:36
  179.2 11.1 %collective-permute-start.24 = (f16[64,2048]{1,0:T(8,128)(2,1)S(1)}, f16[64,2048]{1,0:T(8,128)(2,1)S(1)}, u32[]{:S(2)}, u32[]{:S(2)}) collective-permute-start(f16[64,2048]{1,0:T(8,128)(2,1)S(1)} %multiply_convert_fusion), channel_id=1, source_target_pairs={{0,192},{64,0},{128,64},{192,128},{1,193},{65,1},{129,65},{193,129... | collective-permute-start | bytes 786440 | tf_op jit(solution)/shard_map/ppermute | solution.py:36
  180.9 11.0 %collective-permute-start.21 = (f16[64,2048]{1,0:T(8,128)(2,1)S(1)}, f16[64,2048]{1,0:T(8,128)(2,1)S(1)}, u32[]{:S(2)}, u32[]{:S(2)}) collective-permute-start(f16[64,2048]{1,0:T(8,128)(2,1)S(1)} %multiply_convert_fusion.1), channel_id=1, source_target_pairs={{0,64},{64,128},{128,192},{192,0},{1,65},{65,129},{129,193},{193,1... | collective-permute-start | bytes 786440 | tf_op jit(solution)/shard_map/ppermute | solution.py:36

commit v5 on v4

--- a/solution.py
+++ b/solution.py
@@ -34,6 +34,11 @@
 def step(x, axis, by):
     n = lax.axis_size(axis)
     return lax.ppermute(x, axis, [(i, (i + by) % n) for i in range(n)])
+
+
+def step_apart(x):
+    ends = [(c, i, (i + 1 - 2 * c) % 4) for c in (0, 1) for i in range(4)]
+    return lax.ppermute(x, DP, [(2 * i + c, 2 * j + c) for c, i, j in ends])
 
 
 def everyone(x, axis):
@@ -223,19 +228,31 @@
         i_ref[k] = inverse(limits(at_ref, m_ref, by))
 
 
-def relay_body(at_ref, m0, m1, m3, i_ref, s_ref):
-    for k, (m, by) in enumerate(((m1, 1), (m3, 3))):
-        q = limits(at_ref, m, by)
+def sides(at_ref, near, other):
+    first = at_ref[1] == 0
+    return jnp.where(first, near[...], other[...]), jnp.where(first, other[...], near[...])
+
+
+def limits_of(at_ref, m, ref, by):
+    ref[...] = m
+    return limits(at_ref, ref, by)
+
+
+def relay_body(at_ref, m0, near, other, i_ref, s_ref, tmp):
+    for k, (m, by) in enumerate(zip(sides(at_ref, near, other), (1, 3))):
+        q = limits_of(at_ref, m, tmp, by)
         s_ref[k] = q * (1.0 / 32768.0)
         i_ref[k] = inverse(q + limits(at_ref, m0, by))
 
 
-def share_body(at_ref, m0, m1, m2, m3, t_ref, i_ref, s_ref):
+def share_body(at_ref, m0, near, m2, other, t_ref, i_ref, s_ref, tmp):
+    m1, m3 = sides(at_ref, near, other)
     total = (m0[0:CB, :] + m2[0:CB, :]) + (m1[0:CB, :] + m3[0:CB, :])
     t_ref[...] = total
     over = 1.0 / total
     i_ref[...] = over
-    q1, q2, q3 = (limits(at_ref, m, 0) * (1.0 / 32768.0) for m in (m1, m2, m3))
+    q1, q3 = (limits_of(at_ref, m, tmp, 0) * (1.0 / 32768.0) for m in (m1, m3))
+    q2 = limits(at_ref, m2, 0) * (1.0 / 32768.0)
     for k, q in enumerate((q1, q3, q1 + q2, q3 + q2)):
         s_ref[k] = q * over
 
@@ -342,9 +359,9 @@
         mib=16,
     )
     packs = packs.reshape(3, 1, COLS)
-    chips = {}
-    for by, mass in ((1, chip), (3, chip), (2, None)):
-        chips[by] = step(chips[1], "y", 1) if mass is None else step(mass, "y", by)
+    near = step_apart(chip)
+    other_near = step(near, "core", 1)
+    far_mass = step_apart(near)
     up = ((mine[low] + theirs[low]) * packs[0]).astype(jnp.float16)
     down_ = ((mine[high] + theirs[high]) * packs[0]).astype(jnp.float16)
     first = (send(up, 1), send(down_, 3))
@@ -355,7 +372,11 @@
     down_ = ((mines[1][low] + theirs[1][low]) * packs[2]).astype(jnp.float16)
     second = (send(up, 1), send(down_, 3))
     repacks, unpacks = call(
-        relay_body, [((2, CB, 128), F32)] * 2, [at, chip, chips[1], chips[3]], mib=4
+        relay_body,
+        [((2, CB, 128), F32)] * 2,
+        [at, chip, near, other_near],
+        scratch=[pltpu.VMEM((CB + 8, 128), F32)],
+        mib=4,
     )
     repacks, unpacks = repacks.reshape(2, 1, COLS), unpacks.reshape(2, 1, COLS)
     give, mine0 = products([(0, 1), (0, 0)], at)
@@ -363,7 +384,8 @@
     total, over, shares = call(
         share_body,
         [((CB, 128), F32), ((CB, 128), F32), ((4, CB, 128), F32)],
-        [at, chip, chips[1], chips[2], chips[3]],
+        [at, chip, near, far_mass, other_near],
+        scratch=[pltpu.VMEM((CB + 8, 128), F32)],
         mib=4,
     )
     mines, theirs, *_ = lax.optimization_barrier((mines, theirs, up, down_))

time: 194 us -> 196 us (1.010)
  starting transfers between devices: 31.9 us -> 36.5 us
  waiting for transfers between devices: 30.6 us -> 27.9 us
    ppermute x25 -> x23, waiting for transfers between devices: 30.6 us -> 26.2 us  [step(): return lax.ppermute(x, axis, [(i, (i + by) % n) for i in range(n)])]
    ppermute x25 -> x23, starting transfers between devices: 31.9 us -> 35.7 us  [step(): return lax.ppermute(x, axis, [(i, (i + by) % n) for i in range(n)])]
where the time goes in v5:
time: 196 us; the launch traced here: 195 us
  blocking collectives  90.4 us (46%)
  starting transfers between devices  36.5 us (19%)
  Pallas kernels  34.3 us (17%)
  waiting for transfers between devices  27.9 us (14%)
  local copies, waits for them, and re-layouts  3.1 us (2%)
  other arithmetic  2.19 us (1%)
    all_to_all x7, blocking collectives, everyone(): return lax.all_to_all(x, axis, 0, 0, tiled=True)  90.4 us
    ppermute x23, starting transfers between devices, step(): return lax.ppermute(x, axis, [(i, (i + by) % n) for i in range(n)])  35.7 us
    pallas_call x21, Pallas kernels, call(): pl.pallas_call(body, out_shape=[jax.ShapeDtypeStruct(s, d) for s, d in ou...  34.3 us
    ppermute x23, waiting for transfers between devices, step(): return lax.ppermute(x, axis, [(i, (i + by) % n) for i in range(n)])  26.2 us
  transfers between devices with their start and end apart: 25, of which 10 were waited for; matrix products, arithmetic and copies ran while one was open for 0% of the time, Pallas kernels for 10%

profile of v5, /device:TPU:1, one launch (start us, length us, event | category | flops | bytes accessed | tf_op | source)
XLA Modules:
  0.0 195.4 jit_solution(12213754472482657388)
XLA Ops:
  0.7 2.0 %collective-permute-start = (bf16[32,1024]{1,0:T(8,128)(2,1)}, bf16[32,1024]{1,0:T(8,128)(2,1)S(1)}, u32[]{:S(2)}, u32[]{:S(2)}) collective-permute-start(bf16[32,1024]{1,0:T(8,128)(2,1)} %bitcast.38), channel_id=1, source_target_pairs={{0,1},{1,2},{2,3},{3,0},{4,5},{5,6},{6,7},{7,4},{8,9},{9,10},{10,1... | collective-permute-start | bytes 196616 | tf_op jit(solution)/shard_map/ppermute | solution.py:36
  6.7 2.4 %collective-permute-done.2.d_ref = bf16[32,1024]{1,0:T(8,128)(2,1)S(1)} collective-permute-done((bf16[32,1024]{1,0:T(8,128)(2,1)}, bf16[32,1024]{1,0:T(8,128)(2,1)S(1)}, u32[]{:S(2)}, u32[]{:S(2)}) %collective-permute-start.2) | collective-permute-done | bytes 65568 | tf_op jit(solution)/shard_map/ppermute | solution.py:36
  9.1 5.7 %collective-permute-start.7 = (bf16[128,1024]{1,0:T(8,128)(2,1)S(1)}, bf16[128,1024]{1,0:T(8,128)(2,1)S(1)}, u32[]{:S(2)}, u32[]{:S(2)}) collective-permute-start(bf16[128,1024]{1,0:T(8,128)(2,1)S(1)} %shard_map.60.s_ref), channel_id=1, source_target_pairs={{0,28},{4,0},{8,4},{12,8},{16,12},{20,16},{24,20},{28,24},{1,29},{... | collective-permute-start | bytes 786440 | tf_op jit(solution)/shard_map/ppermute | solution.py:36
  14.7 3.3 %collective-permute-done.7.l = bf16[128,1024]{1,0:T(8,128)(2,1)S(1)} collective-permute-done((bf16[128,1024]{1,0:T(8,128)(2,1)S(1)}, bf16[128,1024]{1,0:T(8,128)(2,1)S(1)}, u32[]{:S(2)}, u32[]{:S(2)}) %collective-permute-start.7) | collective-permute-done | bytes 262176 | tf_op jit(solution)/shard_map/ppermute | solution.py:36
  18.0 3.1 %collective-permute-start.8 = (bf16[128,1024]{1,0:T(8,128)(2,1)S(1)}, bf16[128,1024]{1,0:T(8,128)(2,1)S(1)}, u32[]{:S(2)}, u32[]{:S(2)}) collective-permute-start(bf16[128,1024]{1,0:T(8,128)(2,1)S(1)} %collective-permute-done.7.l), channel_id=1, source_target_pairs={{0,28},{4,0},{8,4},{12,8},{16,12},{20,16},{24,20},{28,24},{1,29},{... | collective-permute-start | bytes 786440 | tf_op jit(solution)/shard_map/ppermute | solution.py:36
  21.2 3.3 %collective-permute-done.8.l = bf16[128,1024]{1,0:T(8,128)(2,1)S(1)} collective-permute-done((bf16[128,1024]{1,0:T(8,128)(2,1)S(1)}, bf16[128,1024]{1,0:T(8,128)(2,1)S(1)}, u32[]{:S(2)}, u32[]{:S(2)}) %collective-permute-start.8) | collective-permute-done | bytes 262176 | tf_op jit(solution)/shard_map/ppermute | solution.py:36
  24.5 3.1 %collective-permute-start.9 = (bf16[128,1024]{1,0:T(8,128)(2,1)S(1)}, bf16[128,1024]{1,0:T(8,128)(2,1)S(1)}, u32[]{:S(2)}, u32[]{:S(2)}) collective-permute-start(bf16[128,1024]{1,0:T(8,128)(2,1)S(1)} %collective-permute-done.8.l), channel_id=1, source_target_pairs={{0,28},{4,0},{8,4},{12,8},{16,12},{20,16},{24,20},{28,24},{1,29},{... | collective-permute-start | bytes 786440 | tf_op jit(solution)/shard_map/ppermute | solution.py:36
  27.6 3.7 %collective-permute-done.9.l = bf16[128,1024]{1,0:T(8,128)(2,1)S(1)} collective-permute-done((bf16[128,1024]{1,0:T(8,128)(2,1)S(1)}, bf16[128,1024]{1,0:T(8,128)(2,1)S(1)}, u32[]{:S(2)}, u32[]{:S(2)}) %collective-permute-start.9) | collective-permute-done | bytes 262176 | tf_op jit(solution)/shard_map/ppermute | solution.py:36
  31.3 3.2 %collective-permute-start.10 = (bf16[64,1024]{1,0:T(8,128)(2,1)S(1)}, bf16[64,1024]{1,0:T(8,128)(2,1)S(1)}, u32[]{:S(2)}, u32[]{:S(2)}) collective-permute-start(bf16[64,1024]{1,0:T(8,128)(2,1)S(1)} %slice.121), channel_id=1, source_target_pairs={{0,28},{4,0},{8,4},{12,8},{16,12},{20,16},{24,20},{28,24},{1,29},{... | collective-permute-start | bytes 393224 | tf_op jit(solution)/shard_map/ppermute | solution.py:36
  35.0 2.2 %copy-done = bf16[2048,1024]{1,0:T(8,128)(2,1)S(1)} copy-done((bf16[2048,1024]{1,0:T(8,128)(2,1)S(1)}, bf16[2048,1024]{1,0:T(8,128)(2,1)}, u32[]{:S(2)}) %copy-start) | copy-done | bytes 4194328
  37.2 2.6 %shard_map.61 = (f32[1024,2048]{1,0:T(8,128)S(1)}, bf16[8,128,1024]{2,1,0:T(8,128)(2,1)S(1)}, f32[8,128]{1,0:T(8,128)S(1)}) custom-call(s32[4]{0:T(128)S(1)} %pad_add_fusion.at_ref, bf16[128,1024]{1,0:T(8,128)(2,1)S(1)} %shard_map.60.s_ref, bf16[2048,1024]{1,0:T(8,128)(2,1)S(1)} %copy-done), custom_call_target="tpu_custom_call" | custom-call | tf_op jit(solution)/shard_map/pallas_call | solution.py:23
  39.8 3.7 %shard_map.62 = (f32[1024,2048]{1,0:T(8,128)S(1)}, bf16[8,128,1024]{2,1,0:T(8,128)(2,1)S(1)}, f32[8,128]{1,0:T(8,128)S(1)}) custom-call(s32[4]{0:T(128)S(1)} %pad_add_fusion.at_ref, bf16[128,1024]{1,0:T(8,128)(2,1)S(1)} %collective-permute-done.7.l, ...), custom_call_target="tpu_custom_call", output_to_operand_aliasing={{0}: (4, {}), {1}: (5, {}), {2}: (6, {})} | custom-call | tf_op jit(solution)/shard_map/pallas_call | solution.py:23
  43.4 3.7 %shard_map.63 = (f32[1024,2048]{1,0:T(8,128)S(1)}, bf16[8,128,1024]{2,1,0:T(8,128)(2,1)S(1)}, f32[8,128]{1,0:T(8,128)S(1)}) custom-call(s32[4]{0:T(128)S(1)} %pad_add_fusion.at_ref, bf16[128,1024]{1,0:T(8,128)(2,1)S(1)} %collective-permute-done.8.l, ...), custom_call_target="tpu_custom_call", output_to_operand_aliasing={{0}: (4, {}), {1}: (5, {}), {2}: (6, {})} | custom-call | tf_op jit(solution)/shard_map/pallas_call | solution.py:23
  47.1 3.7 %shard_map.64 = (f32[1024,2048]{1,0:T(8,128)S(1)}, bf16[8,128,1024]{2,1,0:T(8,128)(2,1)S(1)}, f32[8,128]{1,0:T(8,128)S(1)}) custom-call(s32[4]{0:T(128)S(1)} %pad_add_fusion.at_ref, bf16[128,1024]{1,0:T(8,128)(2,1)S(1)} %collective-permute-done.9.l, ...), custom_call_target="tpu_custom_call", output_to_operand_aliasing={{0}: (4, {}), {1}: (5, {}), {2}: (6, {})} | custom-call | tf_op jit(solution)/shard_map/pallas_call | solution.py:23
  50.8 4.8 %shard_map.65 = (f32[1024,2048]{1,0:T(8,128)S(1)}, bf16[8,128,1024]{2,1,0:T(8,128)(2,1)S(1)}, f32[8,128]{1,0:T(8,128)S(1)}, f32[32,16,128]{2,1,0:T(8,128)S(1)}) custom-call(s32[4]{0:T(128)S(1)} %pad_add_fusion.at_ref, bf16[64,1024]{1,0:T(8,128)(2,1)S(1)} %collective-permute-done.6.h0, ...), custom_call_target="tpu_custom_call", output_to_operand_aliasing={{0}: (4, {}), {1}: (5, {}), {2}: (6, {})} | custom-call | tf_op jit(solution)/shard_map/pallas_call | solution.py:23
  55.7 15.9 %all_to_all.35.e_ref = f32[32,16,128]{2,1,0:T(8,128)S(1)} all-to-all(f32[32,16,128]{2,1,0:T(8,128)S(1)} %get-tuple-element.60.mine_ref), channel_id=1, replica_groups=mesh['y'=4,'core'=2,'z'=8,'x'=4] {'z','x'}, dimensions={0} | all-to-all | bytes 524288 | tf_op jit(solution)/shard_map/all_to_all | solution.py:45
  72.4 18.2 %all_to_all.36.e_ref = f32[8,16,128]{2,1,0:T(8,128)S(1)} all-to-all(f32[8,16,128]{2,1,0:T(8,128)S(1)} %get-tuple-element.62), channel_id=1, replica_groups=mesh['y'=4,'core'=2,'z'=8,'x'=4] {'y','core'}, dimensions={0} | all-to-all | bytes 131072 | tf_op jit(solution)/shard_map/all_to_all | solution.py:45
  91.4 12.7 %all_to_all.37.e_ref = f32[32,8,128]{2,1,0:T(8,128)S(1)} all-to-all(f32[32,8,128]{2,1,0:T(8,128)S(1)} %shard_map.67), channel_id=1, replica_groups=mesh['y'=4,'core'=2,'z'=8,'x'=4] {'z','x'}, dimensions={0} | all-to-all | bytes 262144 | tf_op jit(solution)/shard_map/all_to_all | solution.py:45
  104.8 9.5 %all_to_all.38.e_ref = f32[8,16,128]{2,1,0:T(8,128)S(1)} all-to-all(f32[8,16,128]{2,1,0:T(8,128)S(1)} %shard_map.68), channel_id=1, replica_groups=mesh['y'=4,'core'=2,'z'=8,'x'=4] {'y','core'}, dimensions={0} | all-to-all | bytes 131072 | tf_op jit(solution)/shard_map/all_to_all | solution.py:45
  115.1 12.3 %all_to_all.39.e_ref = f32[32,8,128]{2,1,0:T(8,128)S(1)} all-to-all(f32[32,8,128]{2,1,0:T(8,128)S(1)} %shard_map.69), channel_id=1, replica_groups=mesh['y'=4,'core'=2,'z'=8,'x'=4] {'z','x'}, dimensions={0} | all-to-all | bytes 262144 | tf_op jit(solution)/shard_map/all_to_all | solution.py:45
  128.2 9.4 %all_to_all.40.e_ref = f32[8,16,128]{2,1,0:T(8,128)S(1)} all-to-all(f32[8,16,128]{2,1,0:T(8,128)S(1)} %shard_map.70), channel_id=1, replica_groups=mesh['y'=4,'core'=2,'z'=8,'x'=4] {'y','core'}, dimensions={0} | all-to-all | bytes 131072 | tf_op jit(solution)/shard_map/all_to_all | solution.py:45
  138.5 12.4 %all_to_all.41.e_ref = f32[32,8,128]{2,1,0:T(8,128)S(1)} all-to-all(f32[32,8,128]{2,1,0:T(8,128)S(1)} %get-tuple-element.64), channel_id=1, replica_groups=mesh['y'=4,'core'=2,'z'=8,'x'=4] {'z','x'}, dimensions={0} | all-to-all | bytes 262144 | tf_op jit(solution)/shard_map/all_to_all | solution.py:45
  153.5 2.3 %collective-permute-start.16 = (f32[128,2048]{1,0:T(8,128)S(1)}, f32[128,2048]{1,0:T(8,128)S(1)}, u32[]{:S(2)}, u32[]{:S(2)}) collective-permute-start(f32[128,2048]{1,0:T(8,128)S(1)} %shard_map.74), channel_id=1, source_target_pairs={{0,32},{32,0},{1,33},{33,1},{2,34},{34,2},{3,35},{35,3},{4,36},{36... | collective-permute-start | bytes 3145736 | tf_op jit(solution)/shard_map/ppermute | solution.py:36
  155.9 2.2 %collective-permute-done.12.other_ref = f32[24,128]{1,0:T(8,128)S(1)} collective-permute-done((f32[24,128]{1,0:T(8,128)S(1)}, f32[24,128]{1,0:T(8,128)S(1)}, u32[]{:S(2)}, u32[]{:S(2)}) %collective-permute-start.12) | collective-permute-done | bytes 12320 | tf_op jit(solution)/shard_map/ppermute | solution.py:36
  159.6 1.8 shard_map.77
  164.6 2.7 %collective-permute-start.15 = (f32[24,128]{1,0:T(8,128)S(1)}, f32[24,128]{1,0:T(8,128)S(1)}, u32[]{:S(2)}, u32[]{:S(2)}) collective-permute-start(f32[24,128]{1,0:T(8,128)S(1)} %collective-permute-done.13.near), channel_id=1, source_target_pairs={{0,32},{32,0},{1,33},{33,1},{2,34},{34,2},{3,35},{35,3},{4,36},{36... | collective-permute-start | bytes 36872 | tf_op jit(solution)/shard_map/ppermute | solution.py:36
  167.3 1.8 shard_map.73
  171.0 3.0 %collective-permute-start.23 = (f16[64,2048]{1,0:T(8,128)(2,1)S(1)}, f16[64,2048]{1,0:T(8,128)(2,1)S(1)}, u32[]{:S(2)}, u32[]{:S(2)}) collective-permute-start(f16[64,2048]{1,0:T(8,128)(2,1)S(1)} %get-tuple-element.91), channel_id=1, source_target_pairs={{0,192},{64,0},{128,64},{192,128},{1,193},{65,1},{129,65},{193,129... | collective-permute-start | bytes 786440 | tf_op jit(solution)/shard_map/ppermute | solution.py:36
  175.9 2.8 %collective-permute-start.18 = (f16[64,2048]{1,0:T(8,128)(2,1)S(1)}, f16[64,2048]{1,0:T(8,128)(2,1)S(1)}, u32[]{:S(2)}, u32[]{:S(2)}) collective-permute-start(f16[64,2048]{1,0:T(8,128)(2,1)S(1)} %fusion.4), channel_id=1, source_target_pairs={{0,192},{64,0},{128,64},{192,128},{1,193},{65,1},{129,65},{193,129... | collective-permute-start | bytes 786440 | tf_op jit(solution)/shard_map/ppermute | solution.py:36
  179.8 3.5 %collective-permute-start.24 = (f16[64,2048]{1,0:T(8,128)(2,1)S(1)}, f16[64,2048]{1,0:T(8,128)(2,1)S(1)}, u32[]{:S(2)}, u32[]{:S(2)}) collective-permute-start(f16[64,2048]{1,0:T(8,128)(2,1)S(1)} %multiply_convert_fusion), channel_id=1, source_target_pairs={{0,192},{64,0},{128,64},{192,128},{1,193},{65,1},{129,65},{193,129... | collective-permute-start | bytes 786440 | tf_op jit(solution)/shard_map/ppermute | solution.py:36
  183.7 7.2 %collective-permute-done.24 = f16[64,2048]{1,0:T(8,128)(2,1)S(1)} collective-permute-done((f16[64,2048]{1,0:T(8,128)(2,1)S(1)}, f16[64,2048]{1,0:T(8,128)(2,1)S(1)}, u32[]{:S(2)}, u32[]{:S(2)}) %collective-permute-start.24) | collective-permute-done | bytes 262176 | tf_op jit(solution)/shard_map/ppermute | solution.py:36
  190.9 3.1 %collective-permute-done.21 = f16[64,2048]{1,0:T(8,128)(2,1)S(1)} collective-permute-done((f16[64,2048]{1,0:T(8,128)(2,1)S(1)}, f16[64,2048]{1,0:T(8,128)(2,1)S(1)}, u32[]{:S(2)}, u32[]{:S(2)}) %collective-permute-start.21) | collective-permute-done | bytes 262176 | tf_op jit(solution)/shard_map/ppermute | solution.py:36
  (68 shorter events, 23.1 us)
Async XLA Ops:
  0.7 5.9 %collective-permute-start = (bf16[32,1024]{1,0:T(8,128)(2,1)}, bf16[32,1024]{1,0:T(8,128)(2,1)S(1)}, u32[]{:S(2)}, u32[]{:S(2)}) collective-permute-start(bf16[32,1024]{1,0:T(8,128)(2,1)} %bitcast.38), channel_id=1, source_target_pairs={{0,1},{1,2},{2,3},{3,0},{4,5},{5,6},{6,7},{7,4},{8,9},{9,10},{10,1... | collective-permute-start | bytes 196616 | tf_op jit(solution)/shard_map/ppermute | solution.py:36
  2.8 3.9 %collective-permute-start.1 = (bf16[32,1024]{1,0:T(8,128)(2,1)}, bf16[32,1024]{1,0:T(8,128)(2,1)S(1)}, u32[]{:S(2)}, u32[]{:S(2)}) collective-permute-start(bf16[32,1024]{1,0:T(8,128)(2,1)} %bitcast.39), channel_id=1, source_target_pairs={{0,3},{1,0},{2,1},{3,2},{4,7},{5,4},{6,5},{7,6},{8,11},{9,8},{10,9... | collective-permute-start | bytes 196616 | tf_op jit(solution)/shard_map/ppermute | solution.py:36
  4.1 4.9 %collective-permute-start.2 = (bf16[32,1024]{1,0:T(8,128)(2,1)}, bf16[32,1024]{1,0:T(8,128)(2,1)S(1)}, u32[]{:S(2)}, u32[]{:S(2)}) collective-permute-start(bf16[32,1024]{1,0:T(8,128)(2,1)} %bitcast.40), channel_id=1, source_target_pairs={{0,2},{1,3},{2,0},{3,1},{4,6},{5,7},{6,4},{7,5},{8,10},{9,11},{10,... | collective-permute-start | bytes 196616 | tf_op jit(solution)/shard_map/ppermute | solution.py:36
  5.8 0.9 copy-start.3
  9.1 9.0 %collective-permute-start.7 = (bf16[128,1024]{1,0:T(8,128)(2,1)S(1)}, bf16[128,1024]{1,0:T(8,128)(2,1)S(1)}, u32[]{:S(2)}, u32[]{:S(2)}) collective-permute-start(bf16[128,1024]{1,0:T(8,128)(2,1)S(1)} %shard_map.60.s_ref), channel_id=1, source_target_pairs={{0,28},{4,0},{8,4},{12,8},{16,12},{20,16},{24,20},{28,24},{1,29},{... | collective-permute-start | bytes 786440 | tf_op jit(solution)/shard_map/ppermute | solution.py:36
  14.7 6.4 %collective-permute-start.3 = (bf16[128,1024]{1,0:T(8,128)(2,1)S(1)}, bf16[128,1024]{1,0:T(8,128)(2,1)S(1)}, u32[]{:S(2)}, u32[]{:S(2)}) collective-permute-start(bf16[128,1024]{1,0:T(8,128)(2,1)S(1)} %shard_map.60.s_ref), channel_id=1, source_target_pairs={{0,4},{4,8},{8,12},{12,16},{16,20},{20,24},{24,28},{28,0},{1,5},{5... | collective-permute-start | bytes 786440 | tf_op jit(solution)/shard_map/ppermute | solution.py:36
  18.0 6.4 %collective-permute-start.8 = (bf16[128,1024]{1,0:T(8,128)(2,1)S(1)}, bf16[128,1024]{1,0:T(8,128)(2,1)S(1)}, u32[]{:S(2)}, u32[]{:S(2)}) collective-permute-start(bf16[128,1024]{1,0:T(8,128)(2,1)S(1)} %collective-permute-done.7.l), channel_id=1, source_target_pairs={{0,28},{4,0},{8,4},{12,8},{16,12},{20,16},{24,20},{28,24},{1,29},{... | collective-permute-start | bytes 786440 | tf_op jit(solution)/shard_map/ppermute | solution.py:36
  21.2 6.4 %collective-permute-start.4 = (bf16[128,1024]{1,0:T(8,128)(2,1)S(1)}, bf16[128,1024]{1,0:T(8,128)(2,1)S(1)}, u32[]{:S(2)}, u32[]{:S(2)}) collective-permute-start(bf16[128,1024]{1,0:T(8,128)(2,1)S(1)} %collective-permute-done.3.r), channel_id=1, source_target_pairs={{0,4},{4,8},{8,12},{12,16},{16,20},{20,24},{24,28},{28,0},{1,5},{5... | collective-permute-start | bytes 786440 | tf_op jit(solution)/shard_map/ppermute | solution.py:36
  24.5 6.8 %collective-permute-start.9 = (bf16[128,1024]{1,0:T(8,128)(2,1)S(1)}, bf16[128,1024]{1,0:T(8,128)(2,1)S(1)}, u32[]{:S(2)}, u32[]{:S(2)}) collective-permute-start(bf16[128,1024]{1,0:T(8,128)(2,1)S(1)} %collective-permute-done.8.l), channel_id=1, source_target_pairs={{0,28},{4,0},{8,4},{12,8},{16,12},{20,16},{24,20},{28,24},{1,29},{... | collective-permute-start | bytes 786440 | tf_op jit(solution)/shard_map/ppermute | solution.py:36
  27.6 7.1 %collective-permute-start.5 = (bf16[128,1024]{1,0:T(8,128)(2,1)S(1)}, bf16[128,1024]{1,0:T(8,128)(2,1)S(1)}, u32[]{:S(2)}, u32[]{:S(2)}) collective-permute-start(bf16[128,1024]{1,0:T(8,128)(2,1)S(1)} %collective-permute-done.4.r), channel_id=1, source_target_pairs={{0,4},{4,8},{8,12},{12,16},{16,20},{20,24},{24,28},{28,0},{1,5},{5... | collective-permute-start | bytes 786440 | tf_op jit(solution)/shard_map/ppermute | solution.py:36
  31.3 19.5 %collective-permute-start.10 = (bf16[64,1024]{1,0:T(8,128)(2,1)S(1)}, bf16[64,1024]{1,0:T(8,128)(2,1)S(1)}, u32[]{:S(2)}, u32[]{:S(2)}) collective-permute-start(bf16[64,1024]{1,0:T(8,128)(2,1)S(1)} %slice.121), channel_id=1, source_target_pairs={{0,28},{4,0},{8,4},{12,8},{16,12},{20,16},{24,20},{28,24},{1,29},{... | collective-permute-start | bytes 393224 | tf_op jit(solution)/shard_map/ppermute | solution.py:36
  34.7 16.1 %collective-permute-start.6 = (bf16[64,1024]{1,0:T(8,128)(2,1)S(1)}, bf16[64,1024]{1,0:T(8,128)(2,1)S(1)}, u32[]{:S(2)}, u32[]{:S(2)}) collective-permute-start(bf16[64,1024]{1,0:T(8,128)(2,1)S(1)} %slice.120), channel_id=1, source_target_pairs={{0,4},{4,8},{8,12},{12,16},{16,20},{20,24},{24,28},{28,0},{1,5},{5... | collective-permute-start | bytes 393224 | tf_op jit(solution)/shard_map/ppermute | solution.py:36
  35.0 2.2 %copy-start = (bf16[2048,1024]{1,0:T(8,128)(2,1)S(1)}, bf16[2048,1024]{1,0:T(8,128)(2,1)}, u32[]{:S(2)}) copy-start(bf16[2048,1024]{1,0:T(8,128)(2,1)} %c_ref.9) | copy-start | bytes 12582916
  50.8 20.8 %copy-start.2 = (f32[1024]{0:T(1024)S(1)}, f32[1024]{0:T(1024)}, u32[]{:S(2)}) copy-start(f32[1024]{0:T(1024)} %param.6) | copy-start | bytes 12292
  71.6 18.9 %copy-start.1 = (f32[2048]{0:T(1024)S(1)}, f32[2048]{0:T(1024)}, u32[]{:S(2)}) copy-start(f32[2048]{0:T(1024)} %param.7) | copy-start | bytes 24580
  153.5 5.9 %collective-permute-start.16 = (f32[128,2048]{1,0:T(8,128)S(1)}, f32[128,2048]{1,0:T(8,128)S(1)}, u32[]{:S(2)}, u32[]{:S(2)}) collective-permute-start(f32[128,2048]{1,0:T(8,128)S(1)} %shard_map.74), channel_id=1, source_target_pairs={{0,32},{32,0},{1,33},{33,1},{2,34},{34,2},{3,35},{35,3},{4,36},{36... | collective-permute-start | bytes 3145736 | tf_op jit(solution)/shard_map/ppermute | solution.py:36
  155.8 2.3 %collective-permute-start.12 = (f32[24,128]{1,0:T(8,128)S(1)}, f32[24,128]{1,0:T(8,128)S(1)}, u32[]{:S(2)}, u32[]{:S(2)}) collective-permute-start(f32[24,128]{1,0:T(8,128)S(1)} %get-tuple-element.71.mine_ref), channel_id=1, source_target_pairs={{0,32},{32,0},{1,33},{33,1},{2,34},{34,2},{3,35},{35,3},{4,36},{36... | collective-permute-start | bytes 36872 | tf_op jit(solution)/shard_map/ppermute | solution.py:36
  161.4 14.4 %collective-permute-start.17 = (f32[128,2048]{1,0:T(8,128)S(1)}, f32[128,2048]{1,0:T(8,128)S(1)}, u32[]{:S(2)}, u32[]{:S(2)}) collective-permute-start(f32[128,2048]{1,0:T(8,128)S(1)} %get-tuple-element.78), channel_id=1, source_target_pairs={{0,32},{32,0},{1,33},{33,1},{2,34},{34,2},{3,35},{35,3},{4,36},{36... | collective-permute-start | bytes 3145736 | tf_op jit(solution)/shard_map/ppermute | solution.py:36
  161.9 16.8 %collective-permute-start.19 = (f32[128,2048]{1,0:T(8,128)S(1)}, f32[128,2048]{1,0:T(8,128)S(1)}, u32[]{:S(2)}, u32[]{:S(2)}) collective-permute-start(f32[128,2048]{1,0:T(8,128)S(1)} %get-tuple-element.77), channel_id=1, source_target_pairs={{0,32},{32,0},{1,33},{33,1},{2,34},{34,2},{3,35},{35,3},{4,36},{36... | collective-permute-start | bytes 3145736 | tf_op jit(solution)/shard_map/ppermute | solution.py:36
  162.0 2.5 %collective-permute-start.13 = (f32[24,128]{1,0:T(8,128)S(1)}, f32[24,128]{1,0:T(8,128)S(1)}, u32[]{:S(2)}, u32[]{:S(2)}) collective-permute-start(f32[24,128]{1,0:T(8,128)S(1)} %get-tuple-element.72.m0), channel_id=1, source_target_pairs={{0,64},{64,128},{128,192},{192,0},{32,224},{96,32},{160,96},{224,1... | collective-permute-start | bytes 36872 | tf_op jit(solution)/shard_map/ppermute | solution.py:41
  164.6 4.7 %collective-permute-start.15 = (f32[24,128]{1,0:T(8,128)S(1)}, f32[24,128]{1,0:T(8,128)S(1)}, u32[]{:S(2)}, u32[]{:S(2)}) collective-permute-start(f32[24,128]{1,0:T(8,128)S(1)} %collective-permute-done.13.near), channel_id=1, source_target_pairs={{0,32},{32,0},{1,33},{33,1},{2,34},{34,2},{3,35},{35,3},{4,36},{36... | collective-permute-start | bytes 36872 | tf_op jit(solution)/shard_map/ppermute | solution.py:36
  167.3 2.5 %collective-permute-start.14 = (f32[24,128]{1,0:T(8,128)S(1)}, f32[24,128]{1,0:T(8,128)S(1)}, u32[]{:S(2)}, u32[]{:S(2)}) collective-permute-start(f32[24,128]{1,0:T(8,128)S(1)} %collective-permute-done.13.near), channel_id=1, source_target_pairs={{0,64},{64,128},{128,192},{192,0},{32,224},{96,32},{160,96},{224,1... | collective-permute-start | bytes 36872 | tf_op jit(solution)/shard_map/ppermute | solution.py:41
  169.1 14.4 %collective-permute-start.11 = (f32[128,2048]{1,0:T(8,128)S(1)}, f32[128,2048]{1,0:T(8,128)S(1)}, u32[]{:S(2)}, u32[]{:S(2)}) collective-permute-start(f32[128,2048]{1,0:T(8,128)S(1)} %get-tuple-element.69), channel_id=1, source_target_pairs={{0,32},{32,0},{1,33},{33,1},{2,34},{34,2},{3,35},{35,3},{4,36},{36... | collective-permute-start | bytes 3145736 | tf_op jit(solution)/shard_map/ppermute | solution.py:36
  171.0 8.6 %collective-permute-start.23 = (f16[64,2048]{1,0:T(8,128)(2,1)S(1)}, f16[64,2048]{1,0:T(8,128)(2,1)S(1)}, u32[]{:S(2)}, u32[]{:S(2)}) collective-permute-start(f16[64,2048]{1,0:T(8,128)(2,1)S(1)} %get-tuple-element.91), channel_id=1, source_target_pairs={{0,192},{64,0},{128,64},{192,128},{1,193},{65,1},{129,65},{193,129... | collective-permute-start | bytes 786440 | tf_op jit(solution)/shard_map/ppermute | solution.py:36
  174.0 9.3 %collective-permute-start.20 = (f16[64,2048]{1,0:T(8,128)(2,1)S(1)}, f16[64,2048]{1,0:T(8,128)(2,1)S(1)}, u32[]{:S(2)}, u32[]{:S(2)}) collective-permute-start(f16[64,2048]{1,0:T(8,128)(2,1)S(1)} %get-tuple-element.90), channel_id=1, source_target_pairs={{0,64},{64,128},{128,192},{192,0},{1,65},{65,129},{129,193},{193,1... | collective-permute-start | bytes 786440 | tf_op jit(solution)/shard_map/ppermute | solution.py:36
  175.9 18.1 %collective-permute-start.18 = (f16[64,2048]{1,0:T(8,128)(2,1)S(1)}, f16[64,2048]{1,0:T(8,128)(2,1)S(1)}, u32[]{:S(2)}, u32[]{:S(2)}) collective-permute-start(f16[64,2048]{1,0:T(8,128)(2,1)S(1)} %fusion.4), channel_id=1, source_target_pairs={{0,192},{64,0},{128,64},{192,128},{1,193},{65,1},{129,65},{193,129... | collective-permute-start | bytes 786440 | tf_op jit(solution)/shard_map/ppermute | solution.py:36
  178.8 15.2 %collective-permute-start.22 = (f16[64,2048]{1,0:T(8,128)(2,1)S(1)}, f16[64,2048]{1,0:T(8,128)(2,1)S(1)}, u32[]{:S(2)}, u32[]{:S(2)}) collective-permute-start(f16[64,2048]{1,0:T(8,128)(2,1)S(1)} %fusion.2), channel_id=1, source_target_pairs={{0,64},{64,128},{128,192},{192,0},{1,65},{65,129},{129,193},{193,1... | collective-permute-start | bytes 786440 | tf_op jit(solution)/shard_map/ppermute | solution.py:36
  179.8 11.1 %collective-permute-start.24 = (f16[64,2048]{1,0:T(8,128)(2,1)S(1)}, f16[64,2048]{1,0:T(8,128)(2,1)S(1)}, u32[]{:S(2)}, u32[]{:S(2)}) collective-permute-start(f16[64,2048]{1,0:T(8,128)(2,1)S(1)} %multiply_convert_fusion), channel_id=1, source_target_pairs={{0,192},{64,0},{128,64},{192,128},{1,193},{65,1},{129,65},{193,129... | collective-permute-start | bytes 786440 | tf_op jit(solution)/shard_map/ppermute | solution.py:36
  183.4 10.6 %collective-permute-start.21 = (f16[64,2048]{1,0:T(8,128)(2,1)S(1)}, f16[64,2048]{1,0:T(8,128)(2,1)S(1)}, u32[]{:S(2)}, u32[]{:S(2)}) collective-permute-start(f16[64,2048]{1,0:T(8,128)(2,1)S(1)} %multiply_convert_fusion.1), channel_id=1, source_target_pairs={{0,64},{64,128},{128,192},{192,0},{1,65},{65,129},{129,193},{193,1... | collective-permute-start | bytes 786440 | tf_op jit(solution)/shard_map/ppermute | solution.py:36

commit v6 on v5

--- a/solution.py
+++ b/solution.py
@@ -171,12 +171,13 @@
     acc_ref = refs[-1]
     if len(refs) > 1:
         refs[0][...] = scale
+    small = scale * 2.0**-12
 
     def block(b, carry):
         rows = pl.ds(pl.multiple_of(128 * b, 128), 128)
         acc = jnp.zeros((128, 128), F32)
         for t in range(CB):
-            acc = acc + k_ref[rows, 128 * t : 128 * t + 128] * scale[t : t + 1]
+            acc = acc + k_ref[rows, 128 * t : 128 * t + 128] * small[t : t + 1]
         acc_ref[rows, :] = acc
         return carry
 
@@ -184,7 +185,7 @@
     lines = [
         jnp.sum(acc_ref[128 * b : 128 * b + 128, :].T, axis=0, keepdims=True) for b in range(RB)
     ]
-    y = jnp.concatenate(lines, axis=0) * f_ref[...]
+    y = jnp.concatenate(lines, axis=0) * (f_ref[...] * 2.0**12)
     o_ref[...] = jnp.broadcast_to(y[None], o_ref.shape)
 
 
@@ -213,11 +214,11 @@
 
 
 def limits(at_ref, m, by):
-    return m[0:CB, :] * m[pl.ds(CB + target(at_ref, by, 0), 1), :]
+    return jnp.maximum(m[0:CB, :] * m[pl.ds(CB + target(at_ref, by, 0), 1), :], 2.0**-100)
 
 
 def inverse(q):
-    return jnp.where(q > 0, 32768.0 / jnp.where(q > 0, q, 1.0), 0.0)
+    return 32768.0 / q
 
 
 def chip_body(at_ref, ft_ref, w_ref, mine_ref, other_ref, o_ref, m_ref, i_ref):

time: 196 us -> 196 us (level)
  no operation moved by 1% of the time
where the time goes in v6:
time: 196 us; the launch traced here: 195 us
  blocking collectives  90.4 us (46%)
  starting transfers between devices  36.5 us (19%)
  Pallas kernels  34.3 us (17%)
  waiting for transfers between devices  27.9 us (14%)
  local copies, waits for them, and re-layouts  3.1 us (2%)
  other arithmetic  2.19 us (1%)
    all_to_all x7, blocking collectives, everyone(): return lax.all_to_all(x, axis, 0, 0, tiled=True)  90.4 us
    ppermute x23, starting transfers between devices, step(): return lax.ppermute(x, axis, [(i, (i + by) % n) for i in range(n)])  35.6 us
    pallas_call x21, Pallas kernels, call(): pl.pallas_call(body, out_shape=[jax.ShapeDtypeStruct(s, d) for s, d in ou...  34.3 us
    ppermute x23, waiting for transfers between devices, step(): return lax.ppermute(x, axis, [(i, (i + by) % n) for i in range(n)])  26.2 us
  transfers between devices with their start and end apart: 25, of which 10 were waited for; matrix products, arithmetic and copies ran while one was open for 0% of the time, Pallas kernels for 10%

profile of v6, /device:TPU:1, one launch (start us, length us, event | category | flops | bytes accessed | tf_op | source)
XLA Modules:
  0.0 195.4 jit_solution(13284176369258485777)
XLA Ops:
  0.7 2.0 %collective-permute-start = (bf16[32,1024]{1,0:T(8,128)(2,1)}, bf16[32,1024]{1,0:T(8,128)(2,1)S(1)}, u32[]{:S(2)}, u32[]{:S(2)}) collective-permute-start(bf16[32,1024]{1,0:T(8,128)(2,1)} %bitcast.38), channel_id=1, source_target_pairs={{0,1},{1,2},{2,3},{3,0},{4,5},{5,6},{6,7},{7,4},{8,9},{9,10},{10,1... | collective-permute-start | bytes 196616 | tf_op jit(solution)/shard_map/ppermute | solution.py:36
  6.7 2.4 %collective-permute-done.2.d_ref = bf16[32,1024]{1,0:T(8,128)(2,1)S(1)} collective-permute-done((bf16[32,1024]{1,0:T(8,128)(2,1)}, bf16[32,1024]{1,0:T(8,128)(2,1)S(1)}, u32[]{:S(2)}, u32[]{:S(2)}) %collective-permute-start.2) | collective-permute-done | bytes 65568 | tf_op jit(solution)/shard_map/ppermute | solution.py:36
  9.1 5.7 %collective-permute-start.7 = (bf16[128,1024]{1,0:T(8,128)(2,1)S(1)}, bf16[128,1024]{1,0:T(8,128)(2,1)S(1)}, u32[]{:S(2)}, u32[]{:S(2)}) collective-permute-start(bf16[128,1024]{1,0:T(8,128)(2,1)S(1)} %shard_map.60.s_ref), channel_id=1, source_target_pairs={{0,28},{4,0},{8,4},{12,8},{16,12},{20,16},{24,20},{28,24},{1,29},{... | collective-permute-start | bytes 786440 | tf_op jit(solution)/shard_map/ppermute | solution.py:36
  14.7 3.3 %collective-permute-done.7.l = bf16[128,1024]{1,0:T(8,128)(2,1)S(1)} collective-permute-done((bf16[128,1024]{1,0:T(8,128)(2,1)S(1)}, bf16[128,1024]{1,0:T(8,128)(2,1)S(1)}, u32[]{:S(2)}, u32[]{:S(2)}) %collective-permute-start.7) | collective-permute-done | bytes 262176 | tf_op jit(solution)/shard_map/ppermute | solution.py:36
  18.0 3.1 %collective-permute-start.8 = (bf16[128,1024]{1,0:T(8,128)(2,1)S(1)}, bf16[128,1024]{1,0:T(8,128)(2,1)S(1)}, u32[]{:S(2)}, u32[]{:S(2)}) collective-permute-start(bf16[128,1024]{1,0:T(8,128)(2,1)S(1)} %collective-permute-done.7.l), channel_id=1, source_target_pairs={{0,28},{4,0},{8,4},{12,8},{16,12},{20,16},{24,20},{28,24},{1,29},{... | collective-permute-start | bytes 786440 | tf_op jit(solution)/shard_map/ppermute | solution.py:36
  21.2 3.3 %collective-permute-done.8.l = bf16[128,1024]{1,0:T(8,128)(2,1)S(1)} collective-permute-done((bf16[128,1024]{1,0:T(8,128)(2,1)S(1)}, bf16[128,1024]{1,0:T(8,128)(2,1)S(1)}, u32[]{:S(2)}, u32[]{:S(2)}) %collective-permute-start.8) | collective-permute-done | bytes 262176 | tf_op jit(solution)/shard_map/ppermute | solution.py:36
  24.5 3.1 %collective-permute-start.9 = (bf16[128,1024]{1,0:T(8,128)(2,1)S(1)}, bf16[128,1024]{1,0:T(8,128)(2,1)S(1)}, u32[]{:S(2)}, u32[]{:S(2)}) collective-permute-start(bf16[128,1024]{1,0:T(8,128)(2,1)S(1)} %collective-permute-done.8.l), channel_id=1, source_target_pairs={{0,28},{4,0},{8,4},{12,8},{16,12},{20,16},{24,20},{28,24},{1,29},{... | collective-permute-start | bytes 786440 | tf_op jit(solution)/shard_map/ppermute | solution.py:36
  27.6 3.7 %collective-permute-done.9.l = bf16[128,1024]{1,0:T(8,128)(2,1)S(1)} collective-permute-done((bf16[128,1024]{1,0:T(8,128)(2,1)S(1)}, bf16[128,1024]{1,0:T(8,128)(2,1)S(1)}, u32[]{:S(2)}, u32[]{:S(2)}) %collective-permute-start.9) | collective-permute-done | bytes 262176 | tf_op jit(solution)/shard_map/ppermute | solution.py:36
  31.3 3.2 %collective-permute-start.10 = (bf16[64,1024]{1,0:T(8,128)(2,1)S(1)}, bf16[64,1024]{1,0:T(8,128)(2,1)S(1)}, u32[]{:S(2)}, u32[]{:S(2)}) collective-permute-start(bf16[64,1024]{1,0:T(8,128)(2,1)S(1)} %slice.121), channel_id=1, source_target_pairs={{0,28},{4,0},{8,4},{12,8},{16,12},{20,16},{24,20},{28,24},{1,29},{... | collective-permute-start | bytes 393224 | tf_op jit(solution)/shard_map/ppermute | solution.py:36
  35.0 2.2 %copy-done = bf16[2048,1024]{1,0:T(8,128)(2,1)S(1)} copy-done((bf16[2048,1024]{1,0:T(8,128)(2,1)S(1)}, bf16[2048,1024]{1,0:T(8,128)(2,1)}, u32[]{:S(2)}) %copy-start) | copy-done | bytes 4194328
  37.2 2.6 %shard_map.61 = (f32[1024,2048]{1,0:T(8,128)S(1)}, bf16[8,128,1024]{2,1,0:T(8,128)(2,1)S(1)}, f32[8,128]{1,0:T(8,128)S(1)}) custom-call(s32[4]{0:T(128)S(1)} %pad_add_fusion.at_ref, bf16[128,1024]{1,0:T(8,128)(2,1)S(1)} %shard_map.60.s_ref, bf16[2048,1024]{1,0:T(8,128)(2,1)S(1)} %copy-done), custom_call_target="tpu_custom_call" | custom-call | tf_op jit(solution)/shard_map/pallas_call | solution.py:23
  39.8 3.7 %shard_map.62 = (f32[1024,2048]{1,0:T(8,128)S(1)}, bf16[8,128,1024]{2,1,0:T(8,128)(2,1)S(1)}, f32[8,128]{1,0:T(8,128)S(1)}) custom-call(s32[4]{0:T(128)S(1)} %pad_add_fusion.at_ref, bf16[128,1024]{1,0:T(8,128)(2,1)S(1)} %collective-permute-done.7.l, ...), custom_call_target="tpu_custom_call", output_to_operand_aliasing={{0}: (4, {}), {1}: (5, {}), {2}: (6, {})} | custom-call | tf_op jit(solution)/shard_map/pallas_call | solution.py:23
  43.4 3.7 %shard_map.63 = (f32[1024,2048]{1,0:T(8,128)S(1)}, bf16[8,128,1024]{2,1,0:T(8,128)(2,1)S(1)}, f32[8,128]{1,0:T(8,128)S(1)}) custom-call(s32[4]{0:T(128)S(1)} %pad_add_fusion.at_ref, bf16[128,1024]{1,0:T(8,128)(2,1)S(1)} %collective-permute-done.8.l, ...), custom_call_target="tpu_custom_call", output_to_operand_aliasing={{0}: (4, {}), {1}: (5, {}), {2}: (6, {})} | custom-call | tf_op jit(solution)/shard_map/pallas_call | solution.py:23
  47.1 3.7 %shard_map.64 = (f32[1024,2048]{1,0:T(8,128)S(1)}, bf16[8,128,1024]{2,1,0:T(8,128)(2,1)S(1)}, f32[8,128]{1,0:T(8,128)S(1)}) custom-call(s32[4]{0:T(128)S(1)} %pad_add_fusion.at_ref, bf16[128,1024]{1,0:T(8,128)(2,1)S(1)} %collective-permute-done.9.l, ...), custom_call_target="tpu_custom_call", output_to_operand_aliasing={{0}: (4, {}), {1}: (5, {}), {2}: (6, {})} | custom-call | tf_op jit(solution)/shard_map/pallas_call | solution.py:23
  50.8 4.8 %shard_map.65 = (f32[1024,2048]{1,0:T(8,128)S(1)}, bf16[8,128,1024]{2,1,0:T(8,128)(2,1)S(1)}, f32[8,128]{1,0:T(8,128)S(1)}, f32[32,16,128]{2,1,0:T(8,128)S(1)}) custom-call(s32[4]{0:T(128)S(1)} %pad_add_fusion.at_ref, bf16[64,1024]{1,0:T(8,128)(2,1)S(1)} %collective-permute-done.6.h0, ...), custom_call_target="tpu_custom_call", output_to_operand_aliasing={{0}: (4, {}), {1}: (5, {}), {2}: (6, {})} | custom-call | tf_op jit(solution)/shard_map/pallas_call | solution.py:23
  55.7 15.9 %all_to_all.35.e_ref = f32[32,16,128]{2,1,0:T(8,128)S(1)} all-to-all(f32[32,16,128]{2,1,0:T(8,128)S(1)} %get-tuple-element.60.mine_ref), channel_id=1, replica_groups=mesh['y'=4,'core'=2,'z'=8,'x'=4] {'z','x'}, dimensions={0} | all-to-all | bytes 524288 | tf_op jit(solution)/shard_map/all_to_all | solution.py:45
  72.4 18.2 %all_to_all.36.e_ref = f32[8,16,128]{2,1,0:T(8,128)S(1)} all-to-all(f32[8,16,128]{2,1,0:T(8,128)S(1)} %get-tuple-element.62), channel_id=1, replica_groups=mesh['y'=4,'core'=2,'z'=8,'x'=4] {'y','core'}, dimensions={0} | all-to-all | bytes 131072 | tf_op jit(solution)/shard_map/all_to_all | solution.py:45
  91.4 12.7 %all_to_all.37.e_ref = f32[32,8,128]{2,1,0:T(8,128)S(1)} all-to-all(f32[32,8,128]{2,1,0:T(8,128)S(1)} %shard_map.67), channel_id=1, replica_groups=mesh['y'=4,'core'=2,'z'=8,'x'=4] {'z','x'}, dimensions={0} | all-to-all | bytes 262144 | tf_op jit(solution)/shard_map/all_to_all | solution.py:45
  104.8 9.5 %all_to_all.38.e_ref = f32[8,16,128]{2,1,0:T(8,128)S(1)} all-to-all(f32[8,16,128]{2,1,0:T(8,128)S(1)} %shard_map.68), channel_id=1, replica_groups=mesh['y'=4,'core'=2,'z'=8,'x'=4] {'y','core'}, dimensions={0} | all-to-all | bytes 131072 | tf_op jit(solution)/shard_map/all_to_all | solution.py:45
  115.1 12.3 %all_to_all.39.e_ref = f32[32,8,128]{2,1,0:T(8,128)S(1)} all-to-all(f32[32,8,128]{2,1,0:T(8,128)S(1)} %shard_map.69), channel_id=1, replica_groups=mesh['y'=4,'core'=2,'z'=8,'x'=4] {'z','x'}, dimensions={0} | all-to-all | bytes 262144 | tf_op jit(solution)/shard_map/all_to_all | solution.py:45
  128.2 9.4 %all_to_all.40.e_ref = f32[8,16,128]{2,1,0:T(8,128)S(1)} all-to-all(f32[8,16,128]{2,1,0:T(8,128)S(1)} %shard_map.70), channel_id=1, replica_groups=mesh['y'=4,'core'=2,'z'=8,'x'=4] {'y','core'}, dimensions={0} | all-to-all | bytes 131072 | tf_op jit(solution)/shard_map/all_to_all | solution.py:45
  138.5 12.4 %all_to_all.41.e_ref = f32[32,8,128]{2,1,0:T(8,128)S(1)} all-to-all(f32[32,8,128]{2,1,0:T(8,128)S(1)} %get-tuple-element.64), channel_id=1, replica_groups=mesh['y'=4,'core'=2,'z'=8,'x'=4] {'z','x'}, dimensions={0} | all-to-all | bytes 262144 | tf_op jit(solution)/shard_map/all_to_all | solution.py:45
  153.5 2.3 %collective-permute-start.16 = (f32[128,2048]{1,0:T(8,128)S(1)}, f32[128,2048]{1,0:T(8,128)S(1)}, u32[]{:S(2)}, u32[]{:S(2)}) collective-permute-start(f32[128,2048]{1,0:T(8,128)S(1)} %shard_map.74), channel_id=1, source_target_pairs={{0,32},{32,0},{1,33},{33,1},{2,34},{34,2},{3,35},{35,3},{4,36},{36... | collective-permute-start | bytes 3145736 | tf_op jit(solution)/shard_map/ppermute | solution.py:36
  155.9 2.2 %collective-permute-done.12.other_ref = f32[24,128]{1,0:T(8,128)S(1)} collective-permute-done((f32[24,128]{1,0:T(8,128)S(1)}, f32[24,128]{1,0:T(8,128)S(1)}, u32[]{:S(2)}, u32[]{:S(2)}) %collective-permute-start.12) | collective-permute-done | bytes 12320 | tf_op jit(solution)/shard_map/ppermute | solution.py:36
  159.6 1.8 shard_map.77
  164.6 2.7 %collective-permute-start.15 = (f32[24,128]{1,0:T(8,128)S(1)}, f32[24,128]{1,0:T(8,128)S(1)}, u32[]{:S(2)}, u32[]{:S(2)}) collective-permute-start(f32[24,128]{1,0:T(8,128)S(1)} %collective-permute-done.13.near), channel_id=1, source_target_pairs={{0,32},{32,0},{1,33},{33,1},{2,34},{34,2},{3,35},{35,3},{4,36},{36... | collective-permute-start | bytes 36872 | tf_op jit(solution)/shard_map/ppermute | solution.py:36
  167.3 1.8 shard_map.73
  171.0 3.0 %collective-permute-start.23 = (f16[64,2048]{1,0:T(8,128)(2,1)S(1)}, f16[64,2048]{1,0:T(8,128)(2,1)S(1)}, u32[]{:S(2)}, u32[]{:S(2)}) collective-permute-start(f16[64,2048]{1,0:T(8,128)(2,1)S(1)} %get-tuple-element.91), channel_id=1, source_target_pairs={{0,192},{64,0},{128,64},{192,128},{1,193},{65,1},{129,65},{193,129... | collective-permute-start | bytes 786440 | tf_op jit(solution)/shard_map/ppermute | solution.py:36
  175.9 2.8 %collective-permute-start.18 = (f16[64,2048]{1,0:T(8,128)(2,1)S(1)}, f16[64,2048]{1,0:T(8,128)(2,1)S(1)}, u32[]{:S(2)}, u32[]{:S(2)}) collective-permute-start(f16[64,2048]{1,0:T(8,128)(2,1)S(1)} %fusion.4), channel_id=1, source_target_pairs={{0,192},{64,0},{128,64},{192,128},{1,193},{65,1},{129,65},{193,129... | collective-permute-start | bytes 786440 | tf_op jit(solution)/shard_map/ppermute | solution.py:36
  179.8 3.5 %collective-permute-start.24 = (f16[64,2048]{1,0:T(8,128)(2,1)S(1)}, f16[64,2048]{1,0:T(8,128)(2,1)S(1)}, u32[]{:S(2)}, u32[]{:S(2)}) collective-permute-start(f16[64,2048]{1,0:T(8,128)(2,1)S(1)} %multiply_convert_fusion), channel_id=1, source_target_pairs={{0,192},{64,0},{128,64},{192,128},{1,193},{65,1},{129,65},{193,129... | collective-permute-start | bytes 786440 | tf_op jit(solution)/shard_map/ppermute | solution.py:36
  183.7 7.2 %collective-permute-done.24 = f16[64,2048]{1,0:T(8,128)(2,1)S(1)} collective-permute-done((f16[64,2048]{1,0:T(8,128)(2,1)S(1)}, f16[64,2048]{1,0:T(8,128)(2,1)S(1)}, u32[]{:S(2)}, u32[]{:S(2)}) %collective-permute-start.24) | collective-permute-done | bytes 262176 | tf_op jit(solution)/shard_map/ppermute | solution.py:36
  190.9 3.1 %collective-permute-done.21 = f16[64,2048]{1,0:T(8,128)(2,1)S(1)} collective-permute-done((f16[64,2048]{1,0:T(8,128)(2,1)S(1)}, f16[64,2048]{1,0:T(8,128)(2,1)S(1)}, u32[]{:S(2)}, u32[]{:S(2)}) %collective-permute-start.21) | collective-permute-done | bytes 262176 | tf_op jit(solution)/shard_map/ppermute | solution.py:36
  (68 shorter events, 23.1 us)
Async XLA Ops:
  0.7 5.9 %collective-permute-start = (bf16[32,1024]{1,0:T(8,128)(2,1)}, bf16[32,1024]{1,0:T(8,128)(2,1)S(1)}, u32[]{:S(2)}, u32[]{:S(2)}) collective-permute-start(bf16[32,1024]{1,0:T(8,128)(2,1)} %bitcast.38), channel_id=1, source_target_pairs={{0,1},{1,2},{2,3},{3,0},{4,5},{5,6},{6,7},{7,4},{8,9},{9,10},{10,1... | collective-permute-start | bytes 196616 | tf_op jit(solution)/shard_map/ppermute | solution.py:36
  2.8 3.9 %collective-permute-start.1 = (bf16[32,1024]{1,0:T(8,128)(2,1)}, bf16[32,1024]{1,0:T(8,128)(2,1)S(1)}, u32[]{:S(2)}, u32[]{:S(2)}) collective-permute-start(bf16[32,1024]{1,0:T(8,128)(2,1)} %bitcast.39), channel_id=1, source_target_pairs={{0,3},{1,0},{2,1},{3,2},{4,7},{5,4},{6,5},{7,6},{8,11},{9,8},{10,9... | collective-permute-start | bytes 196616 | tf_op jit(solution)/shard_map/ppermute | solution.py:36
  4.1 4.9 %collective-permute-start.2 = (bf16[32,1024]{1,0:T(8,128)(2,1)}, bf16[32,1024]{1,0:T(8,128)(2,1)S(1)}, u32[]{:S(2)}, u32[]{:S(2)}) collective-permute-start(bf16[32,1024]{1,0:T(8,128)(2,1)} %bitcast.40), channel_id=1, source_target_pairs={{0,2},{1,3},{2,0},{3,1},{4,6},{5,7},{6,4},{7,5},{8,10},{9,11},{10,... | collective-permute-start | bytes 196616 | tf_op jit(solution)/shard_map/ppermute | solution.py:36
  5.8 0.9 copy-start.3
  9.1 9.0 %collective-permute-start.7 = (bf16[128,1024]{1,0:T(8,128)(2,1)S(1)}, bf16[128,1024]{1,0:T(8,128)(2,1)S(1)}, u32[]{:S(2)}, u32[]{:S(2)}) collective-permute-start(bf16[128,1024]{1,0:T(8,128)(2,1)S(1)} %shard_map.60.s_ref), channel_id=1, source_target_pairs={{0,28},{4,0},{8,4},{12,8},{16,12},{20,16},{24,20},{28,24},{1,29},{... | collective-permute-start | bytes 786440 | tf_op jit(solution)/shard_map/ppermute | solution.py:36
  14.7 6.4 %collective-permute-start.3 = (bf16[128,1024]{1,0:T(8,128)(2,1)S(1)}, bf16[128,1024]{1,0:T(8,128)(2,1)S(1)}, u32[]{:S(2)}, u32[]{:S(2)}) collective-permute-start(bf16[128,1024]{1,0:T(8,128)(2,1)S(1)} %shard_map.60.s_ref), channel_id=1, source_target_pairs={{0,4},{4,8},{8,12},{12,16},{16,20},{20,24},{24,28},{28,0},{1,5},{5... | collective-permute-start | bytes 786440 | tf_op jit(solution)/shard_map/ppermute | solution.py:36
  18.0 6.4 %collective-permute-start.8 = (bf16[128,1024]{1,0:T(8,128)(2,1)S(1)}, bf16[128,1024]{1,0:T(8,128)(2,1)S(1)}, u32[]{:S(2)}, u32[]{:S(2)}) collective-permute-start(bf16[128,1024]{1,0:T(8,128)(2,1)S(1)} %collective-permute-done.7.l), channel_id=1, source_target_pairs={{0,28},{4,0},{8,4},{12,8},{16,12},{20,16},{24,20},{28,24},{1,29},{... | collective-permute-start | bytes 786440 | tf_op jit(solution)/shard_map/ppermute | solution.py:36
  21.2 6.4 %collective-permute-start.4 = (bf16[128,1024]{1,0:T(8,128)(2,1)S(1)}, bf16[128,1024]{1,0:T(8,128)(2,1)S(1)}, u32[]{:S(2)}, u32[]{:S(2)}) collective-permute-start(bf16[128,1024]{1,0:T(8,128)(2,1)S(1)} %collective-permute-done.3.r), channel_id=1, source_target_pairs={{0,4},{4,8},{8,12},{12,16},{16,20},{20,24},{24,28},{28,0},{1,5},{5... | collective-permute-start | bytes 786440 | tf_op jit(solution)/shard_map/ppermute | solution.py:36
  24.5 6.8 %collective-permute-start.9 = (bf16[128,1024]{1,0:T(8,128)(2,1)S(1)}, bf16[128,1024]{1,0:T(8,128)(2,1)S(1)}, u32[]{:S(2)}, u32[]{:S(2)}) collective-permute-start(bf16[128,1024]{1,0:T(8,128)(2,1)S(1)} %collective-permute-done.8.l), channel_id=1, source_target_pairs={{0,28},{4,0},{8,4},{12,8},{16,12},{20,16},{24,20},{28,24},{1,29},{... | collective-permute-start | bytes 786440 | tf_op jit(solution)/shard_map/ppermute | solution.py:36
  27.6 7.1 %collective-permute-start.5 = (bf16[128,1024]{1,0:T(8,128)(2,1)S(1)}, bf16[128,1024]{1,0:T(8,128)(2,1)S(1)}, u32[]{:S(2)}, u32[]{:S(2)}) collective-permute-start(bf16[128,1024]{1,0:T(8,128)(2,1)S(1)} %collective-permute-done.4.r), channel_id=1, source_target_pairs={{0,4},{4,8},{8,12},{12,16},{16,20},{20,24},{24,28},{28,0},{1,5},{5... | collective-permute-start | bytes 786440 | tf_op jit(solution)/shard_map/ppermute | solution.py:36
  31.3 19.5 %collective-permute-start.10 = (bf16[64,1024]{1,0:T(8,128)(2,1)S(1)}, bf16[64,1024]{1,0:T(8,128)(2,1)S(1)}, u32[]{:S(2)}, u32[]{:S(2)}) collective-permute-start(bf16[64,1024]{1,0:T(8,128)(2,1)S(1)} %slice.121), channel_id=1, source_target_pairs={{0,28},{4,0},{8,4},{12,8},{16,12},{20,16},{24,20},{28,24},{1,29},{... | collective-permute-start | bytes 393224 | tf_op jit(solution)/shard_map/ppermute | solution.py:36
  34.7 16.1 %collective-permute-start.6 = (bf16[64,1024]{1,0:T(8,128)(2,1)S(1)}, bf16[64,1024]{1,0:T(8,128)(2,1)S(1)}, u32[]{:S(2)}, u32[]{:S(2)}) collective-permute-start(bf16[64,1024]{1,0:T(8,128)(2,1)S(1)} %slice.120), channel_id=1, source_target_pairs={{0,4},{4,8},{8,12},{12,16},{16,20},{20,24},{24,28},{28,0},{1,5},{5... | collective-permute-start | bytes 393224 | tf_op jit(solution)/shard_map/ppermute | solution.py:36
  35.0 2.2 %copy-start = (bf16[2048,1024]{1,0:T(8,128)(2,1)S(1)}, bf16[2048,1024]{1,0:T(8,128)(2,1)}, u32[]{:S(2)}) copy-start(bf16[2048,1024]{1,0:T(8,128)(2,1)} %c_ref.9) | copy-start | bytes 12582916
  50.8 20.8 %copy-start.2 = (f32[1024]{0:T(1024)S(1)}, f32[1024]{0:T(1024)}, u32[]{:S(2)}) copy-start(f32[1024]{0:T(1024)} %param.6) | copy-start | bytes 12292
  71.6 18.9 %copy-start.1 = (f32[2048]{0:T(1024)S(1)}, f32[2048]{0:T(1024)}, u32[]{:S(2)}) copy-start(f32[2048]{0:T(1024)} %param.7) | copy-start | bytes 24580
  153.5 5.9 %collective-permute-start.16 = (f32[128,2048]{1,0:T(8,128)S(1)}, f32[128,2048]{1,0:T(8,128)S(1)}, u32[]{:S(2)}, u32[]{:S(2)}) collective-permute-start(f32[128,2048]{1,0:T(8,128)S(1)} %shard_map.74), channel_id=1, source_target_pairs={{0,32},{32,0},{1,33},{33,1},{2,34},{34,2},{3,35},{35,3},{4,36},{36... | collective-permute-start | bytes 3145736 | tf_op jit(solution)/shard_map/ppermute | solution.py:36
  155.8 2.3 %collective-permute-start.12 = (f32[24,128]{1,0:T(8,128)S(1)}, f32[24,128]{1,0:T(8,128)S(1)}, u32[]{:S(2)}, u32[]{:S(2)}) collective-permute-start(f32[24,128]{1,0:T(8,128)S(1)} %get-tuple-element.71.mine_ref), channel_id=1, source_target_pairs={{0,32},{32,0},{1,33},{33,1},{2,34},{34,2},{3,35},{35,3},{4,36},{36... | collective-permute-start | bytes 36872 | tf_op jit(solution)/shard_map/ppermute | solution.py:36
  161.4 14.4 %collective-permute-start.17 = (f32[128,2048]{1,0:T(8,128)S(1)}, f32[128,2048]{1,0:T(8,128)S(1)}, u32[]{:S(2)}, u32[]{:S(2)}) collective-permute-start(f32[128,2048]{1,0:T(8,128)S(1)} %get-tuple-element.78), channel_id=1, source_target_pairs={{0,32},{32,0},{1,33},{33,1},{2,34},{34,2},{3,35},{35,3},{4,36},{36... | collective-permute-start | bytes 3145736 | tf_op jit(solution)/shard_map/ppermute | solution.py:36
  161.9 16.8 %collective-permute-start.19 = (f32[128,2048]{1,0:T(8,128)S(1)}, f32[128,2048]{1,0:T(8,128)S(1)}, u32[]{:S(2)}, u32[]{:S(2)}) collective-permute-start(f32[128,2048]{1,0:T(8,128)S(1)} %get-tuple-element.77), channel_id=1, source_target_pairs={{0,32},{32,0},{1,33},{33,1},{2,34},{34,2},{3,35},{35,3},{4,36},{36... | collective-permute-start | bytes 3145736 | tf_op jit(solution)/shard_map/ppermute | solution.py:36
  162.0 2.5 %collective-permute-start.13 = (f32[24,128]{1,0:T(8,128)S(1)}, f32[24,128]{1,0:T(8,128)S(1)}, u32[]{:S(2)}, u32[]{:S(2)}) collective-permute-start(f32[24,128]{1,0:T(8,128)S(1)} %get-tuple-element.72.m0), channel_id=1, source_target_pairs={{0,64},{64,128},{128,192},{192,0},{32,224},{96,32},{160,96},{224,1... | collective-permute-start | bytes 36872 | tf_op jit(solution)/shard_map/ppermute | solution.py:41
  164.6 4.7 %collective-permute-start.15 = (f32[24,128]{1,0:T(8,128)S(1)}, f32[24,128]{1,0:T(8,128)S(1)}, u32[]{:S(2)}, u32[]{:S(2)}) collective-permute-start(f32[24,128]{1,0:T(8,128)S(1)} %collective-permute-done.13.near), channel_id=1, source_target_pairs={{0,32},{32,0},{1,33},{33,1},{2,34},{34,2},{3,35},{35,3},{4,36},{36... | collective-permute-start | bytes 36872 | tf_op jit(solution)/shard_map/ppermute | solution.py:36
  167.3 2.5 %collective-permute-start.14 = (f32[24,128]{1,0:T(8,128)S(1)}, f32[24,128]{1,0:T(8,128)S(1)}, u32[]{:S(2)}, u32[]{:S(2)}) collective-permute-start(f32[24,128]{1,0:T(8,128)S(1)} %collective-permute-done.13.near), channel_id=1, source_target_pairs={{0,64},{64,128},{128,192},{192,0},{32,224},{96,32},{160,96},{224,1... | collective-permute-start | bytes 36872 | tf_op jit(solution)/shard_map/ppermute | solution.py:41
  169.1 14.4 %collective-permute-start.11 = (f32[128,2048]{1,0:T(8,128)S(1)}, f32[128,2048]{1,0:T(8,128)S(1)}, u32[]{:S(2)}, u32[]{:S(2)}) collective-permute-start(f32[128,2048]{1,0:T(8,128)S(1)} %get-tuple-element.69), channel_id=1, source_target_pairs={{0,32},{32,0},{1,33},{33,1},{2,34},{34,2},{3,35},{35,3},{4,36},{36... | collective-permute-start | bytes 3145736 | tf_op jit(solution)/shard_map/ppermute | solution.py:36
  171.0 8.6 %collective-permute-start.23 = (f16[64,2048]{1,0:T(8,128)(2,1)S(1)}, f16[64,2048]{1,0:T(8,128)(2,1)S(1)}, u32[]{:S(2)}, u32[]{:S(2)}) collective-permute-start(f16[64,2048]{1,0:T(8,128)(2,1)S(1)} %get-tuple-element.91), channel_id=1, source_target_pairs={{0,192},{64,0},{128,64},{192,128},{1,193},{65,1},{129,65},{193,129... | collective-permute-start | bytes 786440 | tf_op jit(solution)/shard_map/ppermute | solution.py:36
  174.0 9.3 %collective-permute-start.20 = (f16[64,2048]{1,0:T(8,128)(2,1)S(1)}, f16[64,2048]{1,0:T(8,128)(2,1)S(1)}, u32[]{:S(2)}, u32[]{:S(2)}) collective-permute-start(f16[64,2048]{1,0:T(8,128)(2,1)S(1)} %get-tuple-element.90), channel_id=1, source_target_pairs={{0,64},{64,128},{128,192},{192,0},{1,65},{65,129},{129,193},{193,1... | collective-permute-start | bytes 786440 | tf_op jit(solution)/shard_map/ppermute | solution.py:36
  175.9 18.1 %collective-permute-start.18 = (f16[64,2048]{1,0:T(8,128)(2,1)S(1)}, f16[64,2048]{1,0:T(8,128)(2,1)S(1)}, u32[]{:S(2)}, u32[]{:S(2)}) collective-permute-start(f16[64,2048]{1,0:T(8,128)(2,1)S(1)} %fusion.4), channel_id=1, source_target_pairs={{0,192},{64,0},{128,64},{192,128},{1,193},{65,1},{129,65},{193,129... | collective-permute-start | bytes 786440 | tf_op jit(solution)/shard_map/ppermute | solution.py:36
  178.8 15.2 %collective-permute-start.22 = (f16[64,2048]{1,0:T(8,128)(2,1)S(1)}, f16[64,2048]{1,0:T(8,128)(2,1)S(1)}, u32[]{:S(2)}, u32[]{:S(2)}) collective-permute-start(f16[64,2048]{1,0:T(8,128)(2,1)S(1)} %fusion.2), channel_id=1, source_target_pairs={{0,64},{64,128},{128,192},{192,0},{1,65},{65,129},{129,193},{193,1... | collective-permute-start | bytes 786440 | tf_op jit(solution)/shard_map/ppermute | solution.py:36
  179.8 11.1 %collective-permute-start.24 = (f16[64,2048]{1,0:T(8,128)(2,1)S(1)}, f16[64,2048]{1,0:T(8,128)(2,1)S(1)}, u32[]{:S(2)}, u32[]{:S(2)}) collective-permute-start(f16[64,2048]{1,0:T(8,128)(2,1)S(1)} %multiply_convert_fusion), channel_id=1, source_target_pairs={{0,192},{64,0},{128,64},{192,128},{1,193},{65,1},{129,65},{193,129... | collective-permute-start | bytes 786440 | tf_op jit(solution)/shard_map/ppermute | solution.py:36
  183.4 10.6 %collective-permute-start.21 = (f16[64,2048]{1,0:T(8,128)(2,1)S(1)}, f16[64,2048]{1,0:T(8,128)(2,1)S(1)}, u32[]{:S(2)}, u32[]{:S(2)}) collective-permute-start(f16[64,2048]{1,0:T(8,128)(2,1)S(1)} %multiply_convert_fusion.1), channel_id=1, source_target_pairs={{0,64},{64,128},{128,192},{192,0},{1,65},{65,129},{129,193},{193,1... | collective-permute-start | bytes 786440 | tf_op jit(solution)/shard_map/ppermute | solution.py:36

commit v7 on v6

--- a/solution.py
+++ b/solution.py
@@ -396,9 +396,10 @@
 
     over, shares = over.reshape(1, COLS), shares.reshape(4, 1, COLS)
     own_part = (mine0 + theirs0) * over
-    top = own_part[low] + second[1].astype(F32) * shares[1] + third[0].astype(F32) * shares[2]
-    bottom = own_part[high] + second[0].astype(F32) * shares[0] + third[1].astype(F32) * shares[3]
-    return jnp.concatenate([top, bottom], axis=0), total.reshape(COLS)
+    sent = [second[1].astype(F32) * shares[1], second[0].astype(F32) * shares[0]]
+    base = lax.optimization_barrier(own_part + jnp.concatenate(sent, axis=0))
+    last = [third[0].astype(F32) * shares[2], third[1].astype(F32) * shares[3]]
+    return base + jnp.concatenate(last, axis=0), total.reshape(COLS)
 
 
 def solution(mesh):

time: 196 us -> 193 us (0.985)
  waiting for transfers between devices: 27.9 us -> 25.6 us
    ppermute x23, waiting for transfers between devices: 26.2 us -> 23.9 us  [step(): return lax.ppermute(x, axis, [(i, (i + by) % n) for i in range(n)])]
  transfers between devices with their start and end apart: 25 -> 25, of which waited for: 10 -> 11; matrix products, arithmetic and copies ran while one was open for 0% -> 0% of each run, Pallas kernels for 10% -> 11%
where the time goes in v7:
time: 193 us; the launch traced here: 192 us
  blocking collectives  90.4 us (47%)
  starting transfers between devices  35.8 us (19%)
  Pallas kernels  34.3 us (18%)
  waiting for transfers between devices  25.6 us (13%)
  local copies, waits for them, and re-layouts  3.1 us (2%)
  other arithmetic  2.14 us (1%)
    all_to_all x7, blocking collectives, everyone(): return lax.all_to_all(x, axis, 0, 0, tiled=True)  90.4 us
    ppermute x23, starting transfers between devices, step(): return lax.ppermute(x, axis, [(i, (i + by) % n) for i in range(n)])  34.9 us
    pallas_call x21, Pallas kernels, call(): pl.pallas_call(body, out_shape=[jax.ShapeDtypeStruct(s, d) for s, d in ou...  34.3 us
    ppermute x23, waiting for transfers between devices, step(): return lax.ppermute(x, axis, [(i, (i + by) % n) for i in range(n)])  23.9 us
  transfers between devices with their start and end apart: 25, of which 11 were waited for; matrix products, arithmetic and copies ran while one was open for 0% of the time, Pallas kernels for 11%

profile of v7, /device:TPU:1, one launch (start us, length us, event | category | flops | bytes accessed | tf_op | source)
XLA Modules:
  0.0 192.2 jit_solution(1688708358491681112)
XLA Ops:
  0.7 2.0 %collective-permute-start = (bf16[32,1024]{1,0:T(8,128)(2,1)}, bf16[32,1024]{1,0:T(8,128)(2,1)S(1)}, u32[]{:S(2)}, u32[]{:S(2)}) collective-permute-start(bf16[32,1024]{1,0:T(8,128)(2,1)} %bitcast.38), channel_id=1, source_target_pairs={{0,1},{1,2},{2,3},{3,0},{4,5},{5,6},{6,7},{7,4},{8,9},{9,10},{10,1... | collective-permute-start | bytes 196616 | tf_op jit(solution)/shard_map/ppermute | solution.py:36
  6.7 2.4 %collective-permute-done.2.d_ref = bf16[32,1024]{1,0:T(8,128)(2,1)S(1)} collective-permute-done((bf16[32,1024]{1,0:T(8,128)(2,1)}, bf16[32,1024]{1,0:T(8,128)(2,1)S(1)}, u32[]{:S(2)}, u32[]{:S(2)}) %collective-permute-start.2) | collective-permute-done | bytes 65568 | tf_op jit(solution)/shard_map/ppermute | solution.py:36
  9.1 5.7 %collective-permute-start.7 = (bf16[128,1024]{1,0:T(8,128)(2,1)S(1)}, bf16[128,1024]{1,0:T(8,128)(2,1)S(1)}, u32[]{:S(2)}, u32[]{:S(2)}) collective-permute-start(bf16[128,1024]{1,0:T(8,128)(2,1)S(1)} %shard_map.60.s_ref), channel_id=1, source_target_pairs={{0,28},{4,0},{8,4},{12,8},{16,12},{20,16},{24,20},{28,24},{1,29},{... | collective-permute-start | bytes 786440 | tf_op jit(solution)/shard_map/ppermute | solution.py:36
  14.7 3.3 %collective-permute-done.7.l = bf16[128,1024]{1,0:T(8,128)(2,1)S(1)} collective-permute-done((bf16[128,1024]{1,0:T(8,128)(2,1)S(1)}, bf16[128,1024]{1,0:T(8,128)(2,1)S(1)}, u32[]{:S(2)}, u32[]{:S(2)}) %collective-permute-start.7) | collective-permute-done | bytes 262176 | tf_op jit(solution)/shard_map/ppermute | solution.py:36
  18.0 3.1 %collective-permute-start.8 = (bf16[128,1024]{1,0:T(8,128)(2,1)S(1)}, bf16[128,1024]{1,0:T(8,128)(2,1)S(1)}, u32[]{:S(2)}, u32[]{:S(2)}) collective-permute-start(bf16[128,1024]{1,0:T(8,128)(2,1)S(1)} %collective-permute-done.7.l), channel_id=1, source_target_pairs={{0,28},{4,0},{8,4},{12,8},{16,12},{20,16},{24,20},{28,24},{1,29},{... | collective-permute-start | bytes 786440 | tf_op jit(solution)/shard_map/ppermute | solution.py:36
  21.2 3.3 %collective-permute-done.8.l = bf16[128,1024]{1,0:T(8,128)(2,1)S(1)} collective-permute-done((bf16[128,1024]{1,0:T(8,128)(2,1)S(1)}, bf16[128,1024]{1,0:T(8,128)(2,1)S(1)}, u32[]{:S(2)}, u32[]{:S(2)}) %collective-permute-start.8) | collective-permute-done | bytes 262176 | tf_op jit(solution)/shard_map/ppermute | solution.py:36
  24.5 3.1 %collective-permute-start.9 = (bf16[128,1024]{1,0:T(8,128)(2,1)S(1)}, bf16[128,1024]{1,0:T(8,128)(2,1)S(1)}, u32[]{:S(2)}, u32[]{:S(2)}) collective-permute-start(bf16[128,1024]{1,0:T(8,128)(2,1)S(1)} %collective-permute-done.8.l), channel_id=1, source_target_pairs={{0,28},{4,0},{8,4},{12,8},{16,12},{20,16},{24,20},{28,24},{1,29},{... | collective-permute-start | bytes 786440 | tf_op jit(solution)/shard_map/ppermute | solution.py:36
  27.6 3.7 %collective-permute-done.9.l = bf16[128,1024]{1,0:T(8,128)(2,1)S(1)} collective-permute-done((bf16[128,1024]{1,0:T(8,128)(2,1)S(1)}, bf16[128,1024]{1,0:T(8,128)(2,1)S(1)}, u32[]{:S(2)}, u32[]{:S(2)}) %collective-permute-start.9) | collective-permute-done | bytes 262176 | tf_op jit(solution)/shard_map/ppermute | solution.py:36
  31.3 3.2 %collective-permute-start.10 = (bf16[64,1024]{1,0:T(8,128)(2,1)S(1)}, bf16[64,1024]{1,0:T(8,128)(2,1)S(1)}, u32[]{:S(2)}, u32[]{:S(2)}) collective-permute-start(bf16[64,1024]{1,0:T(8,128)(2,1)S(1)} %slice.113), channel_id=1, source_target_pairs={{0,28},{4,0},{8,4},{12,8},{16,12},{20,16},{24,20},{28,24},{1,29},{... | collective-permute-start | bytes 393224 | tf_op jit(solution)/shard_map/ppermute | solution.py:36
  35.0 2.2 %copy-done = bf16[2048,1024]{1,0:T(8,128)(2,1)S(1)} copy-done((bf16[2048,1024]{1,0:T(8,128)(2,1)S(1)}, bf16[2048,1024]{1,0:T(8,128)(2,1)}, u32[]{:S(2)}) %copy-start) | copy-done | bytes 4194328
  37.2 2.6 %shard_map.61 = (f32[1024,2048]{1,0:T(8,128)S(1)}, bf16[8,128,1024]{2,1,0:T(8,128)(2,1)S(1)}, f32[8,128]{1,0:T(8,128)S(1)}) custom-call(s32[4]{0:T(128)S(1)} %pad_add_fusion.at_ref, bf16[128,1024]{1,0:T(8,128)(2,1)S(1)} %shard_map.60.s_ref, bf16[2048,1024]{1,0:T(8,128)(2,1)S(1)} %copy-done), custom_call_target="tpu_custom_call" | custom-call | tf_op jit(solution)/shard_map/pallas_call | solution.py:23
  39.8 3.7 %shard_map.62 = (f32[1024,2048]{1,0:T(8,128)S(1)}, bf16[8,128,1024]{2,1,0:T(8,128)(2,1)S(1)}, f32[8,128]{1,0:T(8,128)S(1)}) custom-call(s32[4]{0:T(128)S(1)} %pad_add_fusion.at_ref, bf16[128,1024]{1,0:T(8,128)(2,1)S(1)} %collective-permute-done.7.l, ...), custom_call_target="tpu_custom_call", output_to_operand_aliasing={{0}: (4, {}), {1}: (5, {}), {2}: (6, {})} | custom-call | tf_op jit(solution)/shard_map/pallas_call | solution.py:23
  43.4 3.7 %shard_map.63 = (f32[1024,2048]{1,0:T(8,128)S(1)}, bf16[8,128,1024]{2,1,0:T(8,128)(2,1)S(1)}, f32[8,128]{1,0:T(8,128)S(1)}) custom-call(s32[4]{0:T(128)S(1)} %pad_add_fusion.at_ref, bf16[128,1024]{1,0:T(8,128)(2,1)S(1)} %collective-permute-done.8.l, ...), custom_call_target="tpu_custom_call", output_to_operand_aliasing={{0}: (4, {}), {1}: (5, {}), {2}: (6, {})} | custom-call | tf_op jit(solution)/shard_map/pallas_call | solution.py:23
  47.1 3.7 %shard_map.64 = (f32[1024,2048]{1,0:T(8,128)S(1)}, bf16[8,128,1024]{2,1,0:T(8,128)(2,1)S(1)}, f32[8,128]{1,0:T(8,128)S(1)}) custom-call(s32[4]{0:T(128)S(1)} %pad_add_fusion.at_ref, bf16[128,1024]{1,0:T(8,128)(2,1)S(1)} %collective-permute-done.9.l, ...), custom_call_target="tpu_custom_call", output_to_operand_aliasing={{0}: (4, {}), {1}: (5, {}), {2}: (6, {})} | custom-call | tf_op jit(solution)/shard_map/pallas_call | solution.py:23
  50.8 4.8 %shard_map.65 = (f32[1024,2048]{1,0:T(8,128)S(1)}, bf16[8,128,1024]{2,1,0:T(8,128)(2,1)S(1)}, f32[8,128]{1,0:T(8,128)S(1)}, f32[32,16,128]{2,1,0:T(8,128)S(1)}) custom-call(s32[4]{0:T(128)S(1)} %pad_add_fusion.at_ref, bf16[64,1024]{1,0:T(8,128)(2,1)S(1)} %collective-permute-done.6.h0, ...), custom_call_target="tpu_custom_call", output_to_operand_aliasing={{0}: (4, {}), {1}: (5, {}), {2}: (6, {})} | custom-call | tf_op jit(solution)/shard_map/pallas_call | solution.py:23
  55.7 15.9 %all_to_all.35.e_ref = f32[32,16,128]{2,1,0:T(8,128)S(1)} all-to-all(f32[32,16,128]{2,1,0:T(8,128)S(1)} %get-tuple-element.60.mine_ref), channel_id=1, replica_groups=mesh['y'=4,'core'=2,'z'=8,'x'=4] {'z','x'}, dimensions={0} | all-to-all | bytes 524288 | tf_op jit(solution)/shard_map/all_to_all | solution.py:45
  72.4 18.2 %all_to_all.36.e_ref = f32[8,16,128]{2,1,0:T(8,128)S(1)} all-to-all(f32[8,16,128]{2,1,0:T(8,128)S(1)} %get-tuple-element.62), channel_id=1, replica_groups=mesh['y'=4,'core'=2,'z'=8,'x'=4] {'y','core'}, dimensions={0} | all-to-all | bytes 131072 | tf_op jit(solution)/shard_map/all_to_all | solution.py:45
  91.4 12.7 %all_to_all.37.e_ref = f32[32,8,128]{2,1,0:T(8,128)S(1)} all-to-all(f32[32,8,128]{2,1,0:T(8,128)S(1)} %shard_map.67), channel_id=1, replica_groups=mesh['y'=4,'core'=2,'z'=8,'x'=4] {'z','x'}, dimensions={0} | all-to-all | bytes 262144 | tf_op jit(solution)/shard_map/all_to_all | solution.py:45
  104.8 9.5 %all_to_all.38.e_ref = f32[8,16,128]{2,1,0:T(8,128)S(1)} all-to-all(f32[8,16,128]{2,1,0:T(8,128)S(1)} %shard_map.68), channel_id=1, replica_groups=mesh['y'=4,'core'=2,'z'=8,'x'=4] {'y','core'}, dimensions={0} | all-to-all | bytes 131072 | tf_op jit(solution)/shard_map/all_to_all | solution.py:45
  115.1 12.3 %all_to_all.39.e_ref = f32[32,8,128]{2,1,0:T(8,128)S(1)} all-to-all(f32[32,8,128]{2,1,0:T(8,128)S(1)} %shard_map.69), channel_id=1, replica_groups=mesh['y'=4,'core'=2,'z'=8,'x'=4] {'z','x'}, dimensions={0} | all-to-all | bytes 262144 | tf_op jit(solution)/shard_map/all_to_all | solution.py:45
  128.2 9.4 %all_to_all.40.e_ref = f32[8,16,128]{2,1,0:T(8,128)S(1)} all-to-all(f32[8,16,128]{2,1,0:T(8,128)S(1)} %shard_map.70), channel_id=1, replica_groups=mesh['y'=4,'core'=2,'z'=8,'x'=4] {'y','core'}, dimensions={0} | all-to-all | bytes 131072 | tf_op jit(solution)/shard_map/all_to_all | solution.py:45
  138.5 12.4 %all_to_all.41.e_ref = f32[32,8,128]{2,1,0:T(8,128)S(1)} all-to-all(f32[32,8,128]{2,1,0:T(8,128)S(1)} %get-tuple-element.64), channel_id=1, replica_groups=mesh['y'=4,'core'=2,'z'=8,'x'=4] {'z','x'}, dimensions={0} | all-to-all | bytes 262144 | tf_op jit(solution)/shard_map/all_to_all | solution.py:45
  153.5 2.3 %collective-permute-start.16 = (f32[128,2048]{1,0:T(8,128)S(1)}, f32[128,2048]{1,0:T(8,128)S(1)}, u32[]{:S(2)}, u32[]{:S(2)}) collective-permute-start(f32[128,2048]{1,0:T(8,128)S(1)} %shard_map.74), channel_id=1, source_target_pairs={{0,32},{32,0},{1,33},{33,1},{2,34},{34,2},{3,35},{35,3},{4,36},{36... | collective-permute-start | bytes 3145736 | tf_op jit(solution)/shard_map/ppermute | solution.py:36
  155.9 2.2 %collective-permute-done.12.other_ref = f32[24,128]{1,0:T(8,128)S(1)} collective-permute-done((f32[24,128]{1,0:T(8,128)S(1)}, f32[24,128]{1,0:T(8,128)S(1)}, u32[]{:S(2)}, u32[]{:S(2)}) %collective-permute-start.12) | collective-permute-done | bytes 12320 | tf_op jit(solution)/shard_map/ppermute | solution.py:36
  159.6 1.8 shard_map.77
  164.6 2.7 %collective-permute-start.15 = (f32[24,128]{1,0:T(8,128)S(1)}, f32[24,128]{1,0:T(8,128)S(1)}, u32[]{:S(2)}, u32[]{:S(2)}) collective-permute-start(f32[24,128]{1,0:T(8,128)S(1)} %collective-permute-done.13.near), channel_id=1, source_target_pairs={{0,32},{32,0},{1,33},{33,1},{2,34},{34,2},{3,35},{35,3},{4,36},{36... | collective-permute-start | bytes 36872 | tf_op jit(solution)/shard_map/ppermute | solution.py:36
  167.3 1.8 shard_map.73
  172.5 1.8 collective-permute-start.23
  174.3 1.8 shard_map.78
  180.1 2.2 %collective-permute-start.24 = (f16[64,2048]{1,0:T(8,128)(2,1)S(1)}, f16[64,2048]{1,0:T(8,128)(2,1)S(1)}, u32[]{:S(2)}, u32[]{:S(2)}) collective-permute-start(f16[64,2048]{1,0:T(8,128)(2,1)S(1)} %multiply_convert_fusion), channel_id=1, source_target_pairs={{0,192},{64,0},{128,64},{192,128},{1,193},{65,1},{129,65},{193,129... | collective-permute-start | bytes 786440 | tf_op jit(solution)/shard_map/ppermute | solution.py:36
  182.3 2.4 %collective-permute-done.18 = f16[64,2048]{1,0:T(8,128)(2,1)S(1)} collective-permute-done((f16[64,2048]{1,0:T(8,128)(2,1)S(1)}, f16[64,2048]{1,0:T(8,128)(2,1)S(1)}, u32[]{:S(2)}, u32[]{:S(2)}) %collective-permute-start.18) | collective-permute-done | bytes 262176 | tf_op jit(solution)/shard_map/ppermute | solution.py:36
  185.7 5.3 %collective-permute-done.22 = f16[64,2048]{1,0:T(8,128)(2,1)S(1)} collective-permute-done((f16[64,2048]{1,0:T(8,128)(2,1)S(1)}, f16[64,2048]{1,0:T(8,128)(2,1)S(1)}, u32[]{:S(2)}, u32[]{:S(2)}) %collective-permute-start.22) | collective-permute-done | bytes 262176 | tf_op jit(solution)/shard_map/ppermute | solution.py:36
  (71 shorter events, 25.9 us)
Async XLA Ops:
  0.7 5.9 %collective-permute-start = (bf16[32,1024]{1,0:T(8,128)(2,1)}, bf16[32,1024]{1,0:T(8,128)(2,1)S(1)}, u32[]{:S(2)}, u32[]{:S(2)}) collective-permute-start(bf16[32,1024]{1,0:T(8,128)(2,1)} %bitcast.38), channel_id=1, source_target_pairs={{0,1},{1,2},{2,3},{3,0},{4,5},{5,6},{6,7},{7,4},{8,9},{9,10},{10,1... | collective-permute-start | bytes 196616 | tf_op jit(solution)/shard_map/ppermute | solution.py:36
  2.8 3.9 %collective-permute-start.1 = (bf16[32,1024]{1,0:T(8,128)(2,1)}, bf16[32,1024]{1,0:T(8,128)(2,1)S(1)}, u32[]{:S(2)}, u32[]{:S(2)}) collective-permute-start(bf16[32,1024]{1,0:T(8,128)(2,1)} %bitcast.39), channel_id=1, source_target_pairs={{0,3},{1,0},{2,1},{3,2},{4,7},{5,4},{6,5},{7,6},{8,11},{9,8},{10,9... | collective-permute-start | bytes 196616 | tf_op jit(solution)/shard_map/ppermute | solution.py:36
  4.1 4.9 %collective-permute-start.2 = (bf16[32,1024]{1,0:T(8,128)(2,1)}, bf16[32,1024]{1,0:T(8,128)(2,1)S(1)}, u32[]{:S(2)}, u32[]{:S(2)}) collective-permute-start(bf16[32,1024]{1,0:T(8,128)(2,1)} %bitcast.40), channel_id=1, source_target_pairs={{0,2},{1,3},{2,0},{3,1},{4,6},{5,7},{6,4},{7,5},{8,10},{9,11},{10,... | collective-permute-start | bytes 196616 | tf_op jit(solution)/shard_map/ppermute | solution.py:36
  5.8 0.9 copy-start.3
  9.1 9.0 %collective-permute-start.7 = (bf16[128,1024]{1,0:T(8,128)(2,1)S(1)}, bf16[128,1024]{1,0:T(8,128)(2,1)S(1)}, u32[]{:S(2)}, u32[]{:S(2)}) collective-permute-start(bf16[128,1024]{1,0:T(8,128)(2,1)S(1)} %shard_map.60.s_ref), channel_id=1, source_target_pairs={{0,28},{4,0},{8,4},{12,8},{16,12},{20,16},{24,20},{28,24},{1,29},{... | collective-permute-start | bytes 786440 | tf_op jit(solution)/shard_map/ppermute | solution.py:36
  14.7 6.4 %collective-permute-start.3 = (bf16[128,1024]{1,0:T(8,128)(2,1)S(1)}, bf16[128,1024]{1,0:T(8,128)(2,1)S(1)}, u32[]{:S(2)}, u32[]{:S(2)}) collective-permute-start(bf16[128,1024]{1,0:T(8,128)(2,1)S(1)} %shard_map.60.s_ref), channel_id=1, source_target_pairs={{0,4},{4,8},{8,12},{12,16},{16,20},{20,24},{24,28},{28,0},{1,5},{5... | collective-permute-start | bytes 786440 | tf_op jit(solution)/shard_map/ppermute | solution.py:36
  18.0 6.4 %collective-permute-start.8 = (bf16[128,1024]{1,0:T(8,128)(2,1)S(1)}, bf16[128,1024]{1,0:T(8,128)(2,1)S(1)}, u32[]{:S(2)}, u32[]{:S(2)}) collective-permute-start(bf16[128,1024]{1,0:T(8,128)(2,1)S(1)} %collective-permute-done.7.l), channel_id=1, source_target_pairs={{0,28},{4,0},{8,4},{12,8},{16,12},{20,16},{24,20},{28,24},{1,29},{... | collective-permute-start | bytes 786440 | tf_op jit(solution)/shard_map/ppermute | solution.py:36
  21.2 6.4 %collective-permute-start.4 = (bf16[128,1024]{1,0:T(8,128)(2,1)S(1)}, bf16[128,1024]{1,0:T(8,128)(2,1)S(1)}, u32[]{:S(2)}, u32[]{:S(2)}) collective-permute-start(bf16[128,1024]{1,0:T(8,128)(2,1)S(1)} %collective-permute-done.3.r), channel_id=1, source_target_pairs={{0,4},{4,8},{8,12},{12,16},{16,20},{20,24},{24,28},{28,0},{1,5},{5... | collective-permute-start | bytes 786440 | tf_op jit(solution)/shard_map/ppermute | solution.py:36
  24.5 6.8 %collective-permute-start.9 = (bf16[128,1024]{1,0:T(8,128)(2,1)S(1)}, bf16[128,1024]{1,0:T(8,128)(2,1)S(1)}, u32[]{:S(2)}, u32[]{:S(2)}) collective-permute-start(bf16[128,1024]{1,0:T(8,128)(2,1)S(1)} %collective-permute-done.8.l), channel_id=1, source_target_pairs={{0,28},{4,0},{8,4},{12,8},{16,12},{20,16},{24,20},{28,24},{1,29},{... | collective-permute-start | bytes 786440 | tf_op jit(solution)/shard_map/ppermute | solution.py:36
  27.6 7.1 %collective-permute-start.5 = (bf16[128,1024]{1,0:T(8,128)(2,1)S(1)}, bf16[128,1024]{1,0:T(8,128)(2,1)S(1)}, u32[]{:S(2)}, u32[]{:S(2)}) collective-permute-start(bf16[128,1024]{1,0:T(8,128)(2,1)S(1)} %collective-permute-done.4.r), channel_id=1, source_target_pairs={{0,4},{4,8},{8,12},{12,16},{16,20},{20,24},{24,28},{28,0},{1,5},{5... | collective-permute-start | bytes 786440 | tf_op jit(solution)/shard_map/ppermute | solution.py:36
  31.3 19.5 %collective-permute-start.10 = (bf16[64,1024]{1,0:T(8,128)(2,1)S(1)}, bf16[64,1024]{1,0:T(8,128)(2,1)S(1)}, u32[]{:S(2)}, u32[]{:S(2)}) collective-permute-start(bf16[64,1024]{1,0:T(8,128)(2,1)S(1)} %slice.113), channel_id=1, source_target_pairs={{0,28},{4,0},{8,4},{12,8},{16,12},{20,16},{24,20},{28,24},{1,29},{... | collective-permute-start | bytes 393224 | tf_op jit(solution)/shard_map/ppermute | solution.py:36
  34.7 16.1 %collective-permute-start.6 = (bf16[64,1024]{1,0:T(8,128)(2,1)S(1)}, bf16[64,1024]{1,0:T(8,128)(2,1)S(1)}, u32[]{:S(2)}, u32[]{:S(2)}) collective-permute-start(bf16[64,1024]{1,0:T(8,128)(2,1)S(1)} %slice.112), channel_id=1, source_target_pairs={{0,4},{4,8},{8,12},{12,16},{16,20},{20,24},{24,28},{28,0},{1,5},{5... | collective-permute-start | bytes 393224 | tf_op jit(solution)/shard_map/ppermute | solution.py:36
  35.0 2.2 %copy-start = (bf16[2048,1024]{1,0:T(8,128)(2,1)S(1)}, bf16[2048,1024]{1,0:T(8,128)(2,1)}, u32[]{:S(2)}) copy-start(bf16[2048,1024]{1,0:T(8,128)(2,1)} %c_ref.9) | copy-start | bytes 12582916
  50.8 20.8 %copy-start.2 = (f32[1024]{0:T(1024)S(1)}, f32[1024]{0:T(1024)}, u32[]{:S(2)}) copy-start(f32[1024]{0:T(1024)} %param.6) | copy-start | bytes 12292
  71.6 18.9 %copy-start.1 = (f32[2048]{0:T(1024)S(1)}, f32[2048]{0:T(1024)}, u32[]{:S(2)}) copy-start(f32[2048]{0:T(1024)} %param.7) | copy-start | bytes 24580
  153.5 5.9 %collective-permute-start.16 = (f32[128,2048]{1,0:T(8,128)S(1)}, f32[128,2048]{1,0:T(8,128)S(1)}, u32[]{:S(2)}, u32[]{:S(2)}) collective-permute-start(f32[128,2048]{1,0:T(8,128)S(1)} %shard_map.74), channel_id=1, source_target_pairs={{0,32},{32,0},{1,33},{33,1},{2,34},{34,2},{3,35},{35,3},{4,36},{36... | collective-permute-start | bytes 3145736 | tf_op jit(solution)/shard_map/ppermute | solution.py:36
  155.8 2.3 %collective-permute-start.12 = (f32[24,128]{1,0:T(8,128)S(1)}, f32[24,128]{1,0:T(8,128)S(1)}, u32[]{:S(2)}, u32[]{:S(2)}) collective-permute-start(f32[24,128]{1,0:T(8,128)S(1)} %get-tuple-element.71.mine_ref), channel_id=1, source_target_pairs={{0,32},{32,0},{1,33},{33,1},{2,34},{34,2},{3,35},{35,3},{4,36},{36... | collective-permute-start | bytes 36872 | tf_op jit(solution)/shard_map/ppermute | solution.py:36
  161.4 14.7 %collective-permute-start.17 = (f32[128,2048]{1,0:T(8,128)S(1)}, f32[128,2048]{1,0:T(8,128)S(1)}, u32[]{:S(2)}, u32[]{:S(2)}) collective-permute-start(f32[128,2048]{1,0:T(8,128)S(1)} %get-tuple-element.78), channel_id=1, source_target_pairs={{0,32},{32,0},{1,33},{33,1},{2,34},{34,2},{3,35},{35,3},{4,36},{36... | collective-permute-start | bytes 3145736 | tf_op jit(solution)/shard_map/ppermute | solution.py:36
  161.9 15.6 %collective-permute-start.19 = (f32[128,2048]{1,0:T(8,128)S(1)}, f32[128,2048]{1,0:T(8,128)S(1)}, u32[]{:S(2)}, u32[]{:S(2)}) collective-permute-start(f32[128,2048]{1,0:T(8,128)S(1)} %get-tuple-element.77), channel_id=1, source_target_pairs={{0,32},{32,0},{1,33},{33,1},{2,34},{34,2},{3,35},{35,3},{4,36},{36... | collective-permute-start | bytes 3145736 | tf_op jit(solution)/shard_map/ppermute | solution.py:36
  162.0 2.5 %collective-permute-start.13 = (f32[24,128]{1,0:T(8,128)S(1)}, f32[24,128]{1,0:T(8,128)S(1)}, u32[]{:S(2)}, u32[]{:S(2)}) collective-permute-start(f32[24,128]{1,0:T(8,128)S(1)} %get-tuple-element.72.m0), channel_id=1, source_target_pairs={{0,64},{64,128},{128,192},{192,0},{32,224},{96,32},{160,96},{224,1... | collective-permute-start | bytes 36872 | tf_op jit(solution)/shard_map/ppermute | solution.py:41
  164.6 4.7 %collective-permute-start.15 = (f32[24,128]{1,0:T(8,128)S(1)}, f32[24,128]{1,0:T(8,128)S(1)}, u32[]{:S(2)}, u32[]{:S(2)}) collective-permute-start(f32[24,128]{1,0:T(8,128)S(1)} %collective-permute-done.13.near), channel_id=1, source_target_pairs={{0,32},{32,0},{1,33},{33,1},{2,34},{34,2},{3,35},{35,3},{4,36},{36... | collective-permute-start | bytes 36872 | tf_op jit(solution)/shard_map/ppermute | solution.py:36
  167.3 2.5 %collective-permute-start.14 = (f32[24,128]{1,0:T(8,128)S(1)}, f32[24,128]{1,0:T(8,128)S(1)}, u32[]{:S(2)}, u32[]{:S(2)}) collective-permute-start(f32[24,128]{1,0:T(8,128)S(1)} %collective-permute-done.13.near), channel_id=1, source_target_pairs={{0,64},{64,128},{128,192},{192,0},{32,224},{96,32},{160,96},{224,1... | collective-permute-start | bytes 36872 | tf_op jit(solution)/shard_map/ppermute | solution.py:41
  169.1 16.3 %collective-permute-start.11 = (f32[128,2048]{1,0:T(8,128)S(1)}, f32[128,2048]{1,0:T(8,128)S(1)}, u32[]{:S(2)}, u32[]{:S(2)}) collective-permute-start(f32[128,2048]{1,0:T(8,128)S(1)} %get-tuple-element.69), channel_id=1, source_target_pairs={{0,32},{32,0},{1,33},{33,1},{2,34},{34,2},{3,35},{35,3},{4,36},{36... | collective-permute-start | bytes 3145736 | tf_op jit(solution)/shard_map/ppermute | solution.py:36
  171.0 7.3 %collective-permute-start.21 = (f16[64,2048]{1,0:T(8,128)(2,1)S(1)}, f16[64,2048]{1,0:T(8,128)(2,1)S(1)}, u32[]{:S(2)}, u32[]{:S(2)}) collective-permute-start(f16[64,2048]{1,0:T(8,128)(2,1)S(1)} %get-tuple-element.91), channel_id=1, source_target_pairs={{0,64},{64,128},{128,192},{192,0},{1,65},{65,129},{129,193},{193,1... | collective-permute-start | bytes 786440 | tf_op jit(solution)/shard_map/ppermute | solution.py:36
  172.5 7.4 %collective-permute-start.23 = (f16[64,2048]{1,0:T(8,128)(2,1)S(1)}, f16[64,2048]{1,0:T(8,128)(2,1)S(1)}, u32[]{:S(2)}, u32[]{:S(2)}) collective-permute-start(f16[64,2048]{1,0:T(8,128)(2,1)S(1)} %get-tuple-element.90), channel_id=1, source_target_pairs={{0,192},{64,0},{128,64},{192,128},{1,193},{65,1},{129,65},{193,129... | collective-permute-start | bytes 786440 | tf_op jit(solution)/shard_map/ppermute | solution.py:36
  176.2 8.5 %collective-permute-start.18 = (f16[64,2048]{1,0:T(8,128)(2,1)S(1)}, f16[64,2048]{1,0:T(8,128)(2,1)S(1)}, u32[]{:S(2)}, u32[]{:S(2)}) collective-permute-start(f16[64,2048]{1,0:T(8,128)(2,1)S(1)} %fusion.3), channel_id=1, source_target_pairs={{0,192},{64,0},{128,64},{192,128},{1,193},{65,1},{129,65},{193,129... | collective-permute-start | bytes 786440 | tf_op jit(solution)/shard_map/ppermute | solution.py:36
  177.5 7.9 %collective-permute-start.20 = (f16[64,2048]{1,0:T(8,128)(2,1)S(1)}, f16[64,2048]{1,0:T(8,128)(2,1)S(1)}, u32[]{:S(2)}, u32[]{:S(2)}) collective-permute-start(f16[64,2048]{1,0:T(8,128)(2,1)S(1)} %fusion.1), channel_id=1, source_target_pairs={{0,64},{64,128},{128,192},{192,0},{1,65},{65,129},{129,193},{193,1... | collective-permute-start | bytes 786440 | tf_op jit(solution)/shard_map/ppermute | solution.py:36
  178.4 12.6 %collective-permute-start.22 = (f16[64,2048]{1,0:T(8,128)(2,1)S(1)}, f16[64,2048]{1,0:T(8,128)(2,1)S(1)}, u32[]{:S(2)}, u32[]{:S(2)}) collective-permute-start(f16[64,2048]{1,0:T(8,128)(2,1)S(1)} %multiply_convert_fusion.1), channel_id=1, source_target_pairs={{0,64},{64,128},{128,192},{192,0},{1,65},{65,129},{129,193},{193,1... | collective-permute-start | bytes 786440 | tf_op jit(solution)/shard_map/ppermute | solution.py:36
  180.1 11.0 %collective-permute-start.24 = (f16[64,2048]{1,0:T(8,128)(2,1)S(1)}, f16[64,2048]{1,0:T(8,128)(2,1)S(1)}, u32[]{:S(2)}, u32[]{:S(2)}) collective-permute-start(f16[64,2048]{1,0:T(8,128)(2,1)S(1)} %multiply_convert_fusion), channel_id=1, source_target_pairs={{0,192},{64,0},{128,64},{192,128},{1,193},{65,1},{129,65},{193,129... | collective-permute-start | bytes 786440 | tf_op jit(solution)/shard_map/ppermute | solution.py:36
